TPU v7x, 256 devices: a whole 4x4x8 slice. The times are simulated.
256 devices in a mesh: ta: 4 (over y), gy: 16 (over z, core), gx: 4 (over x).
Axes of the slice: x: 4, y: 4, z: 8, core: 2. Of those that a mesh axis runs over, the one named last changes fastest.
Arguments:
- features: bfloat16 [16, 32, 416, 192], P('ta', 'gy', 'gx'), may hold values from -6 to 6
- gain_first: float32 [192], replicated, may hold values from 0.1 to 1.9
- kernel_first: bfloat16 [3, 3, 3, 192, 192], replicated, may hold values from -0.078125 to 0.078125
- bias_first: float32 [192], replicated, may hold values from -3 to 3
- gain_second: float32 [192], replicated, may hold values from 0.1 to 1.9
- kernel_second: bfloat16 [3, 3, 3, 192, 192], replicated, may hold values from -0.078125 to 0.078125
- bias_second: float32 [192], replicated, may hold values from -3 to 3
Outputs:
- block_out: bfloat16 [16, 32, 416, 192], P('ta', 'gy', 'gx')
All inputs are finite; a program needn't handle non-finite values.
Results may differ from a plain program's by a relative error of at most 0.0075.
Values may be sent and summed in bfloat16 or wider, within the bound.
No kernel may reach another device: no remote copies, remote signals or barrier semaphores. Data moves between devices by JAX's collectives and lax.ppermute only.
A program may use at most 64 MiB of HBM per device.

v0:
```python
import functools

import jax
import jax.numpy as jnp
from jax import lax
from jax.experimental import pallas as pl
from jax.experimental.pallas import tpu as pltpu
from jax.sharding import PartitionSpec as P


epsilon = 1e-06
axes = ("ta", "gy", "gx")
ROWS, COLS, TILE, CYC, CH, LANE = 2, 104, 8, 112, 192, 128
HI = CH - LANE
TILES = COLS // TILE
VMEM = pl.BlockSpec(memory_space=pltpu.VMEM)
SMEM = pl.BlockSpec(memory_space=pltpu.SMEM)
ANY = pl.BlockSpec(memory_space=pl.ANY)
params = pltpu.CompilerParams(vmem_limit_bytes=56 << 20)


def act(field, gain):
    meansq = jnp.mean(field * field, axis=-1, keepdims=True)
    u = field * lax.rsqrt(meansq + epsilon) * gain
    return u / (1.0 + jnp.exp(-u))


def pack(even, odd):
    high = jnp.concatenate([even[:, LANE:], odd[:, LANE:]], axis=1)
    return even[:, :LANE], odd[:, :LANE], high


def first_kernel(flags, feat, gain, mine, on, cr, edge):
    core = flags[0]
    frames = feat.shape[0]
    for slot in range(ROWS):
        row = jnp.where(core == 0, 1 - slot, slot)
        for f in range(0, frames, 2):
            pair = [act(feat[f + e, row].astype(jnp.float32), gain[...]).astype(jnp.bfloat16) for e in range(2)]
            for k, slab in enumerate(pack(*pair)):
                n = 3 * (f // 2) + k
                mine[slot, n] = slab
                left, right = slab[:TILE], slab[COLS - TILE :]
                edge[slot, n] = jnp.where(core == 0, right, left)
                on[slot_base + slot * 6 + n] = jnp.where(core == 0, left, right)
                if slot == 0:
                    on[n * TILES : (n + 1) * TILES] = slab.reshape(TILES, TILE, LANE)
                else:
                    cr[n * TILES : (n + 1) * TILES] = slab.reshape(TILES, TILE, LANE)


slot_base = 6 * TILES


def weight_copies(kernel, weight, sems, core):
    copies = []
    for q in range(3):
        source = jnp.where(core == 0, 2 - q, q)
        copies.append((kernel.at[:, source, :, :LANE, :], weight.at[:, 4 * q : 4 * q + 3]))
        for r in range(3):
            tile, half = (4 * q + 3, r) if r < 2 else (12 + q // 2, q % 2)
            copies.append(
                (kernel.at[:, source, r, LANE:, :], weight.at[:, tile, HI * half : HI * (half + 1), :])
            )
    return [pltpu.make_async_copy(a, b, sems.at[n]) for n, (a, b) in enumerate(copies)]


def rolled(x, by):
    return jnp.concatenate([x[-by:], x[:-by]], axis=0)


def put_row(taps, row, f, low, high):
    for e in range(2):
        taps[row, f + e, :, 0:128] = rolled(low[e], 1)
        taps[row, f + e, :, 128:256] = low[e]
        taps[row, f + e, :, 256:384] = rolled(low[e], -1)
    before, after = rolled(high, 1), rolled(high, -1)
    for e in range(2):
        half = slice(HI * e, HI * (e + 1))
        taps[row, f + e, :, 384:448] = before[:, half]
        taps[row, f + e, :, 448:512] = high[:, half]
        taps[row, f + e, :, 512:576] = after[:, half]
        if row > 0:
            taps[row - 1, f + e, :, 576:640] = after[:, half]
        if row > 1:
            taps[row, f + e, :, 576:640] = after[:, half]


def conv_row(taps, weight, row, f, count):
    total = None
    for p in range(3):
        span = slice(f + p, f + p + count)
        parts = [(taps[row + q, span, :, :512], weight[p, 4 * q : 4 * q + 4]) for q in range(3)]
        last = jnp.concatenate([taps[row, span, :, 512:], taps[row + 2, span, :, 512:]], axis=-1)
        parts.append((last, weight[p, 12:14]))
        for cells, k in parts:
            term = jnp.dot(
                cells.reshape(count * CYC, -1), k.reshape(-1, CH), preferred_element_type=jnp.float32
            )
            total = term if total is None else total + term
    return total


def middle_kernel(flags, mine, ta, on, on_prev, cr, cr_prev, rim, kernel, bias, gain, on_out, cr_out, taps, weight, sems):
    core = flags[0]
    copies = weight_copies(kernel, weight, sems, core)
    for c in copies:
        c.start()
    weight[:, 13, HI:, :] = jnp.zeros((3, HI, CH), jnp.bfloat16)

    def tiles(ref, n):
        return ref[n * TILES : (n + 1) * TILES].reshape(COLS, LANE)

    for half in range(2):
        for pair in range(2):
            f = 4 * half + 2 * pair
            for row in range(4):
                slabs = []
                for k in range(3):
                    n = 3 * pair + k
                    if row == 0:
                        body = tiles(on if half else on_prev, n)
                        tip = rim[1 - half, 2, n]
                    elif row == 3:
                        body = tiles(cr if half else cr_prev, n)
                        tip = cr_prev[slot_base + (1 - half) * 6 + n]
                    else:
                        body = (mine if half else ta)[row - 1, n]
                        tip = rim[1 - half, row - 1, n]
                    slabs.append(jnp.concatenate([body, tip], axis=0))
                put_row(taps, row, f, slabs[:2], slabs[2])
    for c in copies:
        c.wait()
    col = lax.broadcasted_iota(jnp.int32, (CYC, 1), 0)
    outside = ((col == COLS) & (flags[3] == 1)) | ((col == CYC - 1) & (flags[2] == 1))
    for slot in range(ROWS):
        for f in range(0, 6, 2):
            total = conv_row(taps, weight, slot, f, 2) + bias[...]
            middle = total.astype(jnp.bfloat16).astype(jnp.float32)
            second = act(middle, gain[...])
            pair = []
            for e in range(2):
                drop = outside | (flags[1] == 1) if f == 0 else outside
                pair.append(jnp.where(drop, 0.0, second[e * CYC : (e + 1) * CYC]).astype(jnp.bfloat16))
            for k, slab in enumerate(pack(*pair)):
                (on_out if slot == 0 else cr_out)[3 * (f // 2) + k] = slab


def last_kernel(flags, mine_on, mine_cr, on, cr, feat, kernel, bias, out, taps, weight, sems):
    core = flags[0]
    copies = weight_copies(kernel, weight, sems, core)
    for c in copies:
        c.start()
    weight[:, 13, HI:, :] = jnp.zeros((3, HI, CH), jnp.bfloat16)
    for f in range(0, 6, 2):
        n = 3 * (f // 2)
        for row, ref in enumerate((on, mine_on, mine_cr, cr)):
            put_row(taps, row, f, [ref[n], ref[n + 1]], ref[n + 2])
    for c in copies:
        c.wait()
    for slot in range(ROWS):
        row = jnp.where(core == 0, 1 - slot, slot)
        for f in range(0, 4, 2):
            total = conv_row(taps, weight, slot, f, 2) + bias[...]
            for e in range(2):
                cells = total[e * CYC : e * CYC + COLS] + feat[f + e, row].astype(jnp.float32)
                out[f + e, row] = cells.astype(jnp.bfloat16)


def shape(*dims):
    return jax.ShapeDtypeStruct(dims, jnp.bfloat16)


def conv_scratch(frames):
    return [
        pltpu.VMEM((4, frames, CYC, 640), jnp.bfloat16),
        pltpu.VMEM((3, 14, LANE, CH), jnp.bfloat16),
        pltpu.SemaphoreType.DMA((12,)),
    ]


def routes(sizes, move):
    pairs = []
    for t in range(sizes[0]):
        for y in range(sizes[1]):
            for x in range(sizes[2]):
                to = move(t, y, x)
                if all(0 <= a < n for a, n in zip(to, sizes)):
                    ids = [(i * sizes[1] + j) * sizes[2] + k for i, j, k in ((t, y, x), to)]
                    pairs.append(tuple(ids))
    return pairs


def local(sizes, features, gain_first, kernel_first, bias_first, gain_second, kernel_second, bias_second):
    def send(array, move):
        return lax.ppermute(array, axes, routes(sizes, move))

    def chip(array):
        return send(array, lambda t, y, x: (t, y ^ 1, x))

    def cross(array):
        return send(array, lambda t, y, x: (t, y + 1 if y % 2 else y - 1, x))

    core = lax.axis_index("gy") % 2
    ta_index, gx_index = lax.axis_index("ta"), lax.axis_index("gx")
    flags = jnp.stack([core, ta_index == 0, gx_index == 0, gx_index == sizes[2] - 1]).astype(jnp.int32)
    row = lambda v: v.reshape(1, CH)

    mine, on_row, cr_row, edge = pl.pallas_call(
        first_kernel,
        out_shape=(shape(2, 6, COLS, LANE), shape(slot_base + 12, TILE, LANE), shape(slot_base, TILE, LANE), shape(2, 6, TILE, LANE)),
        in_specs=[SMEM, VMEM, VMEM],
        out_specs=(VMEM,) * 4,
        compiler_params=params,
        name="first",
    )(flags, features, row(gain_first))

    on = chip(on_row)
    ta = send(mine, lambda t, y, x: (t + 1, y, x))
    cr = cross(cr_row)
    edges = jnp.concatenate([edge.reshape(12, TILE, LANE), on[slot_base:]])
    side = send(edges, lambda t, y, x: (t, y, x - 1 if y % 2 else x + 1))
    side_prev = send(edges, lambda t, y, x: (t + 1, y, x - 1 if y % 2 else x + 1))
    sides = jnp.stack([side, side_prev]).reshape(2, 2, 12, TILE, LANE)
    others = chip(sides)[:, ::-1]
    upper = lax.broadcasted_iota(jnp.int32, sides.shape, 3) < TILE // 2
    rim = jnp.where(upper == (core == 0), others, sides).reshape(2, 4, 6, TILE, LANE)
    on_prev = chip(ta[0].reshape(slot_base, TILE, LANE))
    cr_prev = cross(jnp.concatenate([ta[1].reshape(slot_base, TILE, LANE), rim[:, 1].reshape(12, TILE, LANE)]))

    on_second, cr_second = pl.pallas_call(
        middle_kernel,
        out_shape=(shape(9, CYC, LANE), shape(9, CYC, LANE)),
        in_specs=[SMEM] + [VMEM] * 7 + [ANY, VMEM, VMEM],
        out_specs=(VMEM, VMEM),
        scratch_shapes=conv_scratch(8),
        compiler_params=params,
        name="middle",
    )(flags, mine, ta, on, on_prev, cr, cr_prev, rim, kernel_first, row(bias_first), row(gain_second))

    return pl.pallas_call(
        last_kernel,
        out_shape=jax.ShapeDtypeStruct(features.shape, jnp.bfloat16),
        in_specs=[SMEM] + [VMEM] * 5 + [ANY, VMEM],
        out_specs=VMEM,
        scratch_shapes=conv_scratch(6),
        compiler_params=params,
        name="last",
    )(flags, on_second, cr_second, chip(on_second), cross(cr_second), features, kernel_second, row(bias_second))


def solution(mesh):
    sizes = tuple(mesh.shape[a] for a in axes)
    placed = (P("ta", "gy", "gx", None), P(), P(), P(), P(), P(), P())
    return jax.shard_map(
        functools.partial(local, sizes),
        mesh=mesh,
        in_specs=placed,
        out_specs=P("ta", "gy", "gx", None),
        check_vma=False,
    )
```

profile of v0, /device:TPU:107, one launch (start us, length us, event | category | flops | bytes accessed | tf_op | source)
XLA Modules:
  0.0 61.5 jit_solution(16232029458956875241)
XLA Ops:
  0.0 2.0 %copy.8.feat = bf16[4,2,104,192]{3,2,1,0:T(8,128)(2,1)} copy(bf16[4,2,104,192]{2,3,1,0:T(8,128)(2,1)} %param.7) | data formatting | bytes 638976 | tf_op args[0]
  2.0 0.6 pad_add_fusion.flags
  2.5 2.3 %first.1 = (bf16[2,6,104,128]{3,2,1,0:T(8,128)(2,1)}, bf16[90,8,128]{2,1,0:T(8,128)(2,1)}, bf16[78,8,128]{2,1,0:T(8,128)(2,1)}, bf16[2,6,8,128]{3,2,1,0:T(8,128)(2,1)}) custom-call(s32[4]{0:T(128)} %pad_add_fusion.flags, bf16[4,2,104,192]{3,2,1,0:T(8,128)(2,1)} %copy.8.feat, f32[1,192]{1,0:T(1,128)} %bitcast.25), custom_call_target="tpu_custom_call" | custom-call | tf_op jit(solution)/shard_map/first/pallas_call | solution.py:209
  4.8 0.7 %collective-permute-start.1 = (bf16[90,8,128]{2,1,0:T(8,128)(2,1)}, bf16[90,8,128]{2,1,0:T(8,128)(2,1)S(1)}, u32[]{:S(2)}, u32[]{:S(2)}) collective-permute-start(bf16[90,8,128]{2,1,0:T(8,128)(2,1)} %get-tuple-element.12), channel_id=1, source_target_pairs={{0,4},{1,5},{2,6},{3,7},{4,0},{5,1},{6,2},{7,3},{8,12},{9,13},{10,... | collective-permute-start | bytes 552968 | tf_op jit(solution)/shard_map/ppermute | solution.py:196
  5.5 3.2 %collective-permute-start = (bf16[2,6,104,128]{3,2,1,0:T(8,128)(2,1)}, bf16[2,6,104,128]{3,2,1,0:T(8,128)(2,1)S(1)}, u32[]{:S(2)}, u32[]{:S(2)}) collective-permute-start(bf16[2,6,104,128]{3,2,1,0:T(8,128)(2,1)} %get-tuple-element.11.mine), channel_id=1, source_target_pairs={{0,64},{1,65},{2,66},{3,67},{4,68},{5,69},{6,70},{7,71},{8,72},{9,... | collective-permute-start | bytes 958472 | tf_op jit(solution)/shard_map/ppermute | solution.py:196
  8.7 0.0 collective-permute-done.1.on
  8.7 0.0 copy-start.4
  8.8 0.8 %pad_maximum_fusion.2 = bf16[24,8,128]{2,1,0:T(8,128)(2,1)S(1)} fusion(bf16[12,8,128]{2,1,0:T(8,128)(2,1)S(1)} %slice.18, bf16[12,8,128]{2,1,0:T(8,128)(2,1)} %bitcast.24), kind=kLoop, calls=%fused_computation.3 | loop fusion | flops 24576 | bytes 98304 | tf_op jit(solution)/shard_map/concatenate | solution.py:221
  9.5 2.9 %collective-permute-start.5 = (bf16[24,8,128]{2,1,0:T(8,128)(2,1)S(1)}, bf16[24,8,128]{2,1,0:T(8,128)(2,1)S(1)}, u32[]{:S(2)}, u32[]{:S(2)}) collective-permute-start(bf16[24,8,128]{2,1,0:T(8,128)(2,1)S(1)} %pad_maximum_fusion.2), channel_id=1, source_target_pairs={{0,65},{1,66},{2,67},{5,68},{6,69},{7,70},{8,73},{9,74},{10,75},{1... | collective-permute-start | bytes 147464 | tf_op jit(solution)/shard_map/ppermute | solution.py:196
  12.4 1.9 %collective-permute-start.4 = (bf16[24,8,128]{2,1,0:T(8,128)(2,1)S(1)}, bf16[24,8,128]{2,1,0:T(8,128)(2,1)S(1)}, u32[]{:S(2)}, u32[]{:S(2)}) collective-permute-start(bf16[24,8,128]{2,1,0:T(8,128)(2,1)S(1)} %pad_maximum_fusion.2), channel_id=1, source_target_pairs={{0,1},{1,2},{2,3},{5,4},{6,5},{7,6},{8,9},{9,10},{10,11},{13,12},{... | collective-permute-start | bytes 147464 | tf_op jit(solution)/shard_map/ppermute | solution.py:196
  14.4 1.0 %collective-permute-done.5 = bf16[24,8,128]{2,1,0:T(8,128)(2,1)S(1)} collective-permute-done((bf16[24,8,128]{2,1,0:T(8,128)(2,1)S(1)}, bf16[24,8,128]{2,1,0:T(8,128)(2,1)S(1)}, u32[]{:S(2)}, u32[]{:S(2)}) %collective-permute-start.5) | collective-permute-done | bytes 49184 | tf_op jit(solution)/shard_map/ppermute | solution.py:196
  15.4 2.2 %collective-permute-done.4 = bf16[24,8,128]{2,1,0:T(8,128)(2,1)S(1)} collective-permute-done((bf16[24,8,128]{2,1,0:T(8,128)(2,1)S(1)}, bf16[24,8,128]{2,1,0:T(8,128)(2,1)S(1)}, u32[]{:S(2)}, u32[]{:S(2)}) %collective-permute-start.4) | collective-permute-done | bytes 49184 | tf_op jit(solution)/shard_map/ppermute | solution.py:196
  17.6 2.5 %collective-permute-start.6 = (bf16[2,2,12,8,128]{4,3,2,1,0:T(8,128)(2,1)S(1)}, bf16[2,2,12,8,128]{4,3,2,1,0:T(8,128)(2,1)S(1)}, u32[]{:S(2)}, u32[]{:S(2)}) collective-permute-start(bf16[2,2,12,8,128]{4,3,2,1,0:T(8,128)(2,1)S(1)} %pad_maximum_fusion.1), channel_id=1, source_target_pairs={{0,4},{1,5},{2,6},{3,7},{4,0},{5,1},{6,2},{7,3},{8,12},{9,13},{10,... | collective-permute-start | bytes 294920 | tf_op jit(solution)/shard_map/ppermute | solution.py:196
  20.0 0.0 collective-permute-done.ta
  20.0 0.0 copy-start
  20.1 0.9 %collective-permute-done.6 = bf16[2,2,12,8,128]{4,3,2,1,0:T(8,128)(2,1)S(1)} collective-permute-done((bf16[2,2,12,8,128]{4,3,2,1,0:T(8,128)(2,1)S(1)}, bf16[2,2,12,8,128]{4,3,2,1,0:T(8,128)(2,1)S(1)}, u32[]{:S(2)}, u32[]{:S(2)}) %collective-permute-start.6) | collective-permute-done | bytes 98336 | tf_op jit(solution)/shard_map/ppermute | solution.py:196
  21.0 0.1 reverse_select_fusion
  21.1 0.0 copy-start.1
  21.1 5.0 %collective-permute-start.7 = (bf16[90,8,128]{2,1,0:T(8,128)(2,1)S(1)}, bf16[90,8,128]{2,1,0:T(8,128)(2,1)S(1)}, u32[]{:S(2)}, u32[]{:S(2)}) collective-permute-start(bf16[90,8,128]{2,1,0:T(8,128)(2,1)S(1)} %pad_maximum_fusion), channel_id=1, source_target_pairs={{4,8},{5,9},{6,10},{7,11},{8,4},{9,5},{10,6},{11,7},{12,16},{13,17... | collective-permute-start | bytes 552968 | tf_op jit(solution)/shard_map/ppermute | solution.py:196
  26.1 1.9 %collective-permute-start.3 = (bf16[78,8,128]{2,1,0:T(8,128)(2,1)}, bf16[78,8,128]{2,1,0:T(8,128)(2,1)S(1)}, u32[]{:S(2)}, u32[]{:S(2)}) collective-permute-start(bf16[78,8,128]{2,1,0:T(8,128)(2,1)} %get-tuple-element.13), channel_id=1, source_target_pairs={{4,8},{5,9},{6,10},{7,11},{8,4},{9,5},{10,6},{11,7},{12,16},{13,17... | collective-permute-start | bytes 479240 | tf_op jit(solution)/shard_map/ppermute | solution.py:196
  28.1 0.1 collective-permute-start.2
  28.2 6.0 %collective-permute-done.3.cr = bf16[78,8,128]{2,1,0:T(8,128)(2,1)S(1)} collective-permute-done((bf16[78,8,128]{2,1,0:T(8,128)(2,1)}, bf16[78,8,128]{2,1,0:T(8,128)(2,1)S(1)}, u32[]{:S(2)}, u32[]{:S(2)}) %collective-permute-start.3) | collective-permute-done | bytes 159776 | tf_op jit(solution)/shard_map/ppermute | solution.py:196
  34.1 0.0 copy-start.6
  34.1 0.0 collective-permute-done.2.on_prev
  34.1 0.0 copy-start.7
  34.1 0.0 collective-permute-done.7.cr_prev
  34.2 0.0 copy-start.5
  34.2 0.0 copy-done.4
  34.2 0.0 copy-done
  34.2 0.0 copy-done.1
  34.2 0.6 copy-done.6
  34.8 0.1 copy-done.7
  34.9 0.0 copy-done.5
  34.9 8.0 %middle.1 = (bf16[9,112,128]{2,1,0:T(8,128)(2,1)}, bf16[9,112,128]{2,1,0:T(8,128)(2,1)}) custom-call(s32[4]{0:T(128)} %pad_add_fusion.flags, bf16[2,6,104,128]{3,2,1,0:T(8,128)(2,1)} %get-tuple-element.11.mine, bf16[2,6,104,128]{3,2,1,0:T(8,128)(2,1)} %copy-done, bf16[90,8,128]{2,1,0:T(8,128)(2,1)} %copy-done.4, bf16[78,8,128]{2,1,0:T(8,128)(2,1)} %copy-done.7, ...), custom_call_target="tpu_custom_call" | custom-call | tf_op jit(solution)/shard_map/middle/pallas_call | solution.py:231
  43.0 0.1 collective-permute-start.8
  43.1 2.0 %collective-permute-start.9 = (bf16[9,112,128]{2,1,0:T(8,128)(2,1)}, bf16[9,112,128]{2,1,0:T(8,128)(2,1)S(1)}, u32[]{:S(2)}, u32[]{:S(2)}) collective-permute-start(bf16[9,112,128]{2,1,0:T(8,128)(2,1)} %get-tuple-element.16.mine_cr), channel_id=1, source_target_pairs={{4,8},{5,9},{6,10},{7,11},{8,4},{9,5},{10,6},{11,7},{12,16},{13,17... | collective-permute-start | bytes 774152 | tf_op jit(solution)/shard_map/ppermute | solution.py:196
  45.1 0.0 collective-permute-done.8.on
  45.1 0.0 copy-start.2
  45.1 7.0 %collective-permute-done.9.cr = bf16[9,112,128]{2,1,0:T(8,128)(2,1)S(1)} collective-permute-done((bf16[9,112,128]{2,1,0:T(8,128)(2,1)}, bf16[9,112,128]{2,1,0:T(8,128)(2,1)S(1)}, u32[]{:S(2)}, u32[]{:S(2)}) %collective-permute-start.9) | collective-permute-done | bytes 258080 | tf_op jit(solution)/shard_map/ppermute | solution.py:196
  52.1 0.0 copy-start.3
  52.1 0.0 copy-done.2
  52.1 0.7 %copy-done.3 = bf16[9,112,128]{2,1,0:T(8,128)(2,1)} copy-done((bf16[9,112,128]{2,1,0:T(8,128)(2,1)}, bf16[9,112,128]{2,1,0:T(8,128)(2,1)S(1)}, u32[]{:S(2)}) %copy-start.3) | copy-done | bytes 258072
  52.8 6.7 %last.1 = bf16[4,2,104,192]{3,2,1,0:T(8,128)(2,1)} custom-call(s32[4]{0:T(128)} %pad_add_fusion.flags, bf16[9,112,128]{2,1,0:T(8,128)(2,1)} %get-tuple-element.15.mine_on, bf16[9,112,128]{2,1,0:T(8,128)(2,1)} %get-tuple-element.16.mine_cr, bf16[9,112,128]{2,1,0:T(8,128)(2,1)} %copy-done.2, bf16[9,112,128]{2,1,0:T(8,128)(2,1)} %copy-done.3, ...), custom_call_target="tpu_custom_call" | custom-call | tf_op jit(solution)/shard_map/last/pallas_call | solution.py:241
  59.5 2.0 %copy.10 = bf16[4,2,104,192]{2,3,1,0:T(8,128)(2,1)} copy(bf16[4,2,104,192]{3,2,1,0:T(8,128)(2,1)} %last.1) | data formatting | bytes 638976 | tf_op jit(solution)/shard_map/last/pallas_call | solution.py:241
  (6 shorter events, 0.1 us)
Async XLA Ops:
  4.8 3.9 %collective-permute-start.1 = (bf16[90,8,128]{2,1,0:T(8,128)(2,1)}, bf16[90,8,128]{2,1,0:T(8,128)(2,1)S(1)}, u32[]{:S(2)}, u32[]{:S(2)}) collective-permute-start(bf16[90,8,128]{2,1,0:T(8,128)(2,1)} %get-tuple-element.12), channel_id=1, source_target_pairs={{0,4},{1,5},{2,6},{3,7},{4,0},{5,1},{6,2},{7,3},{8,12},{9,13},{10,... | collective-permute-start | bytes 552968 | tf_op jit(solution)/shard_map/ppermute | solution.py:196
  5.5 14.5 %collective-permute-start = (bf16[2,6,104,128]{3,2,1,0:T(8,128)(2,1)}, bf16[2,6,104,128]{3,2,1,0:T(8,128)(2,1)S(1)}, u32[]{:S(2)}, u32[]{:S(2)}) collective-permute-start(bf16[2,6,104,128]{3,2,1,0:T(8,128)(2,1)} %get-tuple-element.11.mine), channel_id=1, source_target_pairs={{0,64},{1,65},{2,66},{3,67},{4,68},{5,69},{6,70},{7,71},{8,72},{9,... | collective-permute-start | bytes 958472 | tf_op jit(solution)/shard_map/ppermute | solution.py:196
  8.7 25.4 %copy-start.4 = (bf16[90,8,128]{2,1,0:T(8,128)(2,1)}, bf16[90,8,128]{2,1,0:T(8,128)(2,1)S(1)}, u32[]{:S(2)}) copy-start(bf16[90,8,128]{2,1,0:T(8,128)(2,1)S(1)} %collective-permute-done.1.on) | copy-start | bytes 552964
  9.5 5.8 %collective-permute-start.5 = (bf16[24,8,128]{2,1,0:T(8,128)(2,1)S(1)}, bf16[24,8,128]{2,1,0:T(8,128)(2,1)S(1)}, u32[]{:S(2)}, u32[]{:S(2)}) collective-permute-start(bf16[24,8,128]{2,1,0:T(8,128)(2,1)S(1)} %pad_maximum_fusion.2), channel_id=1, source_target_pairs={{0,65},{1,66},{2,67},{5,68},{6,69},{7,70},{8,73},{9,74},{10,75},{1... | collective-permute-start | bytes 147464 | tf_op jit(solution)/shard_map/ppermute | solution.py:196
  12.4 5.1 %collective-permute-start.4 = (bf16[24,8,128]{2,1,0:T(8,128)(2,1)S(1)}, bf16[24,8,128]{2,1,0:T(8,128)(2,1)S(1)}, u32[]{:S(2)}, u32[]{:S(2)}) collective-permute-start(bf16[24,8,128]{2,1,0:T(8,128)(2,1)S(1)} %pad_maximum_fusion.2), channel_id=1, source_target_pairs={{0,1},{1,2},{2,3},{5,4},{6,5},{7,6},{8,9},{9,10},{10,11},{13,12},{... | collective-permute-start | bytes 147464 | tf_op jit(solution)/shard_map/ppermute | solution.py:196
  17.6 3.4 %collective-permute-start.6 = (bf16[2,2,12,8,128]{4,3,2,1,0:T(8,128)(2,1)S(1)}, bf16[2,2,12,8,128]{4,3,2,1,0:T(8,128)(2,1)S(1)}, u32[]{:S(2)}, u32[]{:S(2)}) collective-permute-start(bf16[2,2,12,8,128]{4,3,2,1,0:T(8,128)(2,1)S(1)} %pad_maximum_fusion.1), channel_id=1, source_target_pairs={{0,4},{1,5},{2,6},{3,7},{4,0},{5,1},{6,2},{7,3},{8,12},{9,13},{10,... | collective-permute-start | bytes 294920 | tf_op jit(solution)/shard_map/ppermute | solution.py:196
  20.0 14.1 %copy-start = (bf16[2,6,104,128]{3,2,1,0:T(8,128)(2,1)}, bf16[2,6,104,128]{3,2,1,0:T(8,128)(2,1)S(1)}, u32[]{:S(2)}) copy-start(bf16[2,6,104,128]{3,2,1,0:T(8,128)(2,1)S(1)} %collective-permute-done.ta) | copy-start | bytes 958468
  21.1 13.1 %copy-start.1 = (bf16[2,2,12,8,128]{4,3,2,1,0:T(8,128)(2,1)}, bf16[2,2,12,8,128]{4,3,2,1,0:T(8,128)(2,1)S(1)}, u32[]{:S(2)}) copy-start(bf16[2,2,12,8,128]{4,3,2,1,0:T(8,128)(2,1)S(1)} %reverse_select_fusion) | copy-start | bytes 294916
  21.1 13.0 %collective-permute-start.7 = (bf16[90,8,128]{2,1,0:T(8,128)(2,1)S(1)}, bf16[90,8,128]{2,1,0:T(8,128)(2,1)S(1)}, u32[]{:S(2)}, u32[]{:S(2)}) collective-permute-start(bf16[90,8,128]{2,1,0:T(8,128)(2,1)S(1)} %pad_maximum_fusion), channel_id=1, source_target_pairs={{4,8},{5,9},{6,10},{7,11},{8,4},{9,5},{10,6},{11,7},{12,16},{13,17... | collective-permute-start | bytes 552968 | tf_op jit(solution)/shard_map/ppermute | solution.py:196
  26.1 8.0 %collective-permute-start.3 = (bf16[78,8,128]{2,1,0:T(8,128)(2,1)}, bf16[78,8,128]{2,1,0:T(8,128)(2,1)S(1)}, u32[]{:S(2)}, u32[]{:S(2)}) collective-permute-start(bf16[78,8,128]{2,1,0:T(8,128)(2,1)} %get-tuple-element.13), channel_id=1, source_target_pairs={{4,8},{5,9},{6,10},{7,11},{8,4},{9,5},{10,6},{11,7},{12,16},{13,17... | collective-permute-start | bytes 479240 | tf_op jit(solution)/shard_map/ppermute | solution.py:196
  28.1 6.1 %collective-permute-start.2 = (bf16[78,8,128]{2,1,0:T(8,128)(2,1)S(1)}, bf16[78,8,128]{2,1,0:T(8,128)(2,1)S(1)}, u32[]{:S(2)}, u32[]{:S(2)}) collective-permute-start(bf16[78,8,128]{2,1,0:T(8,128)(2,1)S(1)} %bitcast.22), channel_id=1, source_target_pairs={{0,4},{1,5},{2,6},{3,7},{4,0},{5,1},{6,2},{7,3},{8,12},{9,13},{10,... | collective-permute-start | bytes 479240 | tf_op jit(solution)/shard_map/ppermute | solution.py:196
  34.1 0.7 %copy-start.6 = (bf16[78,8,128]{2,1,0:T(8,128)(2,1)}, bf16[78,8,128]{2,1,0:T(8,128)(2,1)S(1)}, u32[]{:S(2)}) copy-start(bf16[78,8,128]{2,1,0:T(8,128)(2,1)S(1)} %collective-permute-done.3.cr) | copy-start | bytes 479236
  34.1 0.7 %copy-start.7 = (bf16[78,8,128]{2,1,0:T(8,128)(2,1)}, bf16[78,8,128]{2,1,0:T(8,128)(2,1)S(1)}, u32[]{:S(2)}) copy-start(bf16[78,8,128]{2,1,0:T(8,128)(2,1)S(1)} %collective-permute-done.2.on_prev) | copy-start | bytes 479236
  34.2 0.8 %copy-start.5 = (bf16[90,8,128]{2,1,0:T(8,128)(2,1)}, bf16[90,8,128]{2,1,0:T(8,128)(2,1)S(1)}, u32[]{:S(2)}) copy-start(bf16[90,8,128]{2,1,0:T(8,128)(2,1)S(1)} %collective-permute-done.7.cr_prev) | copy-start | bytes 552964
  43.0 2.1 %collective-permute-start.8 = (bf16[9,112,128]{2,1,0:T(8,128)(2,1)}, bf16[9,112,128]{2,1,0:T(8,128)(2,1)S(1)}, u32[]{:S(2)}, u32[]{:S(2)}) collective-permute-start(bf16[9,112,128]{2,1,0:T(8,128)(2,1)} %get-tuple-element.15.mine_on), channel_id=1, source_target_pairs={{0,4},{1,5},{2,6},{3,7},{4,0},{5,1},{6,2},{7,3},{8,12},{9,13},{10,... | collective-permute-start | bytes 774152 | tf_op jit(solution)/shard_map/ppermute | solution.py:196
  43.1 9.1 %collective-permute-start.9 = (bf16[9,112,128]{2,1,0:T(8,128)(2,1)}, bf16[9,112,128]{2,1,0:T(8,128)(2,1)S(1)}, u32[]{:S(2)}, u32[]{:S(2)}) collective-permute-start(bf16[9,112,128]{2,1,0:T(8,128)(2,1)} %get-tuple-element.16.mine_cr), channel_id=1, source_target_pairs={{4,8},{5,9},{6,10},{7,11},{8,4},{9,5},{10,6},{11,7},{12,16},{13,17... | collective-permute-start | bytes 774152 | tf_op jit(solution)/shard_map/ppermute | solution.py:196
  45.1 7.0 %copy-start.2 = (bf16[9,112,128]{2,1,0:T(8,128)(2,1)}, bf16[9,112,128]{2,1,0:T(8,128)(2,1)S(1)}, u32[]{:S(2)}) copy-start(bf16[9,112,128]{2,1,0:T(8,128)(2,1)S(1)} %collective-permute-done.8.on) | copy-start | bytes 774148
  52.1 0.7 %copy-start.3 = (bf16[9,112,128]{2,1,0:T(8,128)(2,1)}, bf16[9,112,128]{2,1,0:T(8,128)(2,1)S(1)}, u32[]{:S(2)}) copy-start(bf16[9,112,128]{2,1,0:T(8,128)(2,1)S(1)} %collective-permute-done.9.cr) | copy-start | bytes 774148
where the time goes:
time: 62.3 us; the launch traced here: 61.5 us
  starting transfers between devices  20.2 us (32%)
  Pallas kernels  17.1 us (27%)
  waiting for transfers between devices  17.1 us (27%)
  local copies, waits for them, and re-layouts  5.37 us (9%)
  other arithmetic  1.48 us (2%)
    ppermute x10, starting transfers between devices, send(): return lax.ppermute(array, axes, routes(sizes, move))  20.2 us
    ppermute x10, waiting for transfers between devices, send(): return lax.ppermute(array, axes, routes(sizes, move))  17.1 us
    pallas_call x1, Pallas kernels, local(): pl.pallas_call(middle_kernel, out_shape=(shape(9, CYC, LANE), shape(9, CY...  8.03 us
    pallas_call x1, Pallas kernels, local(): pl.pallas_call(last_kernel, out_shape=jax.ShapeDtypeStruct(features.shape...  6.72 us
    unnamed x17, local copies, waits for them, and re-layouts  3.39 us
    pallas_call x1, Pallas kernels, local(): pl.pallas_call(first_kernel, out_shape=(shape(2, 6, COLS, LANE), shape(sl...  2.32 us
    pallas_call x1, local copies, waits for them, and re-layouts, local(): pl.pallas_call(last_kernel, out_shape=jax.ShapeDtypeStruct(features.shape...  1.95 us
  transfers between devices with their start and end apart: 10, of which 5 were waited for; matrix products, arithmetic and copies ran while one was open for 1% of the time, Pallas kernels for 0%

commit v1 on v0

v1 whole, which is shorter than its diff:
```python
import functools

import jax
import jax.numpy as jnp
from jax import lax
from jax.experimental import pallas as pl
from jax.experimental.pallas import tpu as pltpu
from jax.sharding import PartitionSpec as P


epsilon = 1e-06
axes = ("ta", "gy", "gx")
ROWS, COLS, TILE, CYC, CH, LANE = 2, 104, 8, 112, 192, 128
HI = CH - LANE
TILES = COLS // TILE
VMEM = pl.BlockSpec(memory_space=pltpu.VMEM)
ANY = pl.BlockSpec(memory_space=pl.ANY)
SLABS = 6 * TILES
params = pltpu.CompilerParams(vmem_limit_bytes=16 << 20)


def silu(u):
    return u / (1.0 + jnp.exp(-u))


def pack(even, odd):
    high = jnp.concatenate([even[:, LANE:], odd[:, LANE:]], axis=1)
    return even[:, :LANE], odd[:, :LANE], high


def core_index():
    return lax.rem(lax.axis_index("gy"), 2)


def row_of(slot, core):
    return jnp.where(core == 0, 1 - slot, slot)


def load_weights(kernel, weight, sems, core):
    copies = []
    for q in range(3):
        source = jnp.where(core == 0, 2 - q, q)
        base = (0, 4, 9)[q]
        copies.append((kernel.at[:, source, :, :LANE, :], weight.at[:, base : base + 3]))
        for r in range(3):
            tile, half = (base + 3, r) if r < 2 else ((8, 0), (8, 1), (13, 0))[q]
            copies.append((kernel.at[:, source, r, LANE:, :], weight.at[:, tile, HI * half : HI * (half + 1), :]))
    copies = [pltpu.make_async_copy(a, b, sems.at[n]) for n, (a, b) in enumerate(copies)]
    for c in copies:
        c.start()
    weight[:, 13, HI:, :] = jnp.zeros((3, HI, CH), jnp.bfloat16)
    return copies


def first_kernel(feat, gain, kernel, mine, on, cr, edge, weight, sems):
    core = core_index()
    copies = load_weights(kernel, weight, sems, core)
    frames = feat.shape[0]
    for slot in range(ROWS):
        row = row_of(slot, core)
        for f in range(0, frames, 2):
            pair = []
            for e in range(2):
                field = feat[f + e, row].astype(jnp.float32)
                meansq = jnp.mean(field * field, axis=0, keepdims=True)
                normed = (field * lax.rsqrt(meansq + epsilon)).T
                pair.append(silu(normed * gain[...]).astype(jnp.bfloat16))
            for k, slab in enumerate(pack(*pair)):
                n = 3 * (f // 2) + k
                mine[slot, n] = slab
                left, right = slab[:TILE], slab[COLS - TILE :]
                edge[slot, n] = jnp.where(core == 0, right, left)
                on[SLABS + slot * 6 + n] = jnp.where(core == 0, left, right)
                (cr if slot else on)[n * TILES : (n + 1) * TILES] = slab.reshape(TILES, TILE, LANE)
    for c in copies:
        c.wait()


def rolled(x, by):
    return jnp.concatenate([x[-by:], x[:-by]], axis=0)


def put_row(taps, row, f, low, high):
    for e in range(2):
        taps[row, f + e, :, 0:128] = rolled(low[e], 1)
        taps[row, f + e, :, 128:256] = low[e]
        taps[row, f + e, :, 256:384] = rolled(low[e], -1)
    before, after = rolled(high, 1), rolled(high, -1)
    for e in range(2):
        half = slice(HI * e, HI * (e + 1))
        taps[row, f + e, :, 384:448] = before[:, half]
        taps[row, f + e, :, 448:512] = high[:, half]
        taps[row, f + e, :, 512:576] = after[:, half]
        if row > 0:
            taps[row - 1, f + e, :, 576:640] = after[:, half]
        if row in (0, 2):
            taps[row, f + e, :, 576:640] = after[:, half]


def matmul(cells, weight):
    cells = cells.reshape(cells.shape[0] * CYC, cells.shape[-1])
    return jnp.dot(cells, weight.reshape(-1, CH), preferred_element_type=jnp.float32)


def taps_total(taps, weight, f, count, part):
    total = None
    for p in range(3):
        span = slice(f + p, f + p + count)
        if part == "all":
            cells = [taps[0, span, :, :512], taps[1, span, :, :512], taps[0, span, :, 512:], taps[2, span]]
            k = weight[p]
        elif part == "near":
            cells = [taps[1, span, :, :512], taps[2, span, :, :512], taps[1, span, :, 512:]]
            k = weight[p, :9]
        else:
            cells = [taps[0, span]]
            k = weight[p, 9:]
        term = matmul(jnp.concatenate(cells, axis=-1), k)
        total = term if total is None else total + term
    return total


def put_second(out, total, f, bias, gain):
    gx = lax.axis_index("gx")
    col = lax.broadcasted_iota(jnp.int32, (CYC, 1), 0)
    drop = ((col == COLS) & (gx == lax.axis_size("gx") - 1)) | ((col == CYC - 1) & (gx == 0))
    if f == 0:
        drop = drop | (lax.axis_index("ta") == 0)
    middle = (total + bias[...]).astype(jnp.bfloat16).astype(jnp.float32)
    meansq = jnp.mean(middle * middle, axis=-1, keepdims=True)
    second = silu(middle * lax.rsqrt(meansq + epsilon) * gain[...])
    pair = [jnp.where(drop, 0.0, second[e * CYC : (e + 1) * CYC]).astype(jnp.bfloat16) for e in range(2)]
    for k, slab in enumerate(pack(*pair)):
        out[3 * (f // 2) + k] = slab


def tiles(ref, n, tip):
    return jnp.concatenate([ref[n * TILES : (n + 1) * TILES].reshape(COLS, LANE), tip], axis=0)


def middle_near(mine, ta, on, on_prev, rim, weight, bias, gain, kernel, out, partial, weight_next, taps, sems):
    copies = load_weights(kernel, weight_next, sems, core_index())
    for half in range(2):
        for pair in range(2):
            for row in range(3):
                slabs = []
                for n in range(3 * pair, 3 * pair + 3):
                    if row == 0:
                        slabs.append(tiles(on if half else on_prev, n, rim[1 - half, 2, n]))
                    else:
                        body = (mine if half else ta)[row - 1, n]
                        slabs.append(jnp.concatenate([body, rim[1 - half, row - 1, n]], axis=0))
                put_row(taps, row, 4 * half + 2 * pair, slabs[:2], slabs[2])
    for f in range(0, 6, 2):
        put_second(out, taps_total(taps, weight, f, 2, "all"), f, bias, gain)
    for f in range(0, 6, 2):
        partial[f * CYC : (f + 2) * CYC] = taps_total(taps, weight, f, 2, "near")
    for c in copies:
        c.wait()


def middle_far(cr, partial, weight, bias, gain, out, taps):
    for half in range(2):
        for pair in range(2):
            slabs = []
            for n in range(3 * pair, 3 * pair + 3):
                tip = cr[2 * SLABS + (1 - half) * 6 + n]
                slabs.append(tiles(cr, n + 6 * (1 - half), tip))
            put_row(taps, 0, 4 * half + 2 * pair, slabs[:2], slabs[2])
    for f in range(0, 6, 2):
        total = partial[f * CYC : (f + 2) * CYC] + taps_total(taps, weight, f, 2, "far")
        put_second(out, total, f, bias, gain)


def put_last(store, total, feat, f, row, bias):
    total = total + bias[...]
    for e in range(2):
        cells = total[e * CYC : (e + 1) * CYC].T[:, :COLS] + feat[f + e, row].astype(jnp.float32)
        store(f + e, cells.astype(jnp.bfloat16))


def last_near(mine_on, mine_cr, on, feat, weight, bias, out, partial, taps):
    for f in range(0, 6, 2):
        n = 3 * (f // 2)
        for row, ref in enumerate((on, mine_on, mine_cr)):
            put_row(taps, row, f, [ref[n], ref[n + 1]], ref[n + 2])

    def store(f, cells):
        out[f] = cells

    for f in range(0, 4, 2):
        put_last(store, taps_total(taps, weight, f, 2, "all"), feat, f, row_of(0, core_index()), bias)
    for f in range(0, 4, 2):
        partial[f * CYC : (f + 2) * CYC] = taps_total(taps, weight, f, 2, "near")


def last_far(cr, partial, near, feat, weight, bias, out, taps):
    core = core_index()
    for f in range(0, 6, 2):
        n = 3 * (f // 2)
        put_row(taps, 0, f, [cr[n], cr[n + 1]], cr[n + 2])
    for f in range(out.shape[0]):
        out[f, row_of(0, core)] = near[f]

    def store(f, cells):
        out[f, row_of(1, core)] = cells

    for f in range(0, 4, 2):
        total = partial[f * CYC : (f + 2) * CYC] + taps_total(taps, weight, f, 2, "far")
        put_last(store, total, feat, f, row_of(1, core), bias)


def held(*dims, dtype=jnp.bfloat16):
    return pltpu.VMEM(dims, dtype)


def call(name, body, ins, outs, taps=None, sems=False):
    scratch = [] if taps is None else [held(*taps, CYC, 640)]
    if sems:
        scratch.append(pltpu.SemaphoreType.DMA((12,)))
    return pl.pallas_call(
        body,
        out_shape=outs,
        in_specs=[ANY if a.ndim == 5 and a.shape[0] == 3 else VMEM for a in ins],
        out_specs=jax.tree.map(lambda _: VMEM, outs),
        scratch_shapes=scratch,
        compiler_params=params,
        name=name,
    )(*ins)


def routes(sizes, move):
    pairs = []
    for t in range(sizes[0]):
        for y in range(sizes[1]):
            for x in range(sizes[2]):
                to = move(t, y, x)
                if all(0 <= a < n for a, n in zip(to, sizes)):
                    ids = [(i * sizes[1] + j) * sizes[2] + k for i, j, k in ((t, y, x), to)]
                    pairs.append(tuple(ids))
    return pairs


def local(sizes, features, gain_first, kernel_first, bias_first, gain_second, kernel_second, bias_second):
    def send(array, move):
        return lax.ppermute(array, axes, routes(sizes, move))

    def chip(array):
        return send(array, lambda t, y, x: (t, y ^ 1, x))

    def cross(array):
        return send(array, lambda t, y, x: (t, y + 1 if y % 2 else y - 1, x))

    row = lambda v: v.reshape(1, CH)
    feat = jnp.swapaxes(features, 2, 3)
    weights = held(3, 14, LANE, CH)
    second = held(9, CYC, LANE)

    mine, on_row, cr_row, edge, weight = call(
        "first",
        first_kernel,
        (feat, row(gain_first), kernel_first),
        (held(2, 6, COLS, LANE), held(SLABS + 12, TILE, LANE), held(SLABS, TILE, LANE), held(2, 6, TILE, LANE), weights),
        sems=True,
    )
    on = chip(on_row)
    ta = send(mine, lambda t, y, x: (t + 1, y, x))
    edges = jnp.concatenate([edge.reshape(12, TILE, LANE), on[SLABS:]])
    side = send(edges, lambda t, y, x: (t, y, x - 1 if y % 2 else x + 1))
    side_prev = send(edges, lambda t, y, x: (t + 1, y, x - 1 if y % 2 else x + 1))
    sides = jnp.stack([side, side_prev]).reshape(2, 2, 12, TILE, LANE)
    others = chip(sides)[:, ::-1]
    upper = lax.broadcasted_iota(jnp.int32, sides.shape, 3) < TILE // 2
    rim = jnp.where(upper == (core_index() == 0), others, sides).reshape(2, 4, 6, TILE, LANE)
    on_prev = chip(ta[0].reshape(SLABS, TILE, LANE))
    cr = cross(jnp.concatenate([cr_row, ta[1].reshape(SLABS, TILE, LANE), rim[:, 1].reshape(12, TILE, LANE)]))

    norms = (row(bias_first), row(gain_second))
    near, partial, weight_next = call(
        "middle_near",
        middle_near,
        (mine, ta, on, on_prev, rim, weight, *norms, kernel_second),
        (second, held(6 * CYC, CH, dtype=jnp.float32), weights),
        taps=(3, 8),
        sems=True,
    )
    far = call("middle_far", middle_far, (cr, partial, weight, *norms), second, taps=(1, 8))

    bias = row(bias_second)
    out_near, partial = call(
        "last_near",
        last_near,
        (near, far, chip(near), feat, weight_next, bias),
        (held(4, CH, COLS), held(4 * CYC, CH, dtype=jnp.float32)),
        taps=(3, 6),
    )
    out = call(
        "last_far",
        last_far,
        (cross(far), partial, out_near, feat, weight_next, bias),
        jax.ShapeDtypeStruct(feat.shape, jnp.bfloat16),
        taps=(1, 6),
    )
    return jnp.swapaxes(out, 2, 3)


def solution(mesh):
    sizes = tuple(mesh.shape[a] for a in axes)
    placed = (P("ta", "gy", "gx", None), P(), P(), P(), P(), P(), P())
    return jax.shard_map(
        functools.partial(local, sizes),
        mesh=mesh,
        in_specs=placed,
        out_specs=P("ta", "gy", "gx", None),
        check_vma=False,
    )
```

time: 62.3 us -> 49.6 us (0.80)
  waiting for transfers between devices: 17.1 us -> 9.36 us
  Pallas kernels: 17.1 us -> 12.5 us
  local copies, waits for them, and re-layouts: 5.37 us -> 7.26 us
  starting transfers between devices: 20.2 us -> 19 us
    ppermute x10 -> x9, waiting for transfers between devices: 17.1 us -> 9.36 us  [send(): return lax.ppermute(array, axes, routes(sizes, move))]
    pallas_call x3 -> x5, Pallas kernels: 17.1 us -> 12.5 us  [call(): pl.pallas_call(body, out_shape=outs, in_specs=[ANY if a.ndim == 5 and a.s...]
    unnamed x17 -> x20, local copies, waits for them, and re-layouts: 3.39 us -> 6.49 us
    pallas_call x1 -> x0, local copies, waits for them, and re-layouts: 1.95 us -> none  [local(): pl.pallas_call(last_kernel, out_shape=jax.ShapeDtypeStruct(features.shape...]
    ppermute x10 -> x9, starting transfers between devices: 20.2 us -> 19 us  [send(): return lax.ppermute(array, axes, routes(sizes, move))]
    slice x2, local copies, waits for them, and re-layouts: 0.03 us -> 0.77 us  [the longest x1 0.74 us: local(): edges = jnp.concatenate([edge.reshape(12, TILE, LANE), on[SLABS:]])]
  transfers between devices with their start and end apart: 10 -> 9, of which waited for: 5 -> 5; matrix products, arithmetic and copies ran while one was open for 1% -> 3% of each run, Pallas kernels for 0% -> 18%
where the time goes in v1:
time: 49.6 us; the launch traced here: 49.2 us
  starting transfers between devices  19 us (38%)
  Pallas kernels  12.5 us (25%)
  waiting for transfers between devices  9.36 us (19%)
  local copies, waits for them, and re-layouts  7.26 us (15%)
  other arithmetic  0.9 us (2%)
    ppermute x9, starting transfers between devices, send(): return lax.ppermute(array, axes, routes(sizes, move))  19 us
    pallas_call x5, Pallas kernels, call(): pl.pallas_call(body, out_shape=outs, in_specs=[ANY if a.ndim == 5 and a.s...  12.5 us
    ppermute x9, waiting for transfers between devices, send(): return lax.ppermute(array, axes, routes(sizes, move))  9.36 us
    unnamed x20, local copies, waits for them, and re-layouts  6.49 us
  transfers between devices with their start and end apart: 9, of which 5 were waited for; matrix products, arithmetic and copies ran while one was open for 3% of the time, Pallas kernels for 18%

profile of v1, /device:TPU:107, one launch (start us, length us, event | category | flops | bytes accessed | tf_op | source)
XLA Modules:
  0.0 49.2 jit_solution(3457221225989654465)
XLA Ops:
  0.0 0.0 copy-start.5
  0.0 0.0 copy-start
  0.0 1.0 %copy-done = bf16[4,2,104,192]{2,3,1,0:T(8,128)(2,1)S(1)} copy-done((bf16[4,2,104,192]{2,3,1,0:T(8,128)(2,1)S(1)}, bf16[4,2,104,192]{2,3,1,0:T(8,128)(2,1)}, u32[]{:S(2)}) %copy-start) | copy-done | bytes 319512
  1.0 0.0 copy-start.2
  1.0 1.7 %copy-done.2 = bf16[3,3,3,192,192]{4,3,2,1,0:T(8,128)(2,1)S(1)} copy-done((bf16[3,3,3,192,192]{4,3,2,1,0:T(8,128)(2,1)S(1)}, bf16[3,3,3,192,192]{4,3,2,1,0:T(8,128)(2,1)}, u32[]{:S(2)}) %copy-start.2) | copy-done | bytes 1990680
  2.8 0.0 copy-start.9
  2.8 0.7 %copy-done.9 = f32[192]{0:T(256)S(1)} copy-done((f32[192]{0:T(256)S(1)}, f32[192]{0:T(256)}, u32[]{:S(2)}) %copy-start.9) | copy-done | bytes 792
  3.4 1.8 %first.1 = (bf16[2,6,104,128]{3,2,1,0:T(8,128)(2,1)S(1)}, bf16[90,8,128]{2,1,0:T(8,128)(2,1)}, bf16[78,8,128]{2,1,0:T(8,128)(2,1)S(1)}, bf16[2,6,8,128]{3,2,1,0:T(8,128)(2,1)S(1)}, bf16[3,14,128,192]{3,2,1,0:T(8,128)(2,1)S(1)}) custom-call(bf16[4,2,192,104]{3,2,1,0:T(8,128)(2,1)S(1)} %bitcast.13, f32[1,192]{1,0:T(1,128)S(1)} %bitcast.25, ...), custom_call_target="tpu_custom_call" | custom-call | tf_op jit(solution)/shard_map/first/pallas_call | solution.py:221
  5.2 0.0 copy-start.4
  5.2 0.6 %copy-done.4 = bf16[2,6,8,128]{3,2,1,0:T(8,128)(2,1)} copy-done((bf16[2,6,8,128]{3,2,1,0:T(8,128)(2,1)}, bf16[2,6,8,128]{3,2,1,0:T(8,128)(2,1)S(1)}, u32[]{:S(2)}) %copy-start.4) | copy-done | bytes 24600
  5.8 0.7 %collective-permute-start.1 = (bf16[90,8,128]{2,1,0:T(8,128)(2,1)}, bf16[90,8,128]{2,1,0:T(8,128)(2,1)}, u32[]{:S(2)}, u32[]{:S(2)}) collective-permute-start(bf16[90,8,128]{2,1,0:T(8,128)(2,1)} %get-tuple-element.18), channel_id=1, source_target_pairs={{0,4},{1,5},{2,6},{3,7},{4,0},{5,1},{6,2},{7,3},{8,12},{9,13},{10,... | collective-permute-start | bytes 552968 | tf_op jit(solution)/shard_map/ppermute | solution.py:246
  6.5 3.2 %collective-permute-start = (bf16[2,6,104,128]{3,2,1,0:T(8,128)(2,1)S(1)}, bf16[2,6,104,128]{3,2,1,0:T(8,128)(2,1)S(1)}, u32[]{:S(2)}, u32[]{:S(2)}) collective-permute-start(bf16[2,6,104,128]{3,2,1,0:T(8,128)(2,1)S(1)} %get-tuple-element.16.mine), channel_id=1, source_target_pairs={{0,64},{1,65},{2,66},{3,67},{4,68},{5,69},{6,70},{7,71},{8,72},{9,... | collective-permute-start | bytes 958472 | tf_op jit(solution)/shard_map/ppermute | solution.py:246
  9.7 0.0 collective-permute-done.1.on
  9.7 0.7 %slice.17 = bf16[12,8,128]{2,1,0:T(8,128)(2,1)S(1)} slice(bf16[90,8,128]{2,1,0:T(8,128)(2,1)} %collective-permute-done.1.on), slice={[78:90], [0:8], [0:128]} | slice | bytes 49152 | tf_op jit(solution)/shard_map/slice | solution.py:268
  10.5 0.7 %pad_maximum_fusion.2 = bf16[24,8,128]{2,1,0:T(8,128)(2,1)S(1)} fusion(bf16[12,8,128]{2,1,0:T(8,128)(2,1)S(1)} %slice.17, bf16[12,8,128]{2,1,0:T(8,128)(2,1)} %bitcast.18), kind=kLoop, calls=%fused_computation.3 | loop fusion | flops 24576 | bytes 98304 | tf_op jit(solution)/shard_map/concatenate | solution.py:268
  11.2 2.2 %collective-permute-start.2 = (bf16[24,8,128]{2,1,0:T(8,128)(2,1)S(1)}, bf16[24,8,128]{2,1,0:T(8,128)(2,1)S(1)}, u32[]{:S(2)}, u32[]{:S(2)}) collective-permute-start(bf16[24,8,128]{2,1,0:T(8,128)(2,1)S(1)} %pad_maximum_fusion.2), channel_id=1, source_target_pairs={{0,1},{1,2},{2,3},{5,4},{6,5},{7,6},{8,9},{9,10},{10,11},{13,12},{... | collective-permute-start | bytes 147464 | tf_op jit(solution)/shard_map/ppermute | solution.py:246
  13.4 2.0 %collective-permute-start.3 = (bf16[24,8,128]{2,1,0:T(8,128)(2,1)S(1)}, bf16[24,8,128]{2,1,0:T(8,128)(2,1)S(1)}, u32[]{:S(2)}, u32[]{:S(2)}) collective-permute-start(bf16[24,8,128]{2,1,0:T(8,128)(2,1)S(1)} %pad_maximum_fusion.2), channel_id=1, source_target_pairs={{0,65},{1,66},{2,67},{5,68},{6,69},{7,70},{8,73},{9,74},{10,75},{1... | collective-permute-start | bytes 147464 | tf_op jit(solution)/shard_map/ppermute | solution.py:246
  15.4 0.9 %collective-permute-done.2 = bf16[24,8,128]{2,1,0:T(8,128)(2,1)S(1)} collective-permute-done((bf16[24,8,128]{2,1,0:T(8,128)(2,1)S(1)}, bf16[24,8,128]{2,1,0:T(8,128)(2,1)S(1)}, u32[]{:S(2)}, u32[]{:S(2)}) %collective-permute-start.2) | collective-permute-done | bytes 49184 | tf_op jit(solution)/shard_map/ppermute | solution.py:246
  16.3 2.8 %collective-permute-done.3 = bf16[24,8,128]{2,1,0:T(8,128)(2,1)S(1)} collective-permute-done((bf16[24,8,128]{2,1,0:T(8,128)(2,1)S(1)}, bf16[24,8,128]{2,1,0:T(8,128)(2,1)S(1)}, u32[]{:S(2)}, u32[]{:S(2)}) %collective-permute-start.3) | collective-permute-done | bytes 49184 | tf_op jit(solution)/shard_map/ppermute | solution.py:246
  19.1 2.8 %collective-permute-start.4 = (bf16[2,2,12,8,128]{4,3,2,1,0:T(8,128)(2,1)S(1)}, bf16[2,2,12,8,128]{4,3,2,1,0:T(8,128)(2,1)S(1)}, u32[]{:S(2)}, u32[]{:S(2)}) collective-permute-start(bf16[2,2,12,8,128]{4,3,2,1,0:T(8,128)(2,1)S(1)} %pad_maximum_fusion.1), channel_id=1, source_target_pairs={{0,4},{1,5},{2,6},{3,7},{4,0},{5,1},{6,2},{7,3},{8,12},{9,13},{10,... | collective-permute-start | bytes 294920 | tf_op jit(solution)/shard_map/ppermute | solution.py:246
  21.9 0.0 collective-permute-done.ta
  21.9 0.9 %collective-permute-done.4 = bf16[2,2,12,8,128]{4,3,2,1,0:T(8,128)(2,1)S(1)} collective-permute-done((bf16[2,2,12,8,128]{4,3,2,1,0:T(8,128)(2,1)S(1)}, bf16[2,2,12,8,128]{4,3,2,1,0:T(8,128)(2,1)S(1)}, u32[]{:S(2)}, u32[]{:S(2)}) %collective-permute-start.4) | collective-permute-done | bytes 98336 | tf_op jit(solution)/shard_map/ppermute | solution.py:246
  22.8 0.1 reverse_select_fusion
  23.0 5.0 %collective-permute-start.5 = (bf16[168,8,128]{2,1,0:T(8,128)(2,1)S(1)}, bf16[168,8,128]{2,1,0:T(8,128)(2,1)S(1)}, u32[]{:S(2)}, u32[]{:S(2)}) collective-permute-start(bf16[168,8,128]{2,1,0:T(8,128)(2,1)S(1)} %pad_maximum_fusion), channel_id=1, source_target_pairs={{4,8},{5,9},{6,10},{7,11},{8,4},{9,5},{10,6},{11,7},{12,16},{13,17... | collective-permute-start | bytes 1032200 | tf_op jit(solution)/shard_map/ppermute | solution.py:246
  28.0 0.1 collective-permute-start.6
  28.1 1.4 %collective-permute-done.6.on_prev = bf16[78,8,128]{2,1,0:T(8,128)(2,1)S(1)} collective-permute-done((bf16[78,8,128]{2,1,0:T(8,128)(2,1)S(1)}, bf16[78,8,128]{2,1,0:T(8,128)(2,1)S(1)}, u32[]{:S(2)}, u32[]{:S(2)}) %collective-permute-start.6) | collective-permute-done | bytes 159776 | tf_op jit(solution)/shard_map/ppermute | solution.py:246
  29.5 0.0 copy-done.5
  29.5 0.0 copy-start.3
  29.5 1.7 %copy-done.3 = bf16[3,3,3,192,192]{4,3,2,1,0:T(8,128)(2,1)S(1)} copy-done((bf16[3,3,3,192,192]{4,3,2,1,0:T(8,128)(2,1)S(1)}, bf16[3,3,3,192,192]{4,3,2,1,0:T(8,128)(2,1)}, u32[]{:S(2)}) %copy-start.3) | copy-done | bytes 1990680
  31.2 0.0 copy-start.6
  31.2 0.7 %copy-done.6 = f32[192]{0:T(256)S(1)} copy-done((f32[192]{0:T(256)S(1)}, f32[192]{0:T(256)}, u32[]{:S(2)}) %copy-start.6) | copy-done | bytes 792
  31.9 0.0 copy-start.7
  31.9 5.2 %middle_near.1 = (bf16[9,112,128]{2,1,0:T(8,128)(2,1)S(1)}, f32[672,192]{1,0:T(8,128)S(1)}, bf16[3,14,128,192]{3,2,1,0:T(8,128)(2,1)S(1)}) custom-call(bf16[2,6,104,128]{3,2,1,0:T(8,128)(2,1)S(1)} %get-tuple-element.16.mine, bf16[2,6,104,128]{3,2,1,0:T(8,128)(2,1)S(1)} %collective-permute-done.ta, bf16[90,8,128]{2,1,0:T(8,128)(2,1)} %collective-permute-done.1.on, ...), custom_call_target="tpu_custom_call" | custom-call | tf_op jit(solution)/shard_map/middle_near/pallas_call | solution.py:221
  37.1 0.0 copy-start.1
  37.1 0.0 copy-start.8
  37.1 0.2 collective-permute-start.8
  37.4 0.0 collective-permute-done.5.cr
  37.4 0.0 copy-done.7
  37.4 1.3 %middle_far.1.mine_cr = bf16[9,112,128]{2,1,0:T(8,128)(2,1)S(1)} custom-call(bf16[168,8,128]{2,1,0:T(8,128)(2,1)S(1)} %collective-permute-done.5.cr, f32[672,192]{1,0:T(8,128)S(1)} %get-tuple-element.20.partial, bf16[3,14,128,192]{3,2,1,0:T(8,128)(2,1)S(1)} %get-tuple-element.19.weight, f32[1,192]{1,0:T(1,128)S(1)} %bitcast.20, f32[1,192]{1,0:T(1,128)S(1)} %bitcast.22), custom_call_target="tpu_custom_call" | custom-call | tf_op jit(solution)/shard_map/middle_far/pallas_call | solution.py:221
  38.6 2.9 %collective-permute-start.7 = (bf16[9,112,128]{2,1,0:T(8,128)(2,1)S(1)}, bf16[9,112,128]{2,1,0:T(8,128)(2,1)S(1)}, u32[]{:S(2)}, u32[]{:S(2)}) collective-permute-start(bf16[9,112,128]{2,1,0:T(8,128)(2,1)S(1)} %middle_far.1.mine_cr), channel_id=1, source_target_pairs={{4,8},{5,9},{6,10},{7,11},{8,4},{9,5},{10,6},{11,7},{12,16},{13,17... | collective-permute-start | bytes 774152 | tf_op jit(solution)/shard_map/ppermute | solution.py:246
  41.5 0.0 collective-permute-done.8.on
  41.6 0.0 copy-done.1
  41.6 0.0 copy-done.8
  41.6 2.6 %last_near.1 = (bf16[4,192,104]{2,1,0:T(8,128)(2,1)S(1)}, f32[448,192]{1,0:T(8,128)S(1)}) custom-call(bf16[9,112,128]{2,1,0:T(8,128)(2,1)S(1)} %get-tuple-element.21.mine_on, bf16[9,112,128]{2,1,0:T(8,128)(2,1)S(1)} %middle_far.1.mine_cr, bf16[9,112,128]{2,1,0:T(8,128)(2,1)S(1)} %collective-permute-done.8.on, bf16[4,2,192,104]{3,2,1,0:T(8,128)(2,1)S(1)} %bitcast.14, ...), custom_call_target="tpu_custom_call" | custom-call | tf_op jit(solution)/shard_map/last_near/pallas_call | solution.py:221
  44.1 3.4 %collective-permute-done.7.cr = bf16[9,112,128]{2,1,0:T(8,128)(2,1)S(1)} collective-permute-done((bf16[9,112,128]{2,1,0:T(8,128)(2,1)S(1)}, bf16[9,112,128]{2,1,0:T(8,128)(2,1)S(1)}, u32[]{:S(2)}, u32[]{:S(2)}) %collective-permute-start.7) | collective-permute-done | bytes 258080 | tf_op jit(solution)/shard_map/ppermute | solution.py:246
  47.5 1.7 %last_far.1 = bf16[4,2,192,104]{3,2,1,0:T(8,128)(2,1)} custom-call(bf16[9,112,128]{2,1,0:T(8,128)(2,1)S(1)} %collective-permute-done.7.cr, f32[448,192]{1,0:T(8,128)S(1)} %get-tuple-element.23.partial, bf16[4,192,104]{2,1,0:T(8,128)(2,1)S(1)} %get-tuple-element.24.near, bf16[4,2,192,104]{3,2,1,0:T(8,128)(2,1)S(1)} %bitcast.15, ...), custom_call_target="tpu_custom_call" | custom-call | tf_op jit(solution)/shard_map/last_far/pallas_call | solution.py:221
  (5 shorter events, 0.1 us)
Async XLA Ops:
  0.0 29.5 %copy-start.5 = (f32[192]{0:T(256)S(1)}, f32[192]{0:T(256)}, u32[]{:S(2)}) copy-start(f32[192]{0:T(256)} %param.10) | copy-start | bytes 2308
  0.0 1.0 %copy-start = (bf16[4,2,104,192]{2,3,1,0:T(8,128)(2,1)S(1)}, bf16[4,2,104,192]{2,3,1,0:T(8,128)(2,1)}, u32[]{:S(2)}) copy-start(bf16[4,2,104,192]{2,3,1,0:T(8,128)(2,1)} %param.7) | copy-start | bytes 958468
  1.0 1.7 %copy-start.2 = (bf16[3,3,3,192,192]{4,3,2,1,0:T(8,128)(2,1)S(1)}, bf16[3,3,3,192,192]{4,3,2,1,0:T(8,128)(2,1)}, u32[]{:S(2)}) copy-start(bf16[3,3,3,192,192]{4,3,2,1,0:T(8,128)(2,1)} %kernel.2) | copy-start | bytes 5971972
  2.8 0.7 %copy-start.9 = (f32[192]{0:T(256)S(1)}, f32[192]{0:T(256)}, u32[]{:S(2)}) copy-start(f32[192]{0:T(256)} %param.8) | copy-start | bytes 2308
  5.2 0.6 %copy-start.4 = (bf16[2,6,8,128]{3,2,1,0:T(8,128)(2,1)}, bf16[2,6,8,128]{3,2,1,0:T(8,128)(2,1)S(1)}, u32[]{:S(2)}) copy-start(bf16[2,6,8,128]{3,2,1,0:T(8,128)(2,1)S(1)} %get-tuple-element.17) | copy-start | bytes 73732
  5.8 3.9 %collective-permute-start.1 = (bf16[90,8,128]{2,1,0:T(8,128)(2,1)}, bf16[90,8,128]{2,1,0:T(8,128)(2,1)}, u32[]{:S(2)}, u32[]{:S(2)}) collective-permute-start(bf16[90,8,128]{2,1,0:T(8,128)(2,1)} %get-tuple-element.18), channel_id=1, source_target_pairs={{0,4},{1,5},{2,6},{3,7},{4,0},{5,1},{6,2},{7,3},{8,12},{9,13},{10,... | collective-permute-start | bytes 552968 | tf_op jit(solution)/shard_map/ppermute | solution.py:246
  6.5 15.4 %collective-permute-start = (bf16[2,6,104,128]{3,2,1,0:T(8,128)(2,1)S(1)}, bf16[2,6,104,128]{3,2,1,0:T(8,128)(2,1)S(1)}, u32[]{:S(2)}, u32[]{:S(2)}) collective-permute-start(bf16[2,6,104,128]{3,2,1,0:T(8,128)(2,1)S(1)} %get-tuple-element.16.mine), channel_id=1, source_target_pairs={{0,64},{1,65},{2,66},{3,67},{4,68},{5,69},{6,70},{7,71},{8,72},{9,... | collective-permute-start | bytes 958472 | tf_op jit(solution)/shard_map/ppermute | solution.py:246
  11.2 5.1 %collective-permute-start.2 = (bf16[24,8,128]{2,1,0:T(8,128)(2,1)S(1)}, bf16[24,8,128]{2,1,0:T(8,128)(2,1)S(1)}, u32[]{:S(2)}, u32[]{:S(2)}) collective-permute-start(bf16[24,8,128]{2,1,0:T(8,128)(2,1)S(1)} %pad_maximum_fusion.2), channel_id=1, source_target_pairs={{0,1},{1,2},{2,3},{5,4},{6,5},{7,6},{8,9},{9,10},{10,11},{13,12},{... | collective-permute-start | bytes 147464 | tf_op jit(solution)/shard_map/ppermute | solution.py:246
  13.4 5.7 %collective-permute-start.3 = (bf16[24,8,128]{2,1,0:T(8,128)(2,1)S(1)}, bf16[24,8,128]{2,1,0:T(8,128)(2,1)S(1)}, u32[]{:S(2)}, u32[]{:S(2)}) collective-permute-start(bf16[24,8,128]{2,1,0:T(8,128)(2,1)S(1)} %pad_maximum_fusion.2), channel_id=1, source_target_pairs={{0,65},{1,66},{2,67},{5,68},{6,69},{7,70},{8,73},{9,74},{10,75},{1... | collective-permute-start | bytes 147464 | tf_op jit(solution)/shard_map/ppermute | solution.py:246
  19.1 3.7 %collective-permute-start.4 = (bf16[2,2,12,8,128]{4,3,2,1,0:T(8,128)(2,1)S(1)}, bf16[2,2,12,8,128]{4,3,2,1,0:T(8,128)(2,1)S(1)}, u32[]{:S(2)}, u32[]{:S(2)}) collective-permute-start(bf16[2,2,12,8,128]{4,3,2,1,0:T(8,128)(2,1)S(1)} %pad_maximum_fusion.1), channel_id=1, source_target_pairs={{0,4},{1,5},{2,6},{3,7},{4,0},{5,1},{6,2},{7,3},{8,12},{9,13},{10,... | collective-permute-start | bytes 294920 | tf_op jit(solution)/shard_map/ppermute | solution.py:246
  23.0 14.4 %collective-permute-start.5 = (bf16[168,8,128]{2,1,0:T(8,128)(2,1)S(1)}, bf16[168,8,128]{2,1,0:T(8,128)(2,1)S(1)}, u32[]{:S(2)}, u32[]{:S(2)}) collective-permute-start(bf16[168,8,128]{2,1,0:T(8,128)(2,1)S(1)} %pad_maximum_fusion), channel_id=1, source_target_pairs={{4,8},{5,9},{6,10},{7,11},{8,4},{9,5},{10,6},{11,7},{12,16},{13,17... | collective-permute-start | bytes 1032200 | tf_op jit(solution)/shard_map/ppermute | solution.py:246
  28.0 1.5 %collective-permute-start.6 = (bf16[78,8,128]{2,1,0:T(8,128)(2,1)S(1)}, bf16[78,8,128]{2,1,0:T(8,128)(2,1)S(1)}, u32[]{:S(2)}, u32[]{:S(2)}) collective-permute-start(bf16[78,8,128]{2,1,0:T(8,128)(2,1)S(1)} %bitcast.31), channel_id=1, source_target_pairs={{0,4},{1,5},{2,6},{3,7},{4,0},{5,1},{6,2},{7,3},{8,12},{9,13},{10,... | collective-permute-start | bytes 479240 | tf_op jit(solution)/shard_map/ppermute | solution.py:246
  29.5 1.8 %copy-start.3 = (bf16[3,3,3,192,192]{4,3,2,1,0:T(8,128)(2,1)S(1)}, bf16[3,3,3,192,192]{4,3,2,1,0:T(8,128)(2,1)}, u32[]{:S(2)}) copy-start(bf16[3,3,3,192,192]{4,3,2,1,0:T(8,128)(2,1)} %kernel.3) | copy-start | bytes 5971972
  31.2 0.7 %copy-start.6 = (f32[192]{0:T(256)S(1)}, f32[192]{0:T(256)}, u32[]{:S(2)}) copy-start(f32[192]{0:T(256)} %param.11) | copy-start | bytes 2308
  31.9 5.5 %copy-start.7 = (f32[192]{0:T(256)S(1)}, f32[192]{0:T(256)}, u32[]{:S(2)}) copy-start(f32[192]{0:T(256)} %param.11) | copy-start | bytes 2308
  37.1 4.4 %copy-start.1 = (bf16[4,2,104,192]{2,3,1,0:T(8,128)(2,1)S(1)}, bf16[4,2,104,192]{2,3,1,0:T(8,128)(2,1)}, u32[]{:S(2)}) copy-start(bf16[4,2,104,192]{2,3,1,0:T(8,128)(2,1)} %param.7) | copy-start | bytes 958468
  37.1 4.4 %copy-start.8 = (f32[192]{0:T(256)S(1)}, f32[192]{0:T(256)}, u32[]{:S(2)}) copy-start(f32[192]{0:T(256)} %param.13) | copy-start | bytes 2308
  37.1 4.4 %collective-permute-start.8 = (bf16[9,112,128]{2,1,0:T(8,128)(2,1)S(1)}, bf16[9,112,128]{2,1,0:T(8,128)(2,1)S(1)}, u32[]{:S(2)}, u32[]{:S(2)}) collective-permute-start(bf16[9,112,128]{2,1,0:T(8,128)(2,1)S(1)} %get-tuple-element.21.mine_on), channel_id=1, source_target_pairs={{0,4},{1,5},{2,6},{3,7},{4,0},{5,1},{6,2},{7,3},{8,12},{9,13},{10,... | collective-permute-start | bytes 774152 | tf_op jit(solution)/shard_map/ppermute | solution.py:246
  38.6 8.9 %collective-permute-start.7 = (bf16[9,112,128]{2,1,0:T(8,128)(2,1)S(1)}, bf16[9,112,128]{2,1,0:T(8,128)(2,1)S(1)}, u32[]{:S(2)}, u32[]{:S(2)}) collective-permute-start(bf16[9,112,128]{2,1,0:T(8,128)(2,1)S(1)} %middle_far.1.mine_cr), channel_id=1, source_target_pairs={{4,8},{5,9},{6,10},{7,11},{8,4},{9,5},{10,6},{11,7},{12,16},{13,17... | collective-permute-start | bytes 774152 | tf_op jit(solution)/shard_map/ppermute | solution.py:246

commit v2 on v1

--- a/solution.py
+++ b/solution.py
@@ -14,7 +14,7 @@
 HI = CH - LANE
 TILES = COLS // TILE
 VMEM = pl.BlockSpec(memory_space=pltpu.VMEM)
-ANY = pl.BlockSpec(memory_space=pl.ANY)
+HBM = pl.BlockSpec(memory_space=pltpu.HBM)
 SLABS = 6 * TILES
 params = pltpu.CompilerParams(vmem_limit_bytes=16 << 20)
 
@@ -36,31 +36,37 @@
     return jnp.where(core == 0, 1 - slot, slot)
 
 
-def load_weights(kernel, weight, sems, core):
-    copies = []
+def weight_parts(kernel, weight, core):
+    parts = []
     for q in range(3):
         source = jnp.where(core == 0, 2 - q, q)
         base = (0, 4, 9)[q]
-        copies.append((kernel.at[:, source, :, :LANE, :], weight.at[:, base : base + 3]))
+        parts.append((kernel.at[:, source, :, :LANE, :], weight.at[:, base : base + 3]))
         for r in range(3):
             tile, half = (base + 3, r) if r < 2 else ((8, 0), (8, 1), (13, 0))[q]
-            copies.append((kernel.at[:, source, r, LANE:, :], weight.at[:, tile, HI * half : HI * (half + 1), :]))
-    copies = [pltpu.make_async_copy(a, b, sems.at[n]) for n, (a, b) in enumerate(copies)]
+            parts.append((kernel.at[:, source, r, LANE:, :], weight.at[:, tile, HI * half : HI * (half + 1), :]))
+    return parts
+
+
+def fetch(pairs, sems, start=0):
+    copies = [pltpu.make_async_copy(a, b, sems.at[start + n]) for n, (a, b) in enumerate(pairs)]
     for c in copies:
         c.start()
-    weight[:, 13, HI:, :] = jnp.zeros((3, HI, CH), jnp.bfloat16)
     return copies
 
 
-def first_kernel(feat, gain, kernel, mine, on, cr, edge, weight, sems):
+def first_kernel(feat_in, gain_in, mine, on, cr, edge, feat, gain, sems):
     core = core_index()
-    copies = load_weights(kernel, weight, sems, core)
     frames = feat.shape[0]
+    order = [(row_of(slot, core), f) for slot in range(ROWS) for f in range(frames)]
+    copies = fetch([(gain_in, gain)] + [(feat_in.at[f, row], feat.at[f, row]) for row, f in order], sems)
+    copies[0].wait()
     for slot in range(ROWS):
         row = row_of(slot, core)
         for f in range(0, frames, 2):
             pair = []
             for e in range(2):
+                copies[1 + slot * frames + f + e].wait()
                 field = feat[f + e, row].astype(jnp.float32)
                 meansq = jnp.mean(field * field, axis=0, keepdims=True)
                 normed = (field * lax.rsqrt(meansq + epsilon)).T
@@ -69,11 +75,9 @@
                 n = 3 * (f // 2) + k
                 mine[slot, n] = slab
                 left, right = slab[:TILE], slab[COLS - TILE :]
-                edge[slot, n] = jnp.where(core == 0, right, left)
+                edge[slot * 6 + n] = jnp.where(core == 0, right, left)
                 on[SLABS + slot * 6 + n] = jnp.where(core == 0, left, right)
                 (cr if slot else on)[n * TILES : (n + 1) * TILES] = slab.reshape(TILES, TILE, LANE)
-    for c in copies:
-        c.wait()
 
 
 def rolled(x, by):
@@ -138,8 +142,16 @@
     return jnp.concatenate([ref[n * TILES : (n + 1) * TILES].reshape(COLS, LANE), tip], axis=0)
 
 
-def middle_near(mine, ta, on, on_prev, rim, weight, bias, gain, kernel, out, partial, weight_next, taps, sems):
-    copies = load_weights(kernel, weight_next, sems, core_index())
+def middle_near(
+    mine, ta, on, on_prev, rim, kernel, kernel_next, bias_in, gain_in, bias_next_in,
+    out, partial, weight, weight_next, bias, gain, bias_next, taps, sems,
+):
+    core = core_index()
+    vectors = [(bias_in, bias), (gain_in, gain), (bias_next_in, bias_next)]
+    copies = fetch(weight_parts(kernel, weight, core) + vectors, sems)
+    copies_next = fetch(weight_parts(kernel_next, weight_next, core), sems, len(copies))
+    for ref in (weight, weight_next):
+        ref[:, 13, HI:, :] = jnp.zeros((3, HI, CH), jnp.bfloat16)
     for half in range(2):
         for pair in range(2):
             for row in range(3):
@@ -151,11 +163,13 @@
                         body = (mine if half else ta)[row - 1, n]
                         slabs.append(jnp.concatenate([body, rim[1 - half, row - 1, n]], axis=0))
                 put_row(taps, row, 4 * half + 2 * pair, slabs[:2], slabs[2])
+    for c in copies:
+        c.wait()
     for f in range(0, 6, 2):
         put_second(out, taps_total(taps, weight, f, 2, "all"), f, bias, gain)
     for f in range(0, 6, 2):
         partial[f * CYC : (f + 2) * CYC] = taps_total(taps, weight, f, 2, "near")
-    for c in copies:
+    for c in copies_next:
         c.wait()
 
 
@@ -214,19 +228,19 @@
     return pltpu.VMEM(dims, dtype)
 
 
-def call(name, body, ins, outs, taps=None, sems=False):
+def call(name, body, ins, outs, far=(), taps=None, sems=0):
     scratch = [] if taps is None else [held(*taps, CYC, 640)]
     if sems:
-        scratch.append(pltpu.SemaphoreType.DMA((12,)))
+        scratch.append(pltpu.SemaphoreType.DMA((sems,)))
     return pl.pallas_call(
         body,
         out_shape=outs,
-        in_specs=[ANY if a.ndim == 5 and a.shape[0] == 3 else VMEM for a in ins],
+        in_specs=[VMEM for _ in ins] + [HBM for _ in far],
         out_specs=jax.tree.map(lambda _: VMEM, outs),
         scratch_shapes=scratch,
         compiler_params=params,
         name=name,
-    )(*ins)
+    )(*ins, *(pltpu.with_memory_space_constraint(a, pltpu.HBM) for a in far))
 
 
 def routes(sizes, move):
@@ -252,20 +266,22 @@
         return send(array, lambda t, y, x: (t, y + 1 if y % 2 else y - 1, x))
 
     row = lambda v: v.reshape(1, CH)
-    feat = jnp.swapaxes(features, 2, 3)
     weights = held(3, 14, LANE, CH)
     second = held(9, CYC, LANE)
-
-    mine, on_row, cr_row, edge, weight = call(
+    vector = held(1, CH, dtype=jnp.float32)
+    strip, rims = held(SLABS, TILE, LANE), held(12, TILE, LANE)
+
+    mine, on_row, cr_row, edge, feat, _ = call(
         "first",
         first_kernel,
-        (feat, row(gain_first), kernel_first),
-        (held(2, 6, COLS, LANE), held(SLABS + 12, TILE, LANE), held(SLABS, TILE, LANE), held(2, 6, TILE, LANE), weights),
-        sems=True,
+        (),
+        (held(2, 6, COLS, LANE), held(SLABS + 12, TILE, LANE), strip, rims, held(4, 2, CH, COLS), vector),
+        far=(jnp.swapaxes(features, 2, 3), row(gain_first)),
+        sems=9,
     )
     on = chip(on_row)
+    edges = jnp.concatenate([edge, on[SLABS:]])
     ta = send(mine, lambda t, y, x: (t + 1, y, x))
-    edges = jnp.concatenate([edge.reshape(12, TILE, LANE), on[SLABS:]])
     side = send(edges, lambda t, y, x: (t, y, x - 1 if y % 2 else x + 1))
     side_prev = send(edges, lambda t, y, x: (t + 1, y, x - 1 if y % 2 else x + 1))
     sides = jnp.stack([side, side_prev]).reshape(2, 2, 12, TILE, LANE)
@@ -275,29 +291,27 @@
     on_prev = chip(ta[0].reshape(SLABS, TILE, LANE))
     cr = cross(jnp.concatenate([cr_row, ta[1].reshape(SLABS, TILE, LANE), rim[:, 1].reshape(12, TILE, LANE)]))
 
-    norms = (row(bias_first), row(gain_second))
-    near, partial, weight_next = call(
+    near, partial, weight, weight_next, bias, gain, bias_next = call(
         "middle_near",
         middle_near,
-        (mine, ta, on, on_prev, rim, weight, *norms, kernel_second),
-        (second, held(6 * CYC, CH, dtype=jnp.float32), weights),
+        (mine, ta, on, on_prev, rim),
+        (second, held(6 * CYC, CH, dtype=jnp.float32), weights, weights, vector, vector, vector),
+        far=(kernel_first, kernel_second, row(bias_first), row(gain_second), row(bias_second)),
         taps=(3, 8),
-        sems=True,
-    )
-    far = call("middle_far", middle_far, (cr, partial, weight, *norms), second, taps=(1, 8))
-
-    bias = row(bias_second)
+        sems=27,
+    )
+    far = call("middle_far", middle_far, (cr, partial, weight, bias, gain), second, taps=(1, 8))
     out_near, partial = call(
         "last_near",
         last_near,
-        (near, far, chip(near), feat, weight_next, bias),
+        (near, far, chip(near), feat, weight_next, bias_next),
         (held(4, CH, COLS), held(4 * CYC, CH, dtype=jnp.float32)),
         taps=(3, 6),
     )
     out = call(
         "last_far",
         last_far,
-        (cross(far), partial, out_near, feat, weight_next, bias),
+        (cross(far), partial, out_near, feat, weight_next, bias_next),
         jax.ShapeDtypeStruct(feat.shape, jnp.bfloat16),
         taps=(1, 6),
     )

time: 49.6 us -> 42.9 us (0.86)
  local copies, waits for them, and re-layouts: 7.26 us -> 0.03 us
  Pallas kernels: 12.5 us -> 13.9 us
  other arithmetic: 0.9 us -> 0.17 us
    unnamed x20 -> x0, local copies, waits for them, and re-layouts: 6.49 us -> none
    pallas_call x5, Pallas kernels: 12.5 us -> 13.9 us  [call(): pl.pallas_call(body, out_shape=outs, in_specs=[VMEM for _ in ins] + [HBM...]
    slice x1, local copies, waits for them, and re-layouts: 0.74 us -> 0.01 us  [local(): edges = jnp.concatenate([edge, on[SLABS:]])]
    concatenate x1, other arithmetic: 0.74 us -> 0.01 us  [local(): edges = jnp.concatenate([edge, on[SLABS:]])]
  transfers between devices with their start and end apart: 9 -> 9, of which waited for: 5 -> 5; matrix products, arithmetic and copies ran while one was open for 3% -> 0% of each run, Pallas kernels for 18% -> 22%
where the time goes in v2:
time: 42.9 us; the launch traced here: 42.7 us
  starting transfers between devices  19 us (44%)
  Pallas kernels  13.9 us (32%)
  waiting for transfers between devices  9.43 us (22%)
    ppermute x9, starting transfers between devices, send(): return lax.ppermute(array, axes, routes(sizes, move))  19 us
    pallas_call x5, Pallas kernels, call(): pl.pallas_call(body, out_shape=outs, in_specs=[VMEM for _ in ins] + [HBM...  13.9 us
    ppermute x9, waiting for transfers between devices, send(): return lax.ppermute(array, axes, routes(sizes, move))  9.43 us
  transfers between devices with their start and end apart: 9, of which 5 were waited for; matrix products, arithmetic and copies ran while one was open for 0% of the time, Pallas kernels for 22%

profile of v2, /device:TPU:107, one launch (start us, length us, event | category | flops | bytes accessed | tf_op | source)
XLA Modules:
  0.0 42.7 jit_solution(18058570342380501580)
XLA Ops:
  0.0 2.7 %first.1 = (bf16[2,6,104,128]{3,2,1,0:T(8,128)(2,1)S(1)}, bf16[90,8,128]{2,1,0:T(8,128)(2,1)S(1)}, bf16[78,8,128]{2,1,0:T(8,128)(2,1)S(1)}, bf16[12,8,128]{2,1,0...) custom-call(bf16[4,2,192,104]{3,2,1,0:T(8,128)(2,1)} %bitcast.15, f32[1,192]{1,0:T(1,128)} %bitcast.22), custom_call_target="tpu_custom_call" | custom-call | tf_op jit(solution)/shard_map/first/pallas_call | solution.py:235
  2.8 0.8 %collective-permute-start.1 = (bf16[90,8,128]{2,1,0:T(8,128)(2,1)S(1)}, bf16[90,8,128]{2,1,0:T(8,128)(2,1)S(1)}, u32[]{:S(2)}, u32[]{:S(2)}) collective-permute-start(bf16[90,8,128]{2,1,0:T(8,128)(2,1)S(1)} %get-tuple-element.22), channel_id=1, source_target_pairs={{0,4},{1,5},{2,6},{3,7},{4,0},{5,1},{6,2},{7,3},{8,12},{9,13},{10,... | collective-permute-start | bytes 552968 | tf_op jit(solution)/shard_map/ppermute | solution.py:260
  3.5 3.2 %collective-permute-start = (bf16[2,6,104,128]{3,2,1,0:T(8,128)(2,1)S(1)}, bf16[2,6,104,128]{3,2,1,0:T(8,128)(2,1)S(1)}, u32[]{:S(2)}, u32[]{:S(2)}) collective-permute-start(bf16[2,6,104,128]{3,2,1,0:T(8,128)(2,1)S(1)} %get-tuple-element.20.mine), channel_id=1, source_target_pairs={{0,64},{1,65},{2,66},{3,67},{4,68},{5,69},{6,70},{7,71},{8,72},{9,... | collective-permute-start | bytes 958472 | tf_op jit(solution)/shard_map/ppermute | solution.py:260
  6.7 0.0 collective-permute-done.1.on
  6.8 2.2 %collective-permute-start.2 = (bf16[24,8,128]{2,1,0:T(8,128)(2,1)S(1)}, bf16[24,8,128]{2,1,0:T(8,128)(2,1)S(1)}, u32[]{:S(2)}, u32[]{:S(2)}) collective-permute-start(bf16[24,8,128]{2,1,0:T(8,128)(2,1)S(1)} %pad_maximum_fusion.2), channel_id=1, source_target_pairs={{0,1},{1,2},{2,3},{5,4},{6,5},{7,6},{8,9},{9,10},{10,11},{13,12},{... | collective-permute-start | bytes 147464 | tf_op jit(solution)/shard_map/ppermute | solution.py:260
  8.9 2.0 %collective-permute-start.3 = (bf16[24,8,128]{2,1,0:T(8,128)(2,1)S(1)}, bf16[24,8,128]{2,1,0:T(8,128)(2,1)S(1)}, u32[]{:S(2)}, u32[]{:S(2)}) collective-permute-start(bf16[24,8,128]{2,1,0:T(8,128)(2,1)S(1)} %pad_maximum_fusion.2), channel_id=1, source_target_pairs={{0,65},{1,66},{2,67},{5,68},{6,69},{7,70},{8,73},{9,74},{10,75},{1... | collective-permute-start | bytes 147464 | tf_op jit(solution)/shard_map/ppermute | solution.py:260
  11.0 0.9 %collective-permute-done.2 = bf16[24,8,128]{2,1,0:T(8,128)(2,1)S(1)} collective-permute-done((bf16[24,8,128]{2,1,0:T(8,128)(2,1)S(1)}, bf16[24,8,128]{2,1,0:T(8,128)(2,1)S(1)}, u32[]{:S(2)}, u32[]{:S(2)}) %collective-permute-start.2) | collective-permute-done | bytes 49184 | tf_op jit(solution)/shard_map/ppermute | solution.py:260
  11.9 2.9 %collective-permute-done.3 = bf16[24,8,128]{2,1,0:T(8,128)(2,1)S(1)} collective-permute-done((bf16[24,8,128]{2,1,0:T(8,128)(2,1)S(1)}, bf16[24,8,128]{2,1,0:T(8,128)(2,1)S(1)}, u32[]{:S(2)}, u32[]{:S(2)}) %collective-permute-start.3) | collective-permute-done | bytes 49184 | tf_op jit(solution)/shard_map/ppermute | solution.py:260
  14.8 2.7 %collective-permute-start.4 = (bf16[2,2,12,8,128]{4,3,2,1,0:T(8,128)(2,1)S(1)}, bf16[2,2,12,8,128]{4,3,2,1,0:T(8,128)(2,1)S(1)}, u32[]{:S(2)}, u32[]{:S(2)}) collective-permute-start(bf16[2,2,12,8,128]{4,3,2,1,0:T(8,128)(2,1)S(1)} %pad_maximum_fusion.1), channel_id=1, source_target_pairs={{0,4},{1,5},{2,6},{3,7},{4,0},{5,1},{6,2},{7,3},{8,12},{9,13},{10,... | collective-permute-start | bytes 294920 | tf_op jit(solution)/shard_map/ppermute | solution.py:260
  17.5 0.0 collective-permute-done.ta
  17.5 0.9 %collective-permute-done.4 = bf16[2,2,12,8,128]{4,3,2,1,0:T(8,128)(2,1)S(1)} collective-permute-done((bf16[2,2,12,8,128]{4,3,2,1,0:T(8,128)(2,1)S(1)}, bf16[2,2,12,8,128]{4,3,2,1,0:T(8,128)(2,1)S(1)}, u32[]{:S(2)}, u32[]{:S(2)}) %collective-permute-start.4) | collective-permute-done | bytes 98336 | tf_op jit(solution)/shard_map/ppermute | solution.py:260
  18.4 0.1 reverse_select_fusion
  18.6 5.0 %collective-permute-start.5 = (bf16[168,8,128]{2,1,0:T(8,128)(2,1)S(1)}, bf16[168,8,128]{2,1,0:T(8,128)(2,1)S(1)}, u32[]{:S(2)}, u32[]{:S(2)}) collective-permute-start(bf16[168,8,128]{2,1,0:T(8,128)(2,1)S(1)} %pad_maximum_fusion), channel_id=1, source_target_pairs={{4,8},{5,9},{6,10},{7,11},{8,4},{9,5},{10,6},{11,7},{12,16},{13,17... | collective-permute-start | bytes 1032200 | tf_op jit(solution)/shard_map/ppermute | solution.py:260
  23.6 0.1 collective-permute-start.6
  23.7 1.4 %collective-permute-done.6.on_prev = bf16[78,8,128]{2,1,0:T(8,128)(2,1)S(1)} collective-permute-done((bf16[78,8,128]{2,1,0:T(8,128)(2,1)S(1)}, bf16[78,8,128]{2,1,0:T(8,128)(2,1)S(1)}, u32[]{:S(2)}, u32[]{:S(2)}) %collective-permute-start.6) | collective-permute-done | bytes 159776 | tf_op jit(solution)/shard_map/ppermute | solution.py:260
  25.1 5.5 %middle_near.1 = (bf16[9,112,128]{2,1,0:T(8,128)(2,1)S(1)}, f32[672,192]{1,0:T(8,128)S(1)}, bf16[3,14,128,192]{3,2,1,0:T(8,128)(2,1)S(1)}, bf16[3,14,128,192]{3,...) custom-call(bf16[2,6,104,128]{3,2,1,0:T(8,128)(2,1)S(1)} %get-tuple-element.20.mine, ...), custom_call_target="tpu_custom_call" | custom-call | tf_op jit(solution)/shard_map/middle_near/pallas_call | solution.py:235
  30.5 0.2 collective-permute-start.8
  30.8 0.0 collective-permute-done.5.cr
  30.8 1.4 %middle_far.1.mine_cr = bf16[9,112,128]{2,1,0:T(8,128)(2,1)S(1)} custom-call(bf16[168,8,128]{2,1,0:T(8,128)(2,1)S(1)} %collective-permute-done.5.cr, f32[672,192]{1,0:T(8,128)S(1)} %get-tuple-element.23.partial, bf16[3,14,128,192]{3,2,1,0:T(8,128)(2,1)S(1)} %get-tuple-element.24.weight, f32[1,192]{1,0:T(1,128)S(1)} %get-tuple-element.25.bias, ...), custom_call_target="tpu_custom_call" | custom-call | tf_op jit(solution)/shard_map/middle_far/pallas_call | solution.py:235
  32.1 2.9 %collective-permute-start.7 = (bf16[9,112,128]{2,1,0:T(8,128)(2,1)S(1)}, bf16[9,112,128]{2,1,0:T(8,128)(2,1)S(1)}, u32[]{:S(2)}, u32[]{:S(2)}) collective-permute-start(bf16[9,112,128]{2,1,0:T(8,128)(2,1)S(1)} %middle_far.1.mine_cr), channel_id=1, source_target_pairs={{4,8},{5,9},{6,10},{7,11},{8,4},{9,5},{10,6},{11,7},{12,16},{13,17... | collective-permute-start | bytes 774152 | tf_op jit(solution)/shard_map/ppermute | solution.py:260
  35.0 0.0 collective-permute-done.8.on
  35.0 2.6 %last_near.1 = (bf16[4,192,104]{2,1,0:T(8,128)(2,1)S(1)}, f32[448,192]{1,0:T(8,128)S(1)}) custom-call(bf16[9,112,128]{2,1,0:T(8,128)(2,1)S(1)} %get-tuple-element.27.mine_on, bf16[9,112,128]{2,1,0:T(8,128)(2,1)S(1)} %middle_far.1.mine_cr, bf16[9,112,128]{2,1,0:T(8,128)(2,1)S(1)} %collective-permute-done.8.on, ...), custom_call_target="tpu_custom_call" | custom-call | tf_op jit(solution)/shard_map/last_near/pallas_call | solution.py:235
  37.6 3.3 %collective-permute-done.7.cr = bf16[9,112,128]{2,1,0:T(8,128)(2,1)S(1)} collective-permute-done((bf16[9,112,128]{2,1,0:T(8,128)(2,1)S(1)}, bf16[9,112,128]{2,1,0:T(8,128)(2,1)S(1)}, u32[]{:S(2)}, u32[]{:S(2)}) %collective-permute-start.7) | collective-permute-done | bytes 258080 | tf_op jit(solution)/shard_map/ppermute | solution.py:260
  41.0 1.7 %last_far.1 = bf16[4,2,192,104]{3,2,1,0:T(8,128)(2,1)} custom-call(bf16[9,112,128]{2,1,0:T(8,128)(2,1)S(1)} %collective-permute-done.7.cr, f32[448,192]{1,0:T(8,128)S(1)} %get-tuple-element.31.partial, bf16[4,192,104]{2,1,0:T(8,128)(2,1)S(1)} %get-tuple-element.32.near, bf16[4,2,192,104]{3,2,1,0:T(8,128)(2,1)S(1)} %get-tuple-element.28.feat, ...), custom_call_target="tpu_custom_call" | custom-call | tf_op jit(solution)/shard_map/last_far/pallas_call | solution.py:235
  (7 shorter events, 0.1 us)
Async XLA Ops:
  2.8 4.0 %collective-permute-start.1 = (bf16[90,8,128]{2,1,0:T(8,128)(2,1)S(1)}, bf16[90,8,128]{2,1,0:T(8,128)(2,1)S(1)}, u32[]{:S(2)}, u32[]{:S(2)}) collective-permute-start(bf16[90,8,128]{2,1,0:T(8,128)(2,1)S(1)} %get-tuple-element.22), channel_id=1, source_target_pairs={{0,4},{1,5},{2,6},{3,7},{4,0},{5,1},{6,2},{7,3},{8,12},{9,13},{10,... | collective-permute-start | bytes 552968 | tf_op jit(solution)/shard_map/ppermute | solution.py:260
  3.5 13.9 %collective-permute-start = (bf16[2,6,104,128]{3,2,1,0:T(8,128)(2,1)S(1)}, bf16[2,6,104,128]{3,2,1,0:T(8,128)(2,1)S(1)}, u32[]{:S(2)}, u32[]{:S(2)}) collective-permute-start(bf16[2,6,104,128]{3,2,1,0:T(8,128)(2,1)S(1)} %get-tuple-element.20.mine), channel_id=1, source_target_pairs={{0,64},{1,65},{2,66},{3,67},{4,68},{5,69},{6,70},{7,71},{8,72},{9,... | collective-permute-start | bytes 958472 | tf_op jit(solution)/shard_map/ppermute | solution.py:260
  6.8 5.1 %collective-permute-start.2 = (bf16[24,8,128]{2,1,0:T(8,128)(2,1)S(1)}, bf16[24,8,128]{2,1,0:T(8,128)(2,1)S(1)}, u32[]{:S(2)}, u32[]{:S(2)}) collective-permute-start(bf16[24,8,128]{2,1,0:T(8,128)(2,1)S(1)} %pad_maximum_fusion.2), channel_id=1, source_target_pairs={{0,1},{1,2},{2,3},{5,4},{6,5},{7,6},{8,9},{9,10},{10,11},{13,12},{... | collective-permute-start | bytes 147464 | tf_op jit(solution)/shard_map/ppermute | solution.py:260
  8.9 5.8 %collective-permute-start.3 = (bf16[24,8,128]{2,1,0:T(8,128)(2,1)S(1)}, bf16[24,8,128]{2,1,0:T(8,128)(2,1)S(1)}, u32[]{:S(2)}, u32[]{:S(2)}) collective-permute-start(bf16[24,8,128]{2,1,0:T(8,128)(2,1)S(1)} %pad_maximum_fusion.2), channel_id=1, source_target_pairs={{0,65},{1,66},{2,67},{5,68},{6,69},{7,70},{8,73},{9,74},{10,75},{1... | collective-permute-start | bytes 147464 | tf_op jit(solution)/shard_map/ppermute | solution.py:260
  14.8 3.6 %collective-permute-start.4 = (bf16[2,2,12,8,128]{4,3,2,1,0:T(8,128)(2,1)S(1)}, bf16[2,2,12,8,128]{4,3,2,1,0:T(8,128)(2,1)S(1)}, u32[]{:S(2)}, u32[]{:S(2)}) collective-permute-start(bf16[2,2,12,8,128]{4,3,2,1,0:T(8,128)(2,1)S(1)} %pad_maximum_fusion.1), channel_id=1, source_target_pairs={{0,4},{1,5},{2,6},{3,7},{4,0},{5,1},{6,2},{7,3},{8,12},{9,13},{10,... | collective-permute-start | bytes 294920 | tf_op jit(solution)/shard_map/ppermute | solution.py:260
  18.6 12.2 %collective-permute-start.5 = (bf16[168,8,128]{2,1,0:T(8,128)(2,1)S(1)}, bf16[168,8,128]{2,1,0:T(8,128)(2,1)S(1)}, u32[]{:S(2)}, u32[]{:S(2)}) collective-permute-start(bf16[168,8,128]{2,1,0:T(8,128)(2,1)S(1)} %pad_maximum_fusion), channel_id=1, source_target_pairs={{4,8},{5,9},{6,10},{7,11},{8,4},{9,5},{10,6},{11,7},{12,16},{13,17... | collective-permute-start | bytes 1032200 | tf_op jit(solution)/shard_map/ppermute | solution.py:260
  23.6 1.5 %collective-permute-start.6 = (bf16[78,8,128]{2,1,0:T(8,128)(2,1)S(1)}, bf16[78,8,128]{2,1,0:T(8,128)(2,1)S(1)}, u32[]{:S(2)}, u32[]{:S(2)}) collective-permute-start(bf16[78,8,128]{2,1,0:T(8,128)(2,1)S(1)} %bitcast.20), channel_id=1, source_target_pairs={{0,4},{1,5},{2,6},{3,7},{4,0},{5,1},{6,2},{7,3},{8,12},{9,13},{10,... | collective-permute-start | bytes 479240 | tf_op jit(solution)/shard_map/ppermute | solution.py:260
  30.5 4.5 %collective-permute-start.8 = (bf16[9,112,128]{2,1,0:T(8,128)(2,1)S(1)}, bf16[9,112,128]{2,1,0:T(8,128)(2,1)S(1)}, u32[]{:S(2)}, u32[]{:S(2)}) collective-permute-start(bf16[9,112,128]{2,1,0:T(8,128)(2,1)S(1)} %get-tuple-element.27.mine_on), channel_id=1, source_target_pairs={{0,4},{1,5},{2,6},{3,7},{4,0},{5,1},{6,2},{7,3},{8,12},{9,13},{10,... | collective-permute-start | bytes 774152 | tf_op jit(solution)/shard_map/ppermute | solution.py:260
  32.1 8.9 %collective-permute-start.7 = (bf16[9,112,128]{2,1,0:T(8,128)(2,1)S(1)}, bf16[9,112,128]{2,1,0:T(8,128)(2,1)S(1)}, u32[]{:S(2)}, u32[]{:S(2)}) collective-permute-start(bf16[9,112,128]{2,1,0:T(8,128)(2,1)S(1)} %middle_far.1.mine_cr), channel_id=1, source_target_pairs={{4,8},{5,9},{6,10},{7,11},{8,4},{9,5},{10,6},{11,7},{12,16},{13,17... | collective-permute-start | bytes 774152 | tf_op jit(solution)/shard_map/ppermute | solution.py:260

commit v3 on v2

--- a/solution.py
+++ b/solution.py
@@ -55,22 +55,33 @@
     return copies
 
 
+def load_kernel(after, kernel, kernel_next, *refs):
+    vectors, outs, sems = refs[:3], refs[3:-1], refs[-1]
+    copies = fetch(zip(vectors, outs[2:]), sems)
+    for n, source in enumerate((kernel, kernel_next)):
+        copies += fetch(weight_parts(source, outs[n], core_index()), sems, len(copies))
+        outs[n][:, 13, HI:, :] = jnp.zeros((3, HI, CH), jnp.bfloat16)
+    for c in copies:
+        c.wait()
+
+
 def first_kernel(feat_in, gain_in, mine, on, cr, edge, feat, gain, sems):
     core = core_index()
     frames = feat.shape[0]
     order = [(row_of(slot, core), f) for slot in range(ROWS) for f in range(frames)]
     copies = fetch([(gain_in, gain)] + [(feat_in.at[f, row], feat.at[f, row]) for row, f in order], sems)
-    copies[0].wait()
+    for c in copies:
+        c.wait()
+    gains = jnp.broadcast_to(gain[...], (LANE, CH)).T[:, :COLS]
     for slot in range(ROWS):
         row = row_of(slot, core)
         for f in range(0, frames, 2):
             pair = []
             for e in range(2):
-                copies[1 + slot * frames + f + e].wait()
                 field = feat[f + e, row].astype(jnp.float32)
                 meansq = jnp.mean(field * field, axis=0, keepdims=True)
-                normed = (field * lax.rsqrt(meansq + epsilon)).T
-                pair.append(silu(normed * gain[...]).astype(jnp.bfloat16))
+                first = silu(field * lax.rsqrt(meansq + epsilon) * gains)
+                pair.append(first.astype(jnp.bfloat16).T)
             for k, slab in enumerate(pack(*pair)):
                 n = 3 * (f // 2) + k
                 mine[slot, n] = slab
@@ -106,22 +117,23 @@
     return jnp.dot(cells, weight.reshape(-1, CH), preferred_element_type=jnp.float32)
 
 
+def taps_term(taps, weight, f, count, part, p):
+    span = slice(f + p, f + p + count)
+    if part == "all":
+        cells = [taps[0, span, :, :512], taps[1, span, :, :512], taps[0, span, :, 512:], taps[2, span]]
+        k = weight[p]
+    elif part == "near":
+        cells = [taps[1, span, :, :512], taps[2, span, :, :512], taps[1, span, :, 512:]]
+        k = weight[p, :9]
+    else:
+        cells = [taps[0, span]]
+        k = weight[p, 9:]
+    return matmul(jnp.concatenate(cells, axis=-1), k)
+
+
 def taps_total(taps, weight, f, count, part):
-    total = None
-    for p in range(3):
-        span = slice(f + p, f + p + count)
-        if part == "all":
-            cells = [taps[0, span, :, :512], taps[1, span, :, :512], taps[0, span, :, 512:], taps[2, span]]
-            k = weight[p]
-        elif part == "near":
-            cells = [taps[1, span, :, :512], taps[2, span, :, :512], taps[1, span, :, 512:]]
-            k = weight[p, :9]
-        else:
-            cells = [taps[0, span]]
-            k = weight[p, 9:]
-        term = matmul(jnp.concatenate(cells, axis=-1), k)
-        total = term if total is None else total + term
-    return total
+    first, *others = [taps_term(taps, weight, f, count, part, p) for p in range(3)]
+    return sum(others, first)
 
 
 def put_second(out, total, f, bias, gain):
@@ -142,16 +154,7 @@
     return jnp.concatenate([ref[n * TILES : (n + 1) * TILES].reshape(COLS, LANE), tip], axis=0)
 
 
-def middle_near(
-    mine, ta, on, on_prev, rim, kernel, kernel_next, bias_in, gain_in, bias_next_in,
-    out, partial, weight, weight_next, bias, gain, bias_next, taps, sems,
-):
-    core = core_index()
-    vectors = [(bias_in, bias), (gain_in, gain), (bias_next_in, bias_next)]
-    copies = fetch(weight_parts(kernel, weight, core) + vectors, sems)
-    copies_next = fetch(weight_parts(kernel_next, weight_next, core), sems, len(copies))
-    for ref in (weight, weight_next):
-        ref[:, 13, HI:, :] = jnp.zeros((3, HI, CH), jnp.bfloat16)
+def middle_near(mine, ta, on, on_prev, rim, weight, bias, gain, out, partial, taps):
     for half in range(2):
         for pair in range(2):
             for row in range(3):
@@ -163,14 +166,10 @@
                         body = (mine if half else ta)[row - 1, n]
                         slabs.append(jnp.concatenate([body, rim[1 - half, row - 1, n]], axis=0))
                 put_row(taps, row, 4 * half + 2 * pair, slabs[:2], slabs[2])
-    for c in copies:
-        c.wait()
     for f in range(0, 6, 2):
         put_second(out, taps_total(taps, weight, f, 2, "all"), f, bias, gain)
     for f in range(0, 6, 2):
         partial[f * CYC : (f + 2) * CYC] = taps_total(taps, weight, f, 2, "near")
-    for c in copies_next:
-        c.wait()
 
 
 def middle_far(cr, partial, weight, bias, gain, out, taps):
@@ -208,35 +207,38 @@
         partial[f * CYC : (f + 2) * CYC] = taps_total(taps, weight, f, 2, "near")
 
 
-def last_far(cr, partial, near, feat, weight, bias, out, taps):
-    core = core_index()
+def last_far(cr, partial, near, feat, weight, bias, out, taps, far, sems):
+    row, near_row = row_of(1, core_index()), row_of(0, core_index())
+    frames = feat.shape[0]
+    copies = fetch([(near.at[f], out.at[f, near_row]) for f in range(frames)], sems)
     for f in range(0, 6, 2):
         n = 3 * (f // 2)
         put_row(taps, 0, f, [cr[n], cr[n + 1]], cr[n + 2])
-    for f in range(out.shape[0]):
-        out[f, row_of(0, core)] = near[f]
 
     def store(f, cells):
-        out[f, row_of(1, core)] = cells
+        far[f] = cells
+        copies.extend(fetch([(far.at[f], out.at[f, row])], sems, frames + f))
 
     for f in range(0, 4, 2):
         total = partial[f * CYC : (f + 2) * CYC] + taps_total(taps, weight, f, 2, "far")
-        put_last(store, total, feat, f, row_of(1, core), bias)
+        put_last(store, total, feat, f, row, bias)
+    for c in copies:
+        c.wait()
 
 
 def held(*dims, dtype=jnp.bfloat16):
     return pltpu.VMEM(dims, dtype)
 
 
-def call(name, body, ins, outs, far=(), taps=None, sems=0):
-    scratch = [] if taps is None else [held(*taps, CYC, 640)]
+def call(name, body, ins, outs, far=(), taps=None, scratch=(), sems=0, out_spec=VMEM):
+    scratch = ([] if taps is None else [held(*taps, CYC, 640)]) + list(scratch)
     if sems:
         scratch.append(pltpu.SemaphoreType.DMA((sems,)))
     return pl.pallas_call(
         body,
         out_shape=outs,
         in_specs=[VMEM for _ in ins] + [HBM for _ in far],
-        out_specs=jax.tree.map(lambda _: VMEM, outs),
+        out_specs=jax.tree.map(lambda _: out_spec, outs),
         scratch_shapes=scratch,
         compiler_params=params,
         name=name,
@@ -284,21 +286,31 @@
     ta = send(mine, lambda t, y, x: (t + 1, y, x))
     side = send(edges, lambda t, y, x: (t, y, x - 1 if y % 2 else x + 1))
     side_prev = send(edges, lambda t, y, x: (t + 1, y, x - 1 if y % 2 else x + 1))
+    held_args = call(
+        "load",
+        load_kernel,
+        (edges,),
+        (weights, weights, vector, vector, vector),
+        far=(kernel_first, kernel_second, row(bias_first), row(gain_second), row(bias_second)),
+        sems=27,
+    )
+    side, side_prev, *held_args = lax.optimization_barrier((side, side_prev, *held_args))
+    weight, weight_next, bias, gain, bias_next = held_args
     sides = jnp.stack([side, side_prev]).reshape(2, 2, 12, TILE, LANE)
     others = chip(sides)[:, ::-1]
     upper = lax.broadcasted_iota(jnp.int32, sides.shape, 3) < TILE // 2
     rim = jnp.where(upper == (core_index() == 0), others, sides).reshape(2, 4, 6, TILE, LANE)
     on_prev = chip(ta[0].reshape(SLABS, TILE, LANE))
-    cr = cross(jnp.concatenate([cr_row, ta[1].reshape(SLABS, TILE, LANE), rim[:, 1].reshape(12, TILE, LANE)]))
-
-    near, partial, weight, weight_next, bias, gain, bias_next = call(
+    message = jnp.concatenate([cr_row, ta[1].reshape(SLABS, TILE, LANE), rim[:, 1].reshape(12, TILE, LANE)])
+    message, on_prev = lax.optimization_barrier((message, on_prev))
+    cr = cross(message)
+
+    near, partial = call(
         "middle_near",
         middle_near,
-        (mine, ta, on, on_prev, rim),
-        (second, held(6 * CYC, CH, dtype=jnp.float32), weights, weights, vector, vector, vector),
-        far=(kernel_first, kernel_second, row(bias_first), row(gain_second), row(bias_second)),
+        (mine, ta, on, on_prev, rim, weight, bias, gain),
+        (second, held(6 * CYC, CH, dtype=jnp.float32)),
         taps=(3, 8),
-        sems=27,
     )
     far = call("middle_far", middle_far, (cr, partial, weight, bias, gain), second, taps=(1, 8))
     out_near, partial = call(
@@ -314,6 +326,9 @@
         (cross(far), partial, out_near, feat, weight_next, bias_next),
         jax.ShapeDtypeStruct(feat.shape, jnp.bfloat16),
         taps=(1, 6),
+        scratch=[held(4, CH, COLS)],
+        sems=8,
+        out_spec=HBM,
     )
     return jnp.swapaxes(out, 2, 3)
 

time: 42.9 us -> 40 us (0.932); the launches traced: 42.7 us -> 39.2 us
  waiting for transfers between devices: 9.43 us -> 4.17 us
  starting transfers between devices: 19 us -> 21 us
    ppermute x9, waiting for transfers between devices: 9.43 us -> 4.17 us  [send(): return lax.ppermute(array, axes, routes(sizes, move))]
    ppermute x9, starting transfers between devices: 19 us -> 21 us  [send(): return lax.ppermute(array, axes, routes(sizes, move))]
    pallas_call x5 -> x6, Pallas kernels: 13.9 us -> 13.7 us  [call(): pl.pallas_call(body, out_shape=outs, in_specs=[VMEM for _ in ins] + [HBM...]
  transfers between devices with their start and end apart: 9 -> 9, of which waited for: 5 -> 5; matrix products, arithmetic and copies ran while one was open for 0% -> 1% of each run, Pallas kernels for 22% -> 27%
where the time goes in v3:
time: 40 us; the launch traced here: 39.2 us
  starting transfers between devices  21 us (52%)
  Pallas kernels  13.7 us (34%)
  waiting for transfers between devices  4.17 us (10%)
    ppermute x9, starting transfers between devices, send(): return lax.ppermute(array, axes, routes(sizes, move))  21 us
    pallas_call x6, Pallas kernels, call(): pl.pallas_call(body, out_shape=outs, in_specs=[VMEM for _ in ins] + [HBM...  13.7 us
    ppermute x9, waiting for transfers between devices, send(): return lax.ppermute(array, axes, routes(sizes, move))  4.17 us
  transfers between devices with their start and end apart: 9, of which 5 were waited for; matrix products, arithmetic and copies ran while one was open for 1% of the time, Pallas kernels for 27%

profile of v3, /device:TPU:107, one launch (start us, length us, event | category | flops | bytes accessed | tf_op | source)
XLA Modules:
  0.0 39.2 jit_solution(4448098546270641144)
XLA Ops:
  0.0 1.6 %first.1 = (bf16[2,6,104,128]{3,2,1,0:T(8,128)(2,1)S(1)}, bf16[90,8,128]{2,1,0:T(8,128)(2,1)S(1)}, bf16[78,8,128]{2,1,0:T(8,128)(2,1)S(1)}, bf16[12,8,128]{2,1,0...) custom-call(bf16[4,2,192,104]{3,2,1,0:T(8,128)(2,1)} %bitcast.15, f32[1,192]{1,0:T(1,128)} %bitcast.22), custom_call_target="tpu_custom_call" | custom-call | tf_op jit(solution)/shard_map/first/pallas_call | solution.py:237
  1.6 0.8 %collective-permute-start.1 = (bf16[90,8,128]{2,1,0:T(8,128)(2,1)S(1)}, bf16[90,8,128]{2,1,0:T(8,128)(2,1)S(1)}, u32[]{:S(2)}, u32[]{:S(2)}) collective-permute-start(bf16[90,8,128]{2,1,0:T(8,128)(2,1)S(1)} %get-tuple-element.31), channel_id=1, source_target_pairs={{0,4},{1,5},{2,6},{3,7},{4,0},{5,1},{6,2},{7,3},{8,12},{9,13},{10,... | collective-permute-start | bytes 552968 | tf_op jit(solution)/shard_map/ppermute | solution.py:262
  2.4 3.2 %collective-permute-start = (bf16[2,6,104,128]{3,2,1,0:T(8,128)(2,1)S(1)}, bf16[2,6,104,128]{3,2,1,0:T(8,128)(2,1)S(1)}, u32[]{:S(2)}, u32[]{:S(2)}) collective-permute-start(bf16[2,6,104,128]{3,2,1,0:T(8,128)(2,1)S(1)} %get-tuple-element.29.mine), channel_id=1, source_target_pairs={{0,64},{1,65},{2,66},{3,67},{4,68},{5,69},{6,70},{7,71},{8,72},{9,... | collective-permute-start | bytes 958472 | tf_op jit(solution)/shard_map/ppermute | solution.py:262
  5.6 0.0 collective-permute-done.1.on
  5.6 2.9 %collective-permute-start.3 = (bf16[24,8,128]{2,1,0:T(8,128)(2,1)S(1)}, bf16[24,8,128]{2,1,0:T(8,128)(2,1)S(1)}, u32[]{:S(2)}, u32[]{:S(2)}) collective-permute-start(bf16[24,8,128]{2,1,0:T(8,128)(2,1)S(1)} %pad_maximum_fusion.2.after), channel_id=1, source_target_pairs={{0,65},{1,66},{2,67},{5,68},{6,69},{7,70},{8,73},{9,74},{10,75},{1... | collective-permute-start | bytes 147464 | tf_op jit(solution)/shard_map/ppermute | solution.py:262
  8.5 1.9 %collective-permute-start.2 = (bf16[24,8,128]{2,1,0:T(8,128)(2,1)S(1)}, bf16[24,8,128]{2,1,0:T(8,128)(2,1)S(1)}, u32[]{:S(2)}, u32[]{:S(2)}) collective-permute-start(bf16[24,8,128]{2,1,0:T(8,128)(2,1)S(1)} %pad_maximum_fusion.2.after), channel_id=1, source_target_pairs={{0,1},{1,2},{2,3},{5,4},{6,5},{7,6},{8,9},{9,10},{10,11},{13,12},{... | collective-permute-start | bytes 147464 | tf_op jit(solution)/shard_map/ppermute | solution.py:262
  10.5 2.8 %load.1 = (bf16[3,14,128,192]{3,2,1,0:T(8,128)(2,1)S(1)}, bf16[3,14,128,192]{3,2,1,0:T(8,128)(2,1)S(1)}, f32[1,192]{1,0:T(1,128)S(1)}, f32[1,192]{1,0:T(1,128)S(1)}, f32[1,192]{1,0:T(1,128)S(1)}) custom-call(bf16[24,8,128]{2,1,0:T(8,128)(2,1)S(1)} %pad_maximum_fusion.2.after, bf16[3,3,3,192,192]{4,3,2,1,0:T(8,128)(2,1)} %kernel.1, ...), custom_call_target="tpu_custom_call" | custom-call | tf_op jit(solution)/shard_map/load/pallas_call | solution.py:237
  13.2 0.0 collective-permute-done.3
  13.2 0.4 %collective-permute-done.2 = bf16[24,8,128]{2,1,0:T(8,128)(2,1)S(1)} collective-permute-done((bf16[24,8,128]{2,1,0:T(8,128)(2,1)S(1)}, bf16[24,8,128]{2,1,0:T(8,128)(2,1)S(1)}, u32[]{:S(2)}, u32[]{:S(2)}) %collective-permute-start.2) | collective-permute-done | bytes 49184 | tf_op jit(solution)/shard_map/ppermute | solution.py:262
  13.7 2.5 %collective-permute-start.4 = (bf16[2,2,12,8,128]{4,3,2,1,0:T(8,128)(2,1)S(1)}, bf16[2,2,12,8,128]{4,3,2,1,0:T(8,128)(2,1)S(1)}, u32[]{:S(2)}, u32[]{:S(2)}) collective-permute-start(bf16[2,2,12,8,128]{4,3,2,1,0:T(8,128)(2,1)S(1)} %pad_maximum_fusion.1), channel_id=1, source_target_pairs={{0,4},{1,5},{2,6},{3,7},{4,0},{5,1},{6,2},{7,3},{8,12},{9,13},{10,... | collective-permute-start | bytes 294920 | tf_op jit(solution)/shard_map/ppermute | solution.py:262
  16.1 0.0 collective-permute-done.ta
  16.2 0.1 collective-permute-start.5
  16.3 0.8 %collective-permute-done.4 = bf16[2,2,12,8,128]{4,3,2,1,0:T(8,128)(2,1)S(1)} collective-permute-done((bf16[2,2,12,8,128]{4,3,2,1,0:T(8,128)(2,1)S(1)}, bf16[2,2,12,8,128]{4,3,2,1,0:T(8,128)(2,1)S(1)}, u32[]{:S(2)}, u32[]{:S(2)}) %collective-permute-start.4) | collective-permute-done | bytes 98336 | tf_op jit(solution)/shard_map/ppermute | solution.py:262
  17.1 0.1 reverse_select_fusion
  17.3 0.4 %collective-permute-done.5.on_prev = bf16[78,8,128]{2,1,0:T(8,128)(2,1)S(1)} collective-permute-done((bf16[78,8,128]{2,1,0:T(8,128)(2,1)S(1)}, bf16[78,8,128]{2,1,0:T(8,128)(2,1)S(1)}, u32[]{:S(2)}, u32[]{:S(2)}) %collective-permute-start.5) | collective-permute-done | bytes 159776 | tf_op jit(solution)/shard_map/ppermute | solution.py:262
  17.7 4.8 %collective-permute-start.6 = (bf16[168,8,128]{2,1,0:T(8,128)(2,1)S(1)}, bf16[168,8,128]{2,1,0:T(8,128)(2,1)S(1)}, u32[]{:S(2)}, u32[]{:S(2)}) collective-permute-start(bf16[168,8,128]{2,1,0:T(8,128)(2,1)S(1)} %pad_maximum_fusion), channel_id=1, source_target_pairs={{4,8},{5,9},{6,10},{7,11},{8,4},{9,5},{10,6},{11,7},{12,16},{13,17... | collective-permute-start | bytes 1032200 | tf_op jit(solution)/shard_map/ppermute | solution.py:262
  22.4 3.8 %middle_near.1 = (bf16[9,112,128]{2,1,0:T(8,128)(2,1)S(1)}, f32[672,192]{1,0:T(8,128)S(1)}) custom-call(bf16[2,6,104,128]{3,2,1,0:T(8,128)(2,1)S(1)} %get-tuple-element.29.mine, bf16[2,6,104,128]{3,2,1,0:T(8,128)(2,1)S(1)} %collective-permute-done.ta, bf16[90,8,128]{2,1,0:T(8,128)(2,1)S(1)} %collective-permute-done.1.on, ...), custom_call_target="tpu_custom_call" | custom-call | tf_op jit(solution)/shard_map/middle_near/pallas_call | solution.py:237
  26.2 0.1 collective-permute-start.8
  26.3 1.1 %collective-permute-done.6.cr = bf16[168,8,128]{2,1,0:T(8,128)(2,1)S(1)} collective-permute-done((bf16[168,8,128]{2,1,0:T(8,128)(2,1)S(1)}, bf16[168,8,128]{2,1,0:T(8,128)(2,1)S(1)}, u32[]{:S(2)}, u32[]{:S(2)}) %collective-permute-start.6) | collective-permute-done | bytes 344096 | tf_op jit(solution)/shard_map/ppermute | solution.py:262
  27.4 1.3 %middle_far.1.mine_cr = bf16[9,112,128]{2,1,0:T(8,128)(2,1)S(1)} custom-call(bf16[168,8,128]{2,1,0:T(8,128)(2,1)S(1)} %collective-permute-done.6.cr, f32[672,192]{1,0:T(8,128)S(1)} %get-tuple-element.44.partial, bf16[3,14,128,192]{3,2,1,0:T(8,128)(2,1)S(1)} %get-tuple-element.41.weight, f32[1,192]{1,0:T(1,128)S(1)} %get-tuple-element.42.bias, ...), custom_call_target="tpu_custom_call" | custom-call | tf_op jit(solution)/shard_map/middle_far/pallas_call | solution.py:237
  28.8 4.8 %collective-permute-start.7 = (bf16[9,112,128]{2,1,0:T(8,128)(2,1)S(1)}, bf16[9,112,128]{2,1,0:T(8,128)(2,1)S(1)}, u32[]{:S(2)}, u32[]{:S(2)}) collective-permute-start(bf16[9,112,128]{2,1,0:T(8,128)(2,1)S(1)} %middle_far.1.mine_cr), channel_id=1, source_target_pairs={{4,8},{5,9},{6,10},{7,11},{8,4},{9,5},{10,6},{11,7},{12,16},{13,17... | collective-permute-start | bytes 774152 | tf_op jit(solution)/shard_map/ppermute | solution.py:262
  33.5 0.0 collective-permute-done.8.on
  33.6 2.6 %last_near.1 = (bf16[4,192,104]{2,1,0:T(8,128)(2,1)S(1)}, f32[448,192]{1,0:T(8,128)S(1)}) custom-call(bf16[9,112,128]{2,1,0:T(8,128)(2,1)S(1)} %get-tuple-element.45.mine_on, bf16[9,112,128]{2,1,0:T(8,128)(2,1)S(1)} %middle_far.1.mine_cr, bf16[9,112,128]{2,1,0:T(8,128)(2,1)S(1)} %collective-permute-done.8.on, ...), custom_call_target="tpu_custom_call" | custom-call | tf_op jit(solution)/shard_map/last_near/pallas_call | solution.py:237
  36.2 1.4 %collective-permute-done.7.cr = bf16[9,112,128]{2,1,0:T(8,128)(2,1)S(1)} collective-permute-done((bf16[9,112,128]{2,1,0:T(8,128)(2,1)S(1)}, bf16[9,112,128]{2,1,0:T(8,128)(2,1)S(1)}, u32[]{:S(2)}, u32[]{:S(2)}) %collective-permute-start.7) | collective-permute-done | bytes 258080 | tf_op jit(solution)/shard_map/ppermute | solution.py:262
  37.6 1.6 %last_far.1 = bf16[4,2,192,104]{3,2,1,0:T(8,128)(2,1)} custom-call(bf16[9,112,128]{2,1,0:T(8,128)(2,1)S(1)} %collective-permute-done.7.cr, f32[448,192]{1,0:T(8,128)S(1)} %get-tuple-element.49.partial, bf16[4,192,104]{2,1,0:T(8,128)(2,1)S(1)} %get-tuple-element.50.near, bf16[4,2,192,104]{3,2,1,0:T(8,128)(2,1)S(1)} %get-tuple-element.46.feat, ...), custom_call_target="tpu_custom_call" | custom-call | tf_op jit(solution)/shard_map/last_far/pallas_call | solution.py:237
  (7 shorter events, 0.1 us)
Async XLA Ops:
  1.6 4.0 %collective-permute-start.1 = (bf16[90,8,128]{2,1,0:T(8,128)(2,1)S(1)}, bf16[90,8,128]{2,1,0:T(8,128)(2,1)S(1)}, u32[]{:S(2)}, u32[]{:S(2)}) collective-permute-start(bf16[90,8,128]{2,1,0:T(8,128)(2,1)S(1)} %get-tuple-element.31), channel_id=1, source_target_pairs={{0,4},{1,5},{2,6},{3,7},{4,0},{5,1},{6,2},{7,3},{8,12},{9,13},{10,... | collective-permute-start | bytes 552968 | tf_op jit(solution)/shard_map/ppermute | solution.py:262
  2.4 13.8 %collective-permute-start = (bf16[2,6,104,128]{3,2,1,0:T(8,128)(2,1)S(1)}, bf16[2,6,104,128]{3,2,1,0:T(8,128)(2,1)S(1)}, u32[]{:S(2)}, u32[]{:S(2)}) collective-permute-start(bf16[2,6,104,128]{3,2,1,0:T(8,128)(2,1)S(1)} %get-tuple-element.29.mine), channel_id=1, source_target_pairs={{0,64},{1,65},{2,66},{3,67},{4,68},{5,69},{6,70},{7,71},{8,72},{9,... | collective-permute-start | bytes 958472 | tf_op jit(solution)/shard_map/ppermute | solution.py:262
  5.6 7.6 %collective-permute-start.3 = (bf16[24,8,128]{2,1,0:T(8,128)(2,1)S(1)}, bf16[24,8,128]{2,1,0:T(8,128)(2,1)S(1)}, u32[]{:S(2)}, u32[]{:S(2)}) collective-permute-start(bf16[24,8,128]{2,1,0:T(8,128)(2,1)S(1)} %pad_maximum_fusion.2.after), channel_id=1, source_target_pairs={{0,65},{1,66},{2,67},{5,68},{6,69},{7,70},{8,73},{9,74},{10,75},{1... | collective-permute-start | bytes 147464 | tf_op jit(solution)/shard_map/ppermute | solution.py:262
  8.5 5.1 %collective-permute-start.2 = (bf16[24,8,128]{2,1,0:T(8,128)(2,1)S(1)}, bf16[24,8,128]{2,1,0:T(8,128)(2,1)S(1)}, u32[]{:S(2)}, u32[]{:S(2)}) collective-permute-start(bf16[24,8,128]{2,1,0:T(8,128)(2,1)S(1)} %pad_maximum_fusion.2.after), channel_id=1, source_target_pairs={{0,1},{1,2},{2,3},{5,4},{6,5},{7,6},{8,9},{9,10},{10,11},{13,12},{... | collective-permute-start | bytes 147464 | tf_op jit(solution)/shard_map/ppermute | solution.py:262
  13.7 3.4 %collective-permute-start.4 = (bf16[2,2,12,8,128]{4,3,2,1,0:T(8,128)(2,1)S(1)}, bf16[2,2,12,8,128]{4,3,2,1,0:T(8,128)(2,1)S(1)}, u32[]{:S(2)}, u32[]{:S(2)}) collective-permute-start(bf16[2,2,12,8,128]{4,3,2,1,0:T(8,128)(2,1)S(1)} %pad_maximum_fusion.1), channel_id=1, source_target_pairs={{0,4},{1,5},{2,6},{3,7},{4,0},{5,1},{6,2},{7,3},{8,12},{9,13},{10,... | collective-permute-start | bytes 294920 | tf_op jit(solution)/shard_map/ppermute | solution.py:262
  16.2 1.5 %collective-permute-start.5 = (bf16[78,8,128]{2,1,0:T(8,128)(2,1)S(1)}, bf16[78,8,128]{2,1,0:T(8,128)(2,1)S(1)}, u32[]{:S(2)}, u32[]{:S(2)}) collective-permute-start(bf16[78,8,128]{2,1,0:T(8,128)(2,1)S(1)} %bitcast.20), channel_id=1, source_target_pairs={{0,4},{1,5},{2,6},{3,7},{4,0},{5,1},{6,2},{7,3},{8,12},{9,13},{10,... | collective-permute-start | bytes 479240 | tf_op jit(solution)/shard_map/ppermute | solution.py:262
  17.7 9.8 %collective-permute-start.6 = (bf16[168,8,128]{2,1,0:T(8,128)(2,1)S(1)}, bf16[168,8,128]{2,1,0:T(8,128)(2,1)S(1)}, u32[]{:S(2)}, u32[]{:S(2)}) collective-permute-start(bf16[168,8,128]{2,1,0:T(8,128)(2,1)S(1)} %pad_maximum_fusion), channel_id=1, source_target_pairs={{4,8},{5,9},{6,10},{7,11},{8,4},{9,5},{10,6},{11,7},{12,16},{13,17... | collective-permute-start | bytes 1032200 | tf_op jit(solution)/shard_map/ppermute | solution.py:262
  26.2 7.4 %collective-permute-start.8 = (bf16[9,112,128]{2,1,0:T(8,128)(2,1)S(1)}, bf16[9,112,128]{2,1,0:T(8,128)(2,1)S(1)}, u32[]{:S(2)}, u32[]{:S(2)}) collective-permute-start(bf16[9,112,128]{2,1,0:T(8,128)(2,1)S(1)} %get-tuple-element.45.mine_on), channel_id=1, source_target_pairs={{0,4},{1,5},{2,6},{3,7},{4,0},{5,1},{6,2},{7,3},{8,12},{9,13},{10,... | collective-permute-start | bytes 774152 | tf_op jit(solution)/shard_map/ppermute | solution.py:262
  28.8 8.9 %collective-permute-start.7 = (bf16[9,112,128]{2,1,0:T(8,128)(2,1)S(1)}, bf16[9,112,128]{2,1,0:T(8,128)(2,1)S(1)}, u32[]{:S(2)}, u32[]{:S(2)}) collective-permute-start(bf16[9,112,128]{2,1,0:T(8,128)(2,1)S(1)} %middle_far.1.mine_cr), channel_id=1, source_target_pairs={{4,8},{5,9},{6,10},{7,11},{8,4},{9,5},{10,6},{11,7},{12,16},{13,17... | collective-permute-start | bytes 774152 | tf_op jit(solution)/shard_map/ppermute | solution.py:262

commit v4 on v3

--- a/solution.py
+++ b/solution.py
@@ -55,12 +55,11 @@
     return copies
 
 
-def load_kernel(after, kernel, kernel_next, *refs):
-    vectors, outs, sems = refs[:3], refs[3:-1], refs[-1]
-    copies = fetch(zip(vectors, outs[2:]), sems)
-    for n, source in enumerate((kernel, kernel_next)):
-        copies += fetch(weight_parts(source, outs[n], core_index()), sems, len(copies))
-        outs[n][:, 13, HI:, :] = jnp.zeros((3, HI, CH), jnp.bfloat16)
+def load_kernel(after, kernel, *refs):
+    vectors, (weight, *outs), sems = refs[:3], refs[3:-1], refs[-1]
+    copies = fetch(zip(vectors, outs), sems)
+    copies += fetch(weight_parts(kernel, weight, core_index()), sems, len(copies))
+    weight[:, 13, HI:, :] = jnp.zeros((3, HI, CH), jnp.bfloat16)
     for c in copies:
         c.wait()
 
@@ -85,9 +84,10 @@
             for k, slab in enumerate(pack(*pair)):
                 n = 3 * (f // 2) + k
                 mine[slot, n] = slab
-                left, right = slab[:TILE], slab[COLS - TILE :]
-                edge[slot * 6 + n] = jnp.where(core == 0, right, left)
-                on[SLABS + slot * 6 + n] = jnp.where(core == 0, left, right)
+                left, right = slab[:2], slab[COLS - 2 :]
+                for at in (2 * slot, 4 + 2 * slot):
+                    edge[n, at : at + 2] = jnp.where(core == 0, right, left)
+                    on[SLABS + n, at : at + 2] = jnp.where(core == 0, left, right)
                 (cr if slot else on)[n * TILES : (n + 1) * TILES] = slab.reshape(TILES, TILE, LANE)
 
 
@@ -150,26 +150,40 @@
         out[3 * (f // 2) + k] = slab
 
 
+def tip_of(tile, at, left_first):
+    a, b = tile[at : at + 2], tile[at + 4 : at + 6]
+    left, right = jnp.where(left_first, a, b), jnp.where(left_first, b, a)
+    return jnp.concatenate([right, right, left, left], axis=0)
+
+
 def tiles(ref, n, tip):
     return jnp.concatenate([ref[n * TILES : (n + 1) * TILES].reshape(COLS, LANE), tip], axis=0)
 
 
-def middle_near(mine, ta, on, on_prev, rim, weight, bias, gain, out, partial, taps):
+def middle_near(
+    mine, ta, on, on_prev, mine_rim, on_rim, weight, bias, gain, kernel, out, partial, weight_next, taps, sems
+):
+    core = core_index()
+    copies = fetch(weight_parts(kernel, weight_next, core), sems)
+    weight_next[:, 13, HI:, :] = jnp.zeros((3, HI, CH), jnp.bfloat16)
     for half in range(2):
         for pair in range(2):
             for row in range(3):
                 slabs = []
                 for n in range(3 * pair, 3 * pair + 3):
                     if row == 0:
-                        slabs.append(tiles(on if half else on_prev, n, rim[1 - half, 2, n]))
+                        slabs.append(tiles(on if half else on_prev, n, tip_of(on_rim[1 - half, n], 0, core == 1)))
                     else:
                         body = (mine if half else ta)[row - 1, n]
-                        slabs.append(jnp.concatenate([body, rim[1 - half, row - 1, n]], axis=0))
+                        tip = tip_of(mine_rim[1 - half, n], 2 * (row - 1), core == 0)
+                        slabs.append(jnp.concatenate([body, tip], axis=0))
                 put_row(taps, row, 4 * half + 2 * pair, slabs[:2], slabs[2])
     for f in range(0, 6, 2):
         put_second(out, taps_total(taps, weight, f, 2, "all"), f, bias, gain)
     for f in range(0, 6, 2):
         partial[f * CYC : (f + 2) * CYC] = taps_total(taps, weight, f, 2, "near")
+    for c in copies:
+        c.wait()
 
 
 def middle_far(cr, partial, weight, bias, gain, out, taps):
@@ -177,7 +191,7 @@
         for pair in range(2):
             slabs = []
             for n in range(3 * pair, 3 * pair + 3):
-                tip = cr[2 * SLABS + (1 - half) * 6 + n]
+                tip = tip_of(cr[2 * SLABS + (1 - half) * 6 + n], 2, core_index() == 1)
                 slabs.append(tiles(cr, n + 6 * (1 - half), tip))
             put_row(taps, 0, 4 * half + 2 * pair, slabs[:2], slabs[2])
     for f in range(0, 6, 2):
@@ -271,18 +285,19 @@
     weights = held(3, 14, LANE, CH)
     second = held(9, CYC, LANE)
     vector = held(1, CH, dtype=jnp.float32)
-    strip, rims = held(SLABS, TILE, LANE), held(12, TILE, LANE)
+    strip, rims = held(SLABS, TILE, LANE), held(6, TILE, LANE)
 
     mine, on_row, cr_row, edge, feat, _ = call(
         "first",
         first_kernel,
         (),
-        (held(2, 6, COLS, LANE), held(SLABS + 12, TILE, LANE), strip, rims, held(4, 2, CH, COLS), vector),
+        (held(2, 6, COLS, LANE), held(SLABS + 6, TILE, LANE), strip, rims, held(4, 2, CH, COLS), vector),
         far=(jnp.swapaxes(features, 2, 3), row(gain_first)),
         sems=9,
     )
     on = chip(on_row)
-    edges = jnp.concatenate([edge, on[SLABS:]])
+    upper = lax.broadcasted_iota(jnp.int32, (TILE, LANE), 0) < TILE // 2
+    edges = jnp.where(upper, edge, on[SLABS:])
     ta = send(mine, lambda t, y, x: (t + 1, y, x))
     side = send(edges, lambda t, y, x: (t, y, x - 1 if y % 2 else x + 1))
     side_prev = send(edges, lambda t, y, x: (t + 1, y, x - 1 if y % 2 else x + 1))
@@ -290,27 +305,28 @@
         "load",
         load_kernel,
         (edges,),
-        (weights, weights, vector, vector, vector),
-        far=(kernel_first, kernel_second, row(bias_first), row(gain_second), row(bias_second)),
-        sems=27,
+        (weights, vector, vector, vector),
+        far=(kernel_first, row(bias_first), row(gain_second), row(bias_second)),
+        sems=15,
     )
     side, side_prev, *held_args = lax.optimization_barrier((side, side_prev, *held_args))
-    weight, weight_next, bias, gain, bias_next = held_args
-    sides = jnp.stack([side, side_prev]).reshape(2, 2, 12, TILE, LANE)
-    others = chip(sides)[:, ::-1]
-    upper = lax.broadcasted_iota(jnp.int32, sides.shape, 3) < TILE // 2
-    rim = jnp.where(upper == (core_index() == 0), others, sides).reshape(2, 4, 6, TILE, LANE)
+    weight, bias, gain, bias_next = held_args
+    sides = jnp.stack([side, side_prev])
+    others = chip(sides)
+    mine_rim, on_rim = jnp.where(upper, sides, others), jnp.where(upper, others, sides)
     on_prev = chip(ta[0].reshape(SLABS, TILE, LANE))
-    message = jnp.concatenate([cr_row, ta[1].reshape(SLABS, TILE, LANE), rim[:, 1].reshape(12, TILE, LANE)])
+    message = jnp.concatenate([cr_row, ta[1].reshape(SLABS, TILE, LANE), mine_rim.reshape(12, TILE, LANE)])
     message, on_prev = lax.optimization_barrier((message, on_prev))
     cr = cross(message)
 
-    near, partial = call(
+    near, partial, weight_next = call(
         "middle_near",
         middle_near,
-        (mine, ta, on, on_prev, rim, weight, bias, gain),
-        (second, held(6 * CYC, CH, dtype=jnp.float32)),
+        (mine, ta, on, on_prev, mine_rim, on_rim, weight, bias, gain),
+        (second, held(6 * CYC, CH, dtype=jnp.float32), weights),
+        far=(kernel_second,),
         taps=(3, 8),
+        sems=12,
     )
     far = call("middle_far", middle_far, (cr, partial, weight, bias, gain), second, taps=(1, 8))
     out_near, partial = call(

time: 40 us -> 39.4 us (0.985)
  transfers between devices with their start and end apart: 9 -> 9, of which waited for: 5 -> 5; matrix products, arithmetic and copies ran while one was open for 1% -> 1% of each run, Pallas kernels for 27% -> 26%
where the time goes in v4:
time: 39.4 us; the launch traced here: 38.8 us
  starting transfers between devices  20.9 us (53%)
  Pallas kernels  13.4 us (34%)
  waiting for transfers between devices  4.16 us (11%)
    ppermute x9, starting transfers between devices, send(): return lax.ppermute(array, axes, routes(sizes, move))  20.9 us
    pallas_call x6, Pallas kernels, call(): pl.pallas_call(body, out_shape=outs, in_specs=[VMEM for _ in ins] + [HBM...  13.4 us
    ppermute x9, waiting for transfers between devices, send(): return lax.ppermute(array, axes, routes(sizes, move))  4.16 us
  transfers between devices with their start and end apart: 9, of which 5 were waited for; matrix products, arithmetic and copies ran while one was open for 1% of the time, Pallas kernels for 26%

profile of v4, /device:TPU:107, one launch (start us, length us, event | category | flops | bytes accessed | tf_op | source)
XLA Modules:
  0.0 38.8 jit_solution(1452474126054587137)
XLA Ops:
  0.0 1.6 %first.1 = (bf16[2,6,104,128]{3,2,1,0:T(8,128)(2,1)S(1)}, bf16[84,8,128]{2,1,0:T(8,128)(2,1)S(1)}, bf16[78,8,128]{2,1,0:T(8,128)(2,1)S(1)}, bf16[6,8,128]{2,1,0:...) custom-call(bf16[4,2,192,104]{3,2,1,0:T(8,128)(2,1)} %bitcast.13, f32[1,192]{1,0:T(1,128)} %bitcast.19), custom_call_target="tpu_custom_call" | custom-call | tf_op jit(solution)/shard_map/first/pallas_call | solution.py:251
  1.6 0.8 %collective-permute-start.1 = (bf16[84,8,128]{2,1,0:T(8,128)(2,1)S(1)}, bf16[84,8,128]{2,1,0:T(8,128)(2,1)S(1)}, u32[]{:S(2)}, u32[]{:S(2)}) collective-permute-start(bf16[84,8,128]{2,1,0:T(8,128)(2,1)S(1)} %get-tuple-element.30), channel_id=1, source_target_pairs={{0,4},{1,5},{2,6},{3,7},{4,0},{5,1},{6,2},{7,3},{8,12},{9,13},{10,... | collective-permute-start | bytes 516104 | tf_op jit(solution)/shard_map/ppermute | solution.py:276
  2.4 3.2 %collective-permute-start = (bf16[2,6,104,128]{3,2,1,0:T(8,128)(2,1)S(1)}, bf16[2,6,104,128]{3,2,1,0:T(8,128)(2,1)S(1)}, u32[]{:S(2)}, u32[]{:S(2)}) collective-permute-start(bf16[2,6,104,128]{3,2,1,0:T(8,128)(2,1)S(1)} %get-tuple-element.28.mine), channel_id=1, source_target_pairs={{0,64},{1,65},{2,66},{3,67},{4,68},{5,69},{6,70},{7,71},{8,72},{9,... | collective-permute-start | bytes 958472 | tf_op jit(solution)/shard_map/ppermute | solution.py:276
  5.6 0.0 collective-permute-done.1.on
  5.6 0.1 slice_select_fusion.after
  5.7 2.9 %collective-permute-start.3 = (bf16[6,8,128]{2,1,0:T(8,128)(2,1)S(1)}, bf16[6,8,128]{2,1,0:T(8,128)(2,1)S(1)}, u32[]{:S(2)}, u32[]{:S(2)}) collective-permute-start(bf16[6,8,128]{2,1,0:T(8,128)(2,1)S(1)} %slice_select_fusion.after), channel_id=1, source_target_pairs={{0,65},{1,66},{2,67},{5,68},{6,69},{7,70},{8,73},{9,74},{10,75},{1... | collective-permute-start | bytes 36872 | tf_op jit(solution)/shard_map/ppermute | solution.py:276
  8.6 1.9 %collective-permute-start.2 = (bf16[6,8,128]{2,1,0:T(8,128)(2,1)S(1)}, bf16[6,8,128]{2,1,0:T(8,128)(2,1)S(1)}, u32[]{:S(2)}, u32[]{:S(2)}) collective-permute-start(bf16[6,8,128]{2,1,0:T(8,128)(2,1)S(1)} %slice_select_fusion.after), channel_id=1, source_target_pairs={{0,1},{1,2},{2,3},{5,4},{6,5},{7,6},{8,9},{9,10},{10,11},{13,12},{... | collective-permute-start | bytes 36872 | tf_op jit(solution)/shard_map/ppermute | solution.py:276
  10.5 1.9 %load.1 = (bf16[3,14,128,192]{3,2,1,0:T(8,128)(2,1)S(1)}, f32[1,192]{1,0:T(1,128)S(1)}, f32[1,192]{1,0:T(1,128)S(1)}, f32[1,192]{1,0:T(1,128)S(1)}) custom-call(bf16[6,8,128]{2,1,0:T(8,128)(2,1)S(1)} %slice_select_fusion.after, bf16[3,3,3,192,192]{4,3,2,1,0:T(8,128)(2,1)} %kernel.2, f32[1,192]{1,0:T(1,128)} %bitcast.20, f32[1,192]{1,0:T(1,128)} %bitcast.21, ...), custom_call_target="tpu_custom_call" | custom-call | tf_op jit(solution)/shard_map/load/pallas_call | solution.py:251
  12.4 0.0 collective-permute-done.3
  12.4 0.9 %collective-permute-done.2 = bf16[6,8,128]{2,1,0:T(8,128)(2,1)S(1)} collective-permute-done((bf16[6,8,128]{2,1,0:T(8,128)(2,1)S(1)}, bf16[6,8,128]{2,1,0:T(8,128)(2,1)S(1)}, u32[]{:S(2)}, u32[]{:S(2)}) %collective-permute-start.2) | collective-permute-done | bytes 12320 | tf_op jit(solution)/shard_map/ppermute | solution.py:276
  13.3 2.4 %collective-permute-start.4 = (bf16[2,6,8,128]{3,2,1,0:T(8,128)(2,1)S(1)}, bf16[2,6,8,128]{3,2,1,0:T(8,128)(2,1)S(1)}, u32[]{:S(2)}, u32[]{:S(2)}) collective-permute-start(bf16[2,6,8,128]{3,2,1,0:T(8,128)(2,1)S(1)} %pad_maximum_fusion.1), channel_id=1, source_target_pairs={{0,4},{1,5},{2,6},{3,7},{4,0},{5,1},{6,2},{7,3},{8,12},{9,13},{10,... | collective-permute-start | bytes 73736 | tf_op jit(solution)/shard_map/ppermute | solution.py:276
  15.7 0.0 collective-permute-done.ta
  15.7 0.1 collective-permute-start.5
  15.8 0.7 %collective-permute-done.4 = bf16[2,6,8,128]{3,2,1,0:T(8,128)(2,1)S(1)} collective-permute-done((bf16[2,6,8,128]{3,2,1,0:T(8,128)(2,1)S(1)}, bf16[2,6,8,128]{3,2,1,0:T(8,128)(2,1)S(1)}, u32[]{:S(2)}, u32[]{:S(2)}) %collective-permute-start.4) | collective-permute-done | bytes 24608 | tf_op jit(solution)/shard_map/ppermute | solution.py:276
  16.5 0.1 broadcast_select_fusion
  16.7 0.5 %collective-permute-done.5.on_prev = bf16[78,8,128]{2,1,0:T(8,128)(2,1)S(1)} collective-permute-done((bf16[78,8,128]{2,1,0:T(8,128)(2,1)S(1)}, bf16[78,8,128]{2,1,0:T(8,128)(2,1)S(1)}, u32[]{:S(2)}, u32[]{:S(2)}) %collective-permute-start.5) | collective-permute-done | bytes 159776 | tf_op jit(solution)/shard_map/ppermute | solution.py:276
  17.2 4.8 %collective-permute-start.6 = (bf16[168,8,128]{2,1,0:T(8,128)(2,1)S(1)}, bf16[168,8,128]{2,1,0:T(8,128)(2,1)S(1)}, u32[]{:S(2)}, u32[]{:S(2)}) collective-permute-start(bf16[168,8,128]{2,1,0:T(8,128)(2,1)S(1)} %pad_maximum_fusion), channel_id=1, source_target_pairs={{4,8},{5,9},{6,10},{7,11},{8,4},{9,5},{10,6},{11,7},{12,16},{13,17... | collective-permute-start | bytes 1032200 | tf_op jit(solution)/shard_map/ppermute | solution.py:276
  22.0 4.3 %middle_near.1 = (bf16[9,112,128]{2,1,0:T(8,128)(2,1)S(1)}, f32[672,192]{1,0:T(8,128)S(1)}, bf16[3,14,128,192]{3,2,1,0:T(8,128)(2,1)S(1)}) custom-call(bf16[2,6,104,128]{3,2,1,0:T(8,128)(2,1)S(1)} %get-tuple-element.28.mine, bf16[2,6,104,128]{3,2,1,0:T(8,128)(2,1)S(1)} %collective-permute-done.ta, bf16[84,8,128]{2,1,0:T(8,128)(2,1)S(1)} %collective-permute-done.1.on, ...), custom_call_target="tpu_custom_call" | custom-call | tf_op jit(solution)/shard_map/middle_near/pallas_call | solution.py:251
  26.3 0.1 collective-permute-start.8
  26.4 0.6 %collective-permute-done.6.cr = bf16[168,8,128]{2,1,0:T(8,128)(2,1)S(1)} collective-permute-done((bf16[168,8,128]{2,1,0:T(8,128)(2,1)S(1)}, bf16[168,8,128]{2,1,0:T(8,128)(2,1)S(1)}, u32[]{:S(2)}, u32[]{:S(2)}) %collective-permute-start.6) | collective-permute-done | bytes 344096 | tf_op jit(solution)/shard_map/ppermute | solution.py:276
  27.0 1.3 %middle_far.1.mine_cr = bf16[9,112,128]{2,1,0:T(8,128)(2,1)S(1)} custom-call(bf16[168,8,128]{2,1,0:T(8,128)(2,1)S(1)} %collective-permute-done.6.cr, f32[672,192]{1,0:T(8,128)S(1)} %get-tuple-element.42.partial, bf16[3,14,128,192]{3,2,1,0:T(8,128)(2,1)S(1)} %get-tuple-element.39.weight, f32[1,192]{1,0:T(1,128)S(1)} %get-tuple-element.40.bias, ...), custom_call_target="tpu_custom_call" | custom-call | tf_op jit(solution)/shard_map/middle_far/pallas_call | solution.py:251
  28.3 4.8 %collective-permute-start.7 = (bf16[9,112,128]{2,1,0:T(8,128)(2,1)S(1)}, bf16[9,112,128]{2,1,0:T(8,128)(2,1)S(1)}, u32[]{:S(2)}, u32[]{:S(2)}) collective-permute-start(bf16[9,112,128]{2,1,0:T(8,128)(2,1)S(1)} %middle_far.1.mine_cr), channel_id=1, source_target_pairs={{4,8},{5,9},{6,10},{7,11},{8,4},{9,5},{10,6},{11,7},{12,16},{13,17... | collective-permute-start | bytes 774152 | tf_op jit(solution)/shard_map/ppermute | solution.py:276
  33.1 0.0 collective-permute-done.8.on
  33.1 2.6 %last_near.1 = (bf16[4,192,104]{2,1,0:T(8,128)(2,1)S(1)}, f32[448,192]{1,0:T(8,128)S(1)}) custom-call(bf16[9,112,128]{2,1,0:T(8,128)(2,1)S(1)} %get-tuple-element.43.mine_on, bf16[9,112,128]{2,1,0:T(8,128)(2,1)S(1)} %middle_far.1.mine_cr, bf16[9,112,128]{2,1,0:T(8,128)(2,1)S(1)} %collective-permute-done.8.on, ...), custom_call_target="tpu_custom_call" | custom-call | tf_op jit(solution)/shard_map/last_near/pallas_call | solution.py:251
  35.8 1.4 %collective-permute-done.7.cr = bf16[9,112,128]{2,1,0:T(8,128)(2,1)S(1)} collective-permute-done((bf16[9,112,128]{2,1,0:T(8,128)(2,1)S(1)}, bf16[9,112,128]{2,1,0:T(8,128)(2,1)S(1)}, u32[]{:S(2)}, u32[]{:S(2)}) %collective-permute-start.7) | collective-permute-done | bytes 258080 | tf_op jit(solution)/shard_map/ppermute | solution.py:276
  37.2 1.6 %last_far.1 = bf16[4,2,192,104]{3,2,1,0:T(8,128)(2,1)} custom-call(bf16[9,112,128]{2,1,0:T(8,128)(2,1)S(1)} %collective-permute-done.7.cr, f32[448,192]{1,0:T(8,128)S(1)} %get-tuple-element.47.partial, bf16[4,192,104]{2,1,0:T(8,128)(2,1)S(1)} %get-tuple-element.48.near, bf16[4,2,192,104]{3,2,1,0:T(8,128)(2,1)S(1)} %get-tuple-element.44.feat, ...), custom_call_target="tpu_custom_call" | custom-call | tf_op jit(solution)/shard_map/last_far/pallas_call | solution.py:251
  (4 shorter events, 0.1 us)
Async XLA Ops:
  1.6 4.0 %collective-permute-start.1 = (bf16[84,8,128]{2,1,0:T(8,128)(2,1)S(1)}, bf16[84,8,128]{2,1,0:T(8,128)(2,1)S(1)}, u32[]{:S(2)}, u32[]{:S(2)}) collective-permute-start(bf16[84,8,128]{2,1,0:T(8,128)(2,1)S(1)} %get-tuple-element.30), channel_id=1, source_target_pairs={{0,4},{1,5},{2,6},{3,7},{4,0},{5,1},{6,2},{7,3},{8,12},{9,13},{10,... | collective-permute-start | bytes 516104 | tf_op jit(solution)/shard_map/ppermute | solution.py:276
  2.4 13.3 %collective-permute-start = (bf16[2,6,104,128]{3,2,1,0:T(8,128)(2,1)S(1)}, bf16[2,6,104,128]{3,2,1,0:T(8,128)(2,1)S(1)}, u32[]{:S(2)}, u32[]{:S(2)}) collective-permute-start(bf16[2,6,104,128]{3,2,1,0:T(8,128)(2,1)S(1)} %get-tuple-element.28.mine), channel_id=1, source_target_pairs={{0,64},{1,65},{2,66},{3,67},{4,68},{5,69},{6,70},{7,71},{8,72},{9,... | collective-permute-start | bytes 958472 | tf_op jit(solution)/shard_map/ppermute | solution.py:276
  5.7 6.7 %collective-permute-start.3 = (bf16[6,8,128]{2,1,0:T(8,128)(2,1)S(1)}, bf16[6,8,128]{2,1,0:T(8,128)(2,1)S(1)}, u32[]{:S(2)}, u32[]{:S(2)}) collective-permute-start(bf16[6,8,128]{2,1,0:T(8,128)(2,1)S(1)} %slice_select_fusion.after), channel_id=1, source_target_pairs={{0,65},{1,66},{2,67},{5,68},{6,69},{7,70},{8,73},{9,74},{10,75},{1... | collective-permute-start | bytes 36872 | tf_op jit(solution)/shard_map/ppermute | solution.py:276
  8.6 4.7 %collective-permute-start.2 = (bf16[6,8,128]{2,1,0:T(8,128)(2,1)S(1)}, bf16[6,8,128]{2,1,0:T(8,128)(2,1)S(1)}, u32[]{:S(2)}, u32[]{:S(2)}) collective-permute-start(bf16[6,8,128]{2,1,0:T(8,128)(2,1)S(1)} %slice_select_fusion.after), channel_id=1, source_target_pairs={{0,1},{1,2},{2,3},{5,4},{6,5},{7,6},{8,9},{9,10},{10,11},{13,12},{... | collective-permute-start | bytes 36872 | tf_op jit(solution)/shard_map/ppermute | solution.py:276
  13.3 3.2 %collective-permute-start.4 = (bf16[2,6,8,128]{3,2,1,0:T(8,128)(2,1)S(1)}, bf16[2,6,8,128]{3,2,1,0:T(8,128)(2,1)S(1)}, u32[]{:S(2)}, u32[]{:S(2)}) collective-permute-start(bf16[2,6,8,128]{3,2,1,0:T(8,128)(2,1)S(1)} %pad_maximum_fusion.1), channel_id=1, source_target_pairs={{0,4},{1,5},{2,6},{3,7},{4,0},{5,1},{6,2},{7,3},{8,12},{9,13},{10,... | collective-permute-start | bytes 73736 | tf_op jit(solution)/shard_map/ppermute | solution.py:276
  15.7 1.5 %collective-permute-start.5 = (bf16[78,8,128]{2,1,0:T(8,128)(2,1)S(1)}, bf16[78,8,128]{2,1,0:T(8,128)(2,1)S(1)}, u32[]{:S(2)}, u32[]{:S(2)}) collective-permute-start(bf16[78,8,128]{2,1,0:T(8,128)(2,1)S(1)} %bitcast.14), channel_id=1, source_target_pairs={{0,4},{1,5},{2,6},{3,7},{4,0},{5,1},{6,2},{7,3},{8,12},{9,13},{10,... | collective-permute-start | bytes 479240 | tf_op jit(solution)/shard_map/ppermute | solution.py:276
  17.2 9.8 %collective-permute-start.6 = (bf16[168,8,128]{2,1,0:T(8,128)(2,1)S(1)}, bf16[168,8,128]{2,1,0:T(8,128)(2,1)S(1)}, u32[]{:S(2)}, u32[]{:S(2)}) collective-permute-start(bf16[168,8,128]{2,1,0:T(8,128)(2,1)S(1)} %pad_maximum_fusion), channel_id=1, source_target_pairs={{4,8},{5,9},{6,10},{7,11},{8,4},{9,5},{10,6},{11,7},{12,16},{13,17... | collective-permute-start | bytes 1032200 | tf_op jit(solution)/shard_map/ppermute | solution.py:276
  26.3 6.8 %collective-permute-start.8 = (bf16[9,112,128]{2,1,0:T(8,128)(2,1)S(1)}, bf16[9,112,128]{2,1,0:T(8,128)(2,1)S(1)}, u32[]{:S(2)}, u32[]{:S(2)}) collective-permute-start(bf16[9,112,128]{2,1,0:T(8,128)(2,1)S(1)} %get-tuple-element.43.mine_on), channel_id=1, source_target_pairs={{0,4},{1,5},{2,6},{3,7},{4,0},{5,1},{6,2},{7,3},{8,12},{9,13},{10,... | collective-permute-start | bytes 774152 | tf_op jit(solution)/shard_map/ppermute | solution.py:276
  28.3 8.9 %collective-permute-start.7 = (bf16[9,112,128]{2,1,0:T(8,128)(2,1)S(1)}, bf16[9,112,128]{2,1,0:T(8,128)(2,1)S(1)}, u32[]{:S(2)}, u32[]{:S(2)}) collective-permute-start(bf16[9,112,128]{2,1,0:T(8,128)(2,1)S(1)} %middle_far.1.mine_cr), channel_id=1, source_target_pairs={{4,8},{5,9},{6,10},{7,11},{8,4},{9,5},{10,6},{11,7},{12,16},{13,17... | collective-permute-start | bytes 774152 | tf_op jit(solution)/shard_map/ppermute | solution.py:276

commit v5 on v4

--- a/solution.py
+++ b/solution.py
@@ -86,8 +86,8 @@
                 mine[slot, n] = slab
                 left, right = slab[:2], slab[COLS - 2 :]
                 for at in (2 * slot, 4 + 2 * slot):
-                    edge[n, at : at + 2] = jnp.where(core == 0, right, left)
-                    on[SLABS + n, at : at + 2] = jnp.where(core == 0, left, right)
+                    edge[n, at : at + 2] = jnp.where(core == 0, left, right)
+                    on[SLABS + n, at : at + 2] = jnp.where(core == 0, right, left)
                 (cr if slot else on)[n * TILES : (n + 1) * TILES] = slab.reshape(TILES, TILE, LANE)
 
 
@@ -172,10 +172,10 @@
                 slabs = []
                 for n in range(3 * pair, 3 * pair + 3):
                     if row == 0:
-                        slabs.append(tiles(on if half else on_prev, n, tip_of(on_rim[1 - half, n], 0, core == 1)))
+                        slabs.append(tiles(on if half else on_prev, n, tip_of(on_rim[1 - half, n], 0, core == 0)))
                     else:
                         body = (mine if half else ta)[row - 1, n]
-                        tip = tip_of(mine_rim[1 - half, n], 2 * (row - 1), core == 0)
+                        tip = tip_of(mine_rim[1 - half, n], 2 * (row - 1), core == 1)
                         slabs.append(jnp.concatenate([body, tip], axis=0))
                 put_row(taps, row, 4 * half + 2 * pair, slabs[:2], slabs[2])
     for f in range(0, 6, 2):
@@ -191,7 +191,7 @@
         for pair in range(2):
             slabs = []
             for n in range(3 * pair, 3 * pair + 3):
-                tip = tip_of(cr[2 * SLABS + (1 - half) * 6 + n], 2, core_index() == 1)
+                tip = tip_of(cr[2 * SLABS + (1 - half) * 6 + n], 2, core_index() == 0)
                 slabs.append(tiles(cr, n + 6 * (1 - half), tip))
             put_row(taps, 0, 4 * half + 2 * pair, slabs[:2], slabs[2])
     for f in range(0, 6, 2):
@@ -299,8 +299,8 @@
     upper = lax.broadcasted_iota(jnp.int32, (TILE, LANE), 0) < TILE // 2
     edges = jnp.where(upper, edge, on[SLABS:])
     ta = send(mine, lambda t, y, x: (t + 1, y, x))
-    side = send(edges, lambda t, y, x: (t, y, x - 1 if y % 2 else x + 1))
-    side_prev = send(edges, lambda t, y, x: (t + 1, y, x - 1 if y % 2 else x + 1))
+    side = send(edges, lambda t, y, x: (t, y ^ 1, x + 1 if y % 2 else x - 1))
+    side_prev = send(edges, lambda t, y, x: (t + 1, y ^ 1, x + 1 if y % 2 else x - 1))
     held_args = call(
         "load",
         load_kernel,
@@ -313,7 +313,7 @@
     weight, bias, gain, bias_next = held_args
     sides = jnp.stack([side, side_prev])
     others = chip(sides)
-    mine_rim, on_rim = jnp.where(upper, sides, others), jnp.where(upper, others, sides)
+    mine_rim, on_rim = jnp.where(upper, others, sides), jnp.where(upper, sides, others)
     on_prev = chip(ta[0].reshape(SLABS, TILE, LANE))
     message = jnp.concatenate([cr_row, ta[1].reshape(SLABS, TILE, LANE), mine_rim.reshape(12, TILE, LANE)])
     message, on_prev = lax.optimization_barrier((message, on_prev))

time: 39.4 us -> 38.8 us (0.985)
  waiting for transfers between devices: 4.16 us -> 3.63 us
    ppermute x9, waiting for transfers between devices: 4.16 us -> 3.63 us  [send(): return lax.ppermute(array, axes, routes(sizes, move))]
  transfers between devices with their start and end apart: 9 -> 9, of which waited for: 5 -> 5; matrix products, arithmetic and copies ran while one was open for 1% -> 1% of each run, Pallas kernels for 26% -> 27%
where the time goes in v5:
time: 38.8 us; the launch traced here: 38.1 us
  starting transfers between devices  20.7 us (53%)
  Pallas kernels  13.4 us (35%)
  waiting for transfers between devices  3.63 us (9%)
    ppermute x9, starting transfers between devices, send(): return lax.ppermute(array, axes, routes(sizes, move))  20.7 us
    pallas_call x6, Pallas kernels, call(): pl.pallas_call(body, out_shape=outs, in_specs=[VMEM for _ in ins] + [HBM...  13.4 us
    ppermute x9, waiting for transfers between devices, send(): return lax.ppermute(array, axes, routes(sizes, move))  3.63 us
  transfers between devices with their start and end apart: 9, of which 5 were waited for; matrix products, arithmetic and copies ran while one was open for 1% of the time, Pallas kernels for 27%

profile of v5, /device:TPU:107, one launch (start us, length us, event | category | flops | bytes accessed | tf_op | source)
XLA Modules:
  0.0 38.1 jit_solution(8554378446081395434)
XLA Ops:
  0.0 1.6 %first.1 = (bf16[2,6,104,128]{3,2,1,0:T(8,128)(2,1)S(1)}, bf16[84,8,128]{2,1,0:T(8,128)(2,1)S(1)}, bf16[78,8,128]{2,1,0:T(8,128)(2,1)S(1)}, bf16[6,8,128]{2,1,0:...) custom-call(bf16[4,2,192,104]{3,2,1,0:T(8,128)(2,1)} %bitcast.13, f32[1,192]{1,0:T(1,128)} %bitcast.19), custom_call_target="tpu_custom_call" | custom-call | tf_op jit(solution)/shard_map/first/pallas_call | solution.py:251
  1.6 0.8 %collective-permute-start.1 = (bf16[84,8,128]{2,1,0:T(8,128)(2,1)S(1)}, bf16[84,8,128]{2,1,0:T(8,128)(2,1)S(1)}, u32[]{:S(2)}, u32[]{:S(2)}) collective-permute-start(bf16[84,8,128]{2,1,0:T(8,128)(2,1)S(1)} %get-tuple-element.30), channel_id=1, source_target_pairs={{0,4},{1,5},{2,6},{3,7},{4,0},{5,1},{6,2},{7,3},{8,12},{9,13},{10,... | collective-permute-start | bytes 516104 | tf_op jit(solution)/shard_map/ppermute | solution.py:276
  2.4 3.2 %collective-permute-start = (bf16[2,6,104,128]{3,2,1,0:T(8,128)(2,1)S(1)}, bf16[2,6,104,128]{3,2,1,0:T(8,128)(2,1)S(1)}, u32[]{:S(2)}, u32[]{:S(2)}) collective-permute-start(bf16[2,6,104,128]{3,2,1,0:T(8,128)(2,1)S(1)} %get-tuple-element.28.mine), channel_id=1, source_target_pairs={{0,64},{1,65},{2,66},{3,67},{4,68},{5,69},{6,70},{7,71},{8,72},{9,... | collective-permute-start | bytes 958472 | tf_op jit(solution)/shard_map/ppermute | solution.py:276
  5.6 0.0 collective-permute-done.1.on
  5.6 0.1 slice_select_fusion.after
  5.7 4.0 %collective-permute-start.3 = (bf16[6,8,128]{2,1,0:T(8,128)(2,1)S(1)}, bf16[6,8,128]{2,1,0:T(8,128)(2,1)S(1)}, u32[]{:S(2)}, u32[]{:S(2)}) collective-permute-start(bf16[6,8,128]{2,1,0:T(8,128)(2,1)S(1)} %slice_select_fusion.after), channel_id=1, source_target_pairs={{1,68},{2,69},{3,70},{4,65},{5,66},{6,67},{9,76},{10,77},{11,78},{... | collective-permute-start | bytes 36872 | tf_op jit(solution)/shard_map/ppermute | solution.py:276
  9.7 2.3 %collective-permute-start.2 = (bf16[6,8,128]{2,1,0:T(8,128)(2,1)S(1)}, bf16[6,8,128]{2,1,0:T(8,128)(2,1)S(1)}, u32[]{:S(2)}, u32[]{:S(2)}) collective-permute-start(bf16[6,8,128]{2,1,0:T(8,128)(2,1)S(1)} %slice_select_fusion.after), channel_id=1, source_target_pairs={{1,4},{2,5},{3,6},{4,1},{5,2},{6,3},{9,12},{10,13},{11,14},{12,9},... | collective-permute-start | bytes 36872 | tf_op jit(solution)/shard_map/ppermute | solution.py:276
  12.0 1.9 %load.1 = (bf16[3,14,128,192]{3,2,1,0:T(8,128)(2,1)S(1)}, f32[1,192]{1,0:T(1,128)S(1)}, f32[1,192]{1,0:T(1,128)S(1)}, f32[1,192]{1,0:T(1,128)S(1)}) custom-call(bf16[6,8,128]{2,1,0:T(8,128)(2,1)S(1)} %slice_select_fusion.after, bf16[3,3,3,192,192]{4,3,2,1,0:T(8,128)(2,1)} %kernel.2, f32[1,192]{1,0:T(1,128)} %bitcast.20, f32[1,192]{1,0:T(1,128)} %bitcast.21, ...), custom_call_target="tpu_custom_call" | custom-call | tf_op jit(solution)/shard_map/load/pallas_call | solution.py:251
  13.8 0.0 collective-permute-done.3
  13.8 0.9 %collective-permute-done.2 = bf16[6,8,128]{2,1,0:T(8,128)(2,1)S(1)} collective-permute-done((bf16[6,8,128]{2,1,0:T(8,128)(2,1)S(1)}, bf16[6,8,128]{2,1,0:T(8,128)(2,1)S(1)}, u32[]{:S(2)}, u32[]{:S(2)}) %collective-permute-start.2) | collective-permute-done | bytes 12320 | tf_op jit(solution)/shard_map/ppermute | solution.py:276
  14.7 0.0 collective-permute-start.4
  14.7 0.0 collective-permute-done.ta
  14.8 0.6 %collective-permute-start.5 = (bf16[78,8,128]{2,1,0:T(8,128)(2,1)S(1)}, bf16[78,8,128]{2,1,0:T(8,128)(2,1)S(1)}, u32[]{:S(2)}, u32[]{:S(2)}) collective-permute-start(bf16[78,8,128]{2,1,0:T(8,128)(2,1)S(1)} %bitcast.14), channel_id=1, source_target_pairs={{0,4},{1,5},{2,6},{3,7},{4,0},{5,1},{6,2},{7,3},{8,12},{9,13},{10,... | collective-permute-start | bytes 479240 | tf_op jit(solution)/shard_map/ppermute | solution.py:276
  15.4 0.6 %collective-permute-done.4 = bf16[2,6,8,128]{3,2,1,0:T(8,128)(2,1)S(1)} collective-permute-done((bf16[2,6,8,128]{3,2,1,0:T(8,128)(2,1)S(1)}, bf16[2,6,8,128]{3,2,1,0:T(8,128)(2,1)S(1)}, u32[]{:S(2)}, u32[]{:S(2)}) %collective-permute-start.4) | collective-permute-done | bytes 24608 | tf_op jit(solution)/shard_map/ppermute | solution.py:276
  15.9 0.1 broadcast_select_fusion
  16.1 0.3 collective-permute-done.5.on_prev
  16.4 5.0 %collective-permute-start.6 = (bf16[168,8,128]{2,1,0:T(8,128)(2,1)S(1)}, bf16[168,8,128]{2,1,0:T(8,128)(2,1)S(1)}, u32[]{:S(2)}, u32[]{:S(2)}) collective-permute-start(bf16[168,8,128]{2,1,0:T(8,128)(2,1)S(1)} %pad_maximum_fusion), channel_id=1, source_target_pairs={{4,8},{5,9},{6,10},{7,11},{8,4},{9,5},{10,6},{11,7},{12,16},{13,17... | collective-permute-start | bytes 1032200 | tf_op jit(solution)/shard_map/ppermute | solution.py:276
  21.4 4.3 %middle_near.1 = (bf16[9,112,128]{2,1,0:T(8,128)(2,1)S(1)}, f32[672,192]{1,0:T(8,128)S(1)}, bf16[3,14,128,192]{3,2,1,0:T(8,128)(2,1)S(1)}) custom-call(bf16[2,6,104,128]{3,2,1,0:T(8,128)(2,1)S(1)} %get-tuple-element.28.mine, bf16[2,6,104,128]{3,2,1,0:T(8,128)(2,1)S(1)} %collective-permute-done.ta, bf16[84,8,128]{2,1,0:T(8,128)(2,1)S(1)} %collective-permute-done.1.on, ...), custom_call_target="tpu_custom_call" | custom-call | tf_op jit(solution)/shard_map/middle_near/pallas_call | solution.py:251
  25.7 0.1 collective-permute-start.8
  25.8 0.5 %collective-permute-done.6.cr = bf16[168,8,128]{2,1,0:T(8,128)(2,1)S(1)} collective-permute-done((bf16[168,8,128]{2,1,0:T(8,128)(2,1)S(1)}, bf16[168,8,128]{2,1,0:T(8,128)(2,1)S(1)}, u32[]{:S(2)}, u32[]{:S(2)}) %collective-permute-start.6) | collective-permute-done | bytes 344096 | tf_op jit(solution)/shard_map/ppermute | solution.py:276
  26.3 1.3 %middle_far.1.mine_cr = bf16[9,112,128]{2,1,0:T(8,128)(2,1)S(1)} custom-call(bf16[168,8,128]{2,1,0:T(8,128)(2,1)S(1)} %collective-permute-done.6.cr, f32[672,192]{1,0:T(8,128)S(1)} %get-tuple-element.42.partial, bf16[3,14,128,192]{3,2,1,0:T(8,128)(2,1)S(1)} %get-tuple-element.39.weight, f32[1,192]{1,0:T(1,128)S(1)} %get-tuple-element.40.bias, ...), custom_call_target="tpu_custom_call" | custom-call | tf_op jit(solution)/shard_map/middle_far/pallas_call | solution.py:251
  27.7 4.8 %collective-permute-start.7 = (bf16[9,112,128]{2,1,0:T(8,128)(2,1)S(1)}, bf16[9,112,128]{2,1,0:T(8,128)(2,1)S(1)}, u32[]{:S(2)}, u32[]{:S(2)}) collective-permute-start(bf16[9,112,128]{2,1,0:T(8,128)(2,1)S(1)} %middle_far.1.mine_cr), channel_id=1, source_target_pairs={{4,8},{5,9},{6,10},{7,11},{8,4},{9,5},{10,6},{11,7},{12,16},{13,17... | collective-permute-start | bytes 774152 | tf_op jit(solution)/shard_map/ppermute | solution.py:276
  32.5 0.0 collective-permute-done.8.on
  32.5 2.6 %last_near.1 = (bf16[4,192,104]{2,1,0:T(8,128)(2,1)S(1)}, f32[448,192]{1,0:T(8,128)S(1)}) custom-call(bf16[9,112,128]{2,1,0:T(8,128)(2,1)S(1)} %get-tuple-element.43.mine_on, bf16[9,112,128]{2,1,0:T(8,128)(2,1)S(1)} %middle_far.1.mine_cr, bf16[9,112,128]{2,1,0:T(8,128)(2,1)S(1)} %collective-permute-done.8.on, ...), custom_call_target="tpu_custom_call" | custom-call | tf_op jit(solution)/shard_map/last_near/pallas_call | solution.py:251
  35.2 1.3 %collective-permute-done.7.cr = bf16[9,112,128]{2,1,0:T(8,128)(2,1)S(1)} collective-permute-done((bf16[9,112,128]{2,1,0:T(8,128)(2,1)S(1)}, bf16[9,112,128]{2,1,0:T(8,128)(2,1)S(1)}, u32[]{:S(2)}, u32[]{:S(2)}) %collective-permute-start.7) | collective-permute-done | bytes 258080 | tf_op jit(solution)/shard_map/ppermute | solution.py:276
  36.5 1.6 %last_far.1 = bf16[4,2,192,104]{3,2,1,0:T(8,128)(2,1)} custom-call(bf16[9,112,128]{2,1,0:T(8,128)(2,1)S(1)} %collective-permute-done.7.cr, f32[448,192]{1,0:T(8,128)S(1)} %get-tuple-element.47.partial, bf16[4,192,104]{2,1,0:T(8,128)(2,1)S(1)} %get-tuple-element.48.near, bf16[4,2,192,104]{3,2,1,0:T(8,128)(2,1)S(1)} %get-tuple-element.44.feat, ...), custom_call_target="tpu_custom_call" | custom-call | tf_op jit(solution)/shard_map/last_far/pallas_call | solution.py:251
  (4 shorter events, 0.1 us)
Async XLA Ops:
  1.6 4.0 %collective-permute-start.1 = (bf16[84,8,128]{2,1,0:T(8,128)(2,1)S(1)}, bf16[84,8,128]{2,1,0:T(8,128)(2,1)S(1)}, u32[]{:S(2)}, u32[]{:S(2)}) collective-permute-start(bf16[84,8,128]{2,1,0:T(8,128)(2,1)S(1)} %get-tuple-element.30), channel_id=1, source_target_pairs={{0,4},{1,5},{2,6},{3,7},{4,0},{5,1},{6,2},{7,3},{8,12},{9,13},{10,... | collective-permute-start | bytes 516104 | tf_op jit(solution)/shard_map/ppermute | solution.py:276
  2.4 12.3 %collective-permute-start = (bf16[2,6,104,128]{3,2,1,0:T(8,128)(2,1)S(1)}, bf16[2,6,104,128]{3,2,1,0:T(8,128)(2,1)S(1)}, u32[]{:S(2)}, u32[]{:S(2)}) collective-permute-start(bf16[2,6,104,128]{3,2,1,0:T(8,128)(2,1)S(1)} %get-tuple-element.28.mine), channel_id=1, source_target_pairs={{0,64},{1,65},{2,66},{3,67},{4,68},{5,69},{6,70},{7,71},{8,72},{9,... | collective-permute-start | bytes 958472 | tf_op jit(solution)/shard_map/ppermute | solution.py:276
  5.7 8.1 %collective-permute-start.3 = (bf16[6,8,128]{2,1,0:T(8,128)(2,1)S(1)}, bf16[6,8,128]{2,1,0:T(8,128)(2,1)S(1)}, u32[]{:S(2)}, u32[]{:S(2)}) collective-permute-start(bf16[6,8,128]{2,1,0:T(8,128)(2,1)S(1)} %slice_select_fusion.after), channel_id=1, source_target_pairs={{1,68},{2,69},{3,70},{4,65},{5,66},{6,67},{9,76},{10,77},{11,78},{... | collective-permute-start | bytes 36872 | tf_op jit(solution)/shard_map/ppermute | solution.py:276
  9.7 5.0 %collective-permute-start.2 = (bf16[6,8,128]{2,1,0:T(8,128)(2,1)S(1)}, bf16[6,8,128]{2,1,0:T(8,128)(2,1)S(1)}, u32[]{:S(2)}, u32[]{:S(2)}) collective-permute-start(bf16[6,8,128]{2,1,0:T(8,128)(2,1)S(1)} %slice_select_fusion.after), channel_id=1, source_target_pairs={{1,4},{2,5},{3,6},{4,1},{5,2},{6,3},{9,12},{10,13},{11,14},{12,9},... | collective-permute-start | bytes 36872 | tf_op jit(solution)/shard_map/ppermute | solution.py:276
  14.7 1.2 %collective-permute-start.4 = (bf16[2,6,8,128]{3,2,1,0:T(8,128)(2,1)S(1)}, bf16[2,6,8,128]{3,2,1,0:T(8,128)(2,1)S(1)}, u32[]{:S(2)}, u32[]{:S(2)}) collective-permute-start(bf16[2,6,8,128]{3,2,1,0:T(8,128)(2,1)S(1)} %pad_maximum_fusion.1), channel_id=1, source_target_pairs={{0,4},{1,5},{2,6},{3,7},{4,0},{5,1},{6,2},{7,3},{8,12},{9,13},{10,... | collective-permute-start | bytes 73736 | tf_op jit(solution)/shard_map/ppermute | solution.py:276
  14.8 1.6 %collective-permute-start.5 = (bf16[78,8,128]{2,1,0:T(8,128)(2,1)S(1)}, bf16[78,8,128]{2,1,0:T(8,128)(2,1)S(1)}, u32[]{:S(2)}, u32[]{:S(2)}) collective-permute-start(bf16[78,8,128]{2,1,0:T(8,128)(2,1)S(1)} %bitcast.14), channel_id=1, source_target_pairs={{0,4},{1,5},{2,6},{3,7},{4,0},{5,1},{6,2},{7,3},{8,12},{9,13},{10,... | collective-permute-start | bytes 479240 | tf_op jit(solution)/shard_map/ppermute | solution.py:276
  16.4 9.9 %collective-permute-start.6 = (bf16[168,8,128]{2,1,0:T(8,128)(2,1)S(1)}, bf16[168,8,128]{2,1,0:T(8,128)(2,1)S(1)}, u32[]{:S(2)}, u32[]{:S(2)}) collective-permute-start(bf16[168,8,128]{2,1,0:T(8,128)(2,1)S(1)} %pad_maximum_fusion), channel_id=1, source_target_pairs={{4,8},{5,9},{6,10},{7,11},{8,4},{9,5},{10,6},{11,7},{12,16},{13,17... | collective-permute-start | bytes 1032200 | tf_op jit(solution)/shard_map/ppermute | solution.py:276
  25.7 6.8 %collective-permute-start.8 = (bf16[9,112,128]{2,1,0:T(8,128)(2,1)S(1)}, bf16[9,112,128]{2,1,0:T(8,128)(2,1)S(1)}, u32[]{:S(2)}, u32[]{:S(2)}) collective-permute-start(bf16[9,112,128]{2,1,0:T(8,128)(2,1)S(1)} %get-tuple-element.43.mine_on), channel_id=1, source_target_pairs={{0,4},{1,5},{2,6},{3,7},{4,0},{5,1},{6,2},{7,3},{8,12},{9,13},{10,... | collective-permute-start | bytes 774152 | tf_op jit(solution)/shard_map/ppermute | solution.py:276
  27.7 8.9 %collective-permute-start.7 = (bf16[9,112,128]{2,1,0:T(8,128)(2,1)S(1)}, bf16[9,112,128]{2,1,0:T(8,128)(2,1)S(1)}, u32[]{:S(2)}, u32[]{:S(2)}) collective-permute-start(bf16[9,112,128]{2,1,0:T(8,128)(2,1)S(1)} %middle_far.1.mine_cr), channel_id=1, source_target_pairs={{4,8},{5,9},{6,10},{7,11},{8,4},{9,5},{10,6},{11,7},{12,16},{13,17... | collective-permute-start | bytes 774152 | tf_op jit(solution)/shard_map/ppermute | solution.py:276

commit v6 on v5

--- a/solution.py
+++ b/solution.py
@@ -312,17 +312,16 @@
     side, side_prev, *held_args = lax.optimization_barrier((side, side_prev, *held_args))
     weight, bias, gain, bias_next = held_args
     sides = jnp.stack([side, side_prev])
-    others = chip(sides)
+    swapped = chip(jnp.concatenate([ta[0].reshape(SLABS, TILE, LANE), sides.reshape(12, TILE, LANE)]))
+    others = swapped[SLABS:].reshape(sides.shape)
     mine_rim, on_rim = jnp.where(upper, others, sides), jnp.where(upper, sides, others)
-    on_prev = chip(ta[0].reshape(SLABS, TILE, LANE))
     message = jnp.concatenate([cr_row, ta[1].reshape(SLABS, TILE, LANE), mine_rim.reshape(12, TILE, LANE)])
-    message, on_prev = lax.optimization_barrier((message, on_prev))
     cr = cross(message)
 
     near, partial, weight_next = call(
         "middle_near",
         middle_near,
-        (mine, ta, on, on_prev, mine_rim, on_rim, weight, bias, gain),
+        (mine, ta, on, swapped, mine_rim, on_rim, weight, bias, gain),
         (second, held(6 * CYC, CH, dtype=jnp.float32), weights),
         far=(kernel_second,),
         taps=(3, 8),

time: 38.8 us -> 38.6 us (level)
  waiting for transfers between devices: 3.63 us -> 4.65 us
  starting transfers between devices: 20.7 us -> 20 us
  Pallas kernels: 13.4 us -> 12.9 us
    ppermute x9 -> x8, waiting for transfers between devices: 3.63 us -> 4.65 us  [send(): return lax.ppermute(array, axes, routes(sizes, move))]
    ppermute x9 -> x8, starting transfers between devices: 20.7 us -> 20 us  [send(): return lax.ppermute(array, axes, routes(sizes, move))]
    pallas_call x6, Pallas kernels: 13.4 us -> 12.9 us  [call(): pl.pallas_call(body, out_shape=outs, in_specs=[VMEM for _ in ins] + [HBM...]
  transfers between devices with their start and end apart: 9 -> 8, of which waited for: 5 -> 4; matrix products, arithmetic and copies ran while one was open for 1% -> 0% of each run, Pallas kernels for 27% -> 25%
where the time goes in v6:
time: 38.6 us; the launch traced here: 37.9 us
  starting transfers between devices  20 us (52%)
  Pallas kernels  12.9 us (33%)
  waiting for transfers between devices  4.65 us (12%)
    ppermute x8, starting transfers between devices, send(): return lax.ppermute(array, axes, routes(sizes, move))  20 us
    pallas_call x6, Pallas kernels, call(): pl.pallas_call(body, out_shape=outs, in_specs=[VMEM for _ in ins] + [HBM...  12.9 us
    ppermute x8, waiting for transfers between devices, send(): return lax.ppermute(array, axes, routes(sizes, move))  4.65 us
  transfers between devices with their start and end apart: 8, of which 4 were waited for; matrix products, arithmetic and copies ran while one was open for 0% of the time, Pallas kernels for 25%

profile of v6, /device:TPU:107, one launch (start us, length us, event | category | flops | bytes accessed | tf_op | source)
XLA Modules:
  0.0 37.9 jit_solution(16612822045489120134)
XLA Ops:
  0.0 1.6 %first.1 = (bf16[2,6,104,128]{3,2,1,0:T(8,128)(2,1)S(1)}, bf16[84,8,128]{2,1,0:T(8,128)(2,1)S(1)}, bf16[78,8,128]{2,1,0:T(8,128)(2,1)S(1)}, bf16[6,8,128]{2,1,0:...) custom-call(bf16[4,2,192,104]{3,2,1,0:T(8,128)(2,1)} %bitcast.15, f32[1,192]{1,0:T(1,128)} %bitcast.22), custom_call_target="tpu_custom_call" | custom-call | tf_op jit(solution)/shard_map/first/pallas_call | solution.py:251
  1.6 0.8 %collective-permute-start.1 = (bf16[84,8,128]{2,1,0:T(8,128)(2,1)S(1)}, bf16[84,8,128]{2,1,0:T(8,128)(2,1)S(1)}, u32[]{:S(2)}, u32[]{:S(2)}) collective-permute-start(bf16[84,8,128]{2,1,0:T(8,128)(2,1)S(1)} %get-tuple-element.28), channel_id=1, source_target_pairs={{0,4},{1,5},{2,6},{3,7},{4,0},{5,1},{6,2},{7,3},{8,12},{9,13},{10,... | collective-permute-start | bytes 516104 | tf_op jit(solution)/shard_map/ppermute | solution.py:276
  2.4 3.2 %collective-permute-start = (bf16[2,6,104,128]{3,2,1,0:T(8,128)(2,1)S(1)}, bf16[2,6,104,128]{3,2,1,0:T(8,128)(2,1)S(1)}, u32[]{:S(2)}, u32[]{:S(2)}) collective-permute-start(bf16[2,6,104,128]{3,2,1,0:T(8,128)(2,1)S(1)} %get-tuple-element.26.mine), channel_id=1, source_target_pairs={{0,64},{1,65},{2,66},{3,67},{4,68},{5,69},{6,70},{7,71},{8,72},{9,... | collective-permute-start | bytes 958472 | tf_op jit(solution)/shard_map/ppermute | solution.py:276
  5.6 0.0 collective-permute-done.1.on
  5.6 0.1 slice_select_fusion.after
  5.7 4.0 %collective-permute-start.3 = (bf16[6,8,128]{2,1,0:T(8,128)(2,1)S(1)}, bf16[6,8,128]{2,1,0:T(8,128)(2,1)S(1)}, u32[]{:S(2)}, u32[]{:S(2)}) collective-permute-start(bf16[6,8,128]{2,1,0:T(8,128)(2,1)S(1)} %slice_select_fusion.after), channel_id=1, source_target_pairs={{1,68},{2,69},{3,70},{4,65},{5,66},{6,67},{9,76},{10,77},{11,78},{... | collective-permute-start | bytes 36872 | tf_op jit(solution)/shard_map/ppermute | solution.py:276
  9.7 2.3 %collective-permute-start.2 = (bf16[6,8,128]{2,1,0:T(8,128)(2,1)S(1)}, bf16[6,8,128]{2,1,0:T(8,128)(2,1)S(1)}, u32[]{:S(2)}, u32[]{:S(2)}) collective-permute-start(bf16[6,8,128]{2,1,0:T(8,128)(2,1)S(1)} %slice_select_fusion.after), channel_id=1, source_target_pairs={{1,4},{2,5},{3,6},{4,1},{5,2},{6,3},{9,12},{10,13},{11,14},{12,9},... | collective-permute-start | bytes 36872 | tf_op jit(solution)/shard_map/ppermute | solution.py:276
  12.0 1.9 %load.1 = (bf16[3,14,128,192]{3,2,1,0:T(8,128)(2,1)S(1)}, f32[1,192]{1,0:T(1,128)S(1)}, f32[1,192]{1,0:T(1,128)S(1)}, f32[1,192]{1,0:T(1,128)S(1)}) custom-call(bf16[6,8,128]{2,1,0:T(8,128)(2,1)S(1)} %slice_select_fusion.after, bf16[3,3,3,192,192]{4,3,2,1,0:T(8,128)(2,1)} %kernel.2, f32[1,192]{1,0:T(1,128)} %bitcast.23, f32[1,192]{1,0:T(1,128)} %bitcast.24, ...), custom_call_target="tpu_custom_call" | custom-call | tf_op jit(solution)/shard_map/load/pallas_call | solution.py:251
  13.8 0.0 collective-permute-done.3
  13.8 0.9 %collective-permute-done.2 = bf16[6,8,128]{2,1,0:T(8,128)(2,1)S(1)} collective-permute-done((bf16[6,8,128]{2,1,0:T(8,128)(2,1)S(1)}, bf16[6,8,128]{2,1,0:T(8,128)(2,1)S(1)}, u32[]{:S(2)}, u32[]{:S(2)}) %collective-permute-start.2) | collective-permute-done | bytes 12320 | tf_op jit(solution)/shard_map/ppermute | solution.py:276
  14.7 0.0 collective-permute-done.ta
  14.8 0.1 collective-permute-start.4
  14.9 1.4 %collective-permute-done.4.on_prev = bf16[90,8,128]{2,1,0:T(8,128)(2,1)S(1)} collective-permute-done((bf16[90,8,128]{2,1,0:T(8,128)(2,1)S(1)}, bf16[90,8,128]{2,1,0:T(8,128)(2,1)S(1)}, u32[]{:S(2)}, u32[]{:S(2)}) %collective-permute-start.4) | collective-permute-done | bytes 184352 | tf_op jit(solution)/shard_map/ppermute | solution.py:276
  16.3 0.1 fusion.1
  16.4 4.8 %collective-permute-start.5 = (bf16[168,8,128]{2,1,0:T(8,128)(2,1)S(1)}, bf16[168,8,128]{2,1,0:T(8,128)(2,1)S(1)}, u32[]{:S(2)}, u32[]{:S(2)}) collective-permute-start(bf16[168,8,128]{2,1,0:T(8,128)(2,1)S(1)} %pad_maximum_fusion), channel_id=1, source_target_pairs={{4,8},{5,9},{6,10},{7,11},{8,4},{9,5},{10,6},{11,7},{12,16},{13,17... | collective-permute-start | bytes 1032200 | tf_op jit(solution)/shard_map/ppermute | solution.py:276
  21.2 0.1 broadcast_select_fusion
  21.3 4.0 %middle_near.1 = (bf16[9,112,128]{2,1,0:T(8,128)(2,1)S(1)}, f32[672,192]{1,0:T(8,128)S(1)}, bf16[3,14,128,192]{3,2,1,0:T(8,128)(2,1)S(1)}) custom-call(bf16[2,6,104,128]{3,2,1,0:T(8,128)(2,1)S(1)} %get-tuple-element.26.mine, bf16[2,6,104,128]{3,2,1,0:T(8,128)(2,1)S(1)} %collective-permute-done.ta, bf16[84,8,128]{2,1,0:T(8,128)(2,1)S(1)} %collective-permute-done.1.on, ...), custom_call_target="tpu_custom_call" | custom-call | tf_op jit(solution)/shard_map/middle_near/pallas_call | solution.py:251
  25.3 0.1 collective-permute-start.7
  25.4 0.8 %collective-permute-done.5.cr = bf16[168,8,128]{2,1,0:T(8,128)(2,1)S(1)} collective-permute-done((bf16[168,8,128]{2,1,0:T(8,128)(2,1)S(1)}, bf16[168,8,128]{2,1,0:T(8,128)(2,1)S(1)}, u32[]{:S(2)}, u32[]{:S(2)}) %collective-permute-start.5) | collective-permute-done | bytes 344096 | tf_op jit(solution)/shard_map/ppermute | solution.py:276
  26.2 1.3 %middle_far.1.mine_cr = bf16[9,112,128]{2,1,0:T(8,128)(2,1)S(1)} custom-call(bf16[168,8,128]{2,1,0:T(8,128)(2,1)S(1)} %collective-permute-done.5.cr, f32[672,192]{1,0:T(8,128)S(1)} %get-tuple-element.38.partial, bf16[3,14,128,192]{3,2,1,0:T(8,128)(2,1)S(1)} %get-tuple-element.35.weight, f32[1,192]{1,0:T(1,128)S(1)} %get-tuple-element.36.bias, ...), custom_call_target="tpu_custom_call" | custom-call | tf_op jit(solution)/shard_map/middle_far/pallas_call | solution.py:251
  27.5 4.8 %collective-permute-start.6 = (bf16[9,112,128]{2,1,0:T(8,128)(2,1)S(1)}, bf16[9,112,128]{2,1,0:T(8,128)(2,1)S(1)}, u32[]{:S(2)}, u32[]{:S(2)}) collective-permute-start(bf16[9,112,128]{2,1,0:T(8,128)(2,1)S(1)} %middle_far.1.mine_cr), channel_id=1, source_target_pairs={{4,8},{5,9},{6,10},{7,11},{8,4},{9,5},{10,6},{11,7},{12,16},{13,17... | collective-permute-start | bytes 774152 | tf_op jit(solution)/shard_map/ppermute | solution.py:276
  32.3 0.0 collective-permute-done.7.on
  32.3 2.5 %last_near.1 = (bf16[4,192,104]{2,1,0:T(8,128)(2,1)S(1)}, f32[448,192]{1,0:T(8,128)S(1)}) custom-call(bf16[9,112,128]{2,1,0:T(8,128)(2,1)S(1)} %get-tuple-element.39.mine_on, bf16[9,112,128]{2,1,0:T(8,128)(2,1)S(1)} %middle_far.1.mine_cr, bf16[9,112,128]{2,1,0:T(8,128)(2,1)S(1)} %collective-permute-done.7.on, ...), custom_call_target="tpu_custom_call" | custom-call | tf_op jit(solution)/shard_map/last_near/pallas_call | solution.py:251
  34.8 1.5 %collective-permute-done.6.cr = bf16[9,112,128]{2,1,0:T(8,128)(2,1)S(1)} collective-permute-done((bf16[9,112,128]{2,1,0:T(8,128)(2,1)S(1)}, bf16[9,112,128]{2,1,0:T(8,128)(2,1)S(1)}, u32[]{:S(2)}, u32[]{:S(2)}) %collective-permute-start.6) | collective-permute-done | bytes 258080 | tf_op jit(solution)/shard_map/ppermute | solution.py:276
  36.3 1.6 %last_far.1 = bf16[4,2,192,104]{3,2,1,0:T(8,128)(2,1)} custom-call(bf16[9,112,128]{2,1,0:T(8,128)(2,1)S(1)} %collective-permute-done.6.cr, f32[448,192]{1,0:T(8,128)S(1)} %get-tuple-element.43.partial, bf16[4,192,104]{2,1,0:T(8,128)(2,1)S(1)} %get-tuple-element.44.near, bf16[4,2,192,104]{3,2,1,0:T(8,128)(2,1)S(1)} %get-tuple-element.40.feat, ...), custom_call_target="tpu_custom_call" | custom-call | tf_op jit(solution)/shard_map/last_far/pallas_call | solution.py:251
  (5 shorter events, 0.1 us)
Async XLA Ops:
  1.6 4.0 %collective-permute-start.1 = (bf16[84,8,128]{2,1,0:T(8,128)(2,1)S(1)}, bf16[84,8,128]{2,1,0:T(8,128)(2,1)S(1)}, u32[]{:S(2)}, u32[]{:S(2)}) collective-permute-start(bf16[84,8,128]{2,1,0:T(8,128)(2,1)S(1)} %get-tuple-element.28), channel_id=1, source_target_pairs={{0,4},{1,5},{2,6},{3,7},{4,0},{5,1},{6,2},{7,3},{8,12},{9,13},{10,... | collective-permute-start | bytes 516104 | tf_op jit(solution)/shard_map/ppermute | solution.py:276
  2.4 12.3 %collective-permute-start = (bf16[2,6,104,128]{3,2,1,0:T(8,128)(2,1)S(1)}, bf16[2,6,104,128]{3,2,1,0:T(8,128)(2,1)S(1)}, u32[]{:S(2)}, u32[]{:S(2)}) collective-permute-start(bf16[2,6,104,128]{3,2,1,0:T(8,128)(2,1)S(1)} %get-tuple-element.26.mine), channel_id=1, source_target_pairs={{0,64},{1,65},{2,66},{3,67},{4,68},{5,69},{6,70},{7,71},{8,72},{9,... | collective-permute-start | bytes 958472 | tf_op jit(solution)/shard_map/ppermute | solution.py:276
  5.7 8.1 %collective-permute-start.3 = (bf16[6,8,128]{2,1,0:T(8,128)(2,1)S(1)}, bf16[6,8,128]{2,1,0:T(8,128)(2,1)S(1)}, u32[]{:S(2)}, u32[]{:S(2)}) collective-permute-start(bf16[6,8,128]{2,1,0:T(8,128)(2,1)S(1)} %slice_select_fusion.after), channel_id=1, source_target_pairs={{1,68},{2,69},{3,70},{4,65},{5,66},{6,67},{9,76},{10,77},{11,78},{... | collective-permute-start | bytes 36872 | tf_op jit(solution)/shard_map/ppermute | solution.py:276
  9.7 5.0 %collective-permute-start.2 = (bf16[6,8,128]{2,1,0:T(8,128)(2,1)S(1)}, bf16[6,8,128]{2,1,0:T(8,128)(2,1)S(1)}, u32[]{:S(2)}, u32[]{:S(2)}) collective-permute-start(bf16[6,8,128]{2,1,0:T(8,128)(2,1)S(1)} %slice_select_fusion.after), channel_id=1, source_target_pairs={{1,4},{2,5},{3,6},{4,1},{5,2},{6,3},{9,12},{10,13},{11,14},{12,9},... | collective-permute-start | bytes 36872 | tf_op jit(solution)/shard_map/ppermute | solution.py:276
  14.8 1.5 %collective-permute-start.4 = (bf16[90,8,128]{2,1,0:T(8,128)(2,1)S(1)}, bf16[90,8,128]{2,1,0:T(8,128)(2,1)S(1)}, u32[]{:S(2)}, u32[]{:S(2)}) collective-permute-start(bf16[90,8,128]{2,1,0:T(8,128)(2,1)S(1)} %pad_maximum_fusion.1), channel_id=1, source_target_pairs={{0,4},{1,5},{2,6},{3,7},{4,0},{5,1},{6,2},{7,3},{8,12},{9,13},{10,... | collective-permute-start | bytes 552968 | tf_op jit(solution)/shard_map/ppermute | solution.py:276
  16.4 9.8 %collective-permute-start.5 = (bf16[168,8,128]{2,1,0:T(8,128)(2,1)S(1)}, bf16[168,8,128]{2,1,0:T(8,128)(2,1)S(1)}, u32[]{:S(2)}, u32[]{:S(2)}) collective-permute-start(bf16[168,8,128]{2,1,0:T(8,128)(2,1)S(1)} %pad_maximum_fusion), channel_id=1, source_target_pairs={{4,8},{5,9},{6,10},{7,11},{8,4},{9,5},{10,6},{11,7},{12,16},{13,17... | collective-permute-start | bytes 1032200 | tf_op jit(solution)/shard_map/ppermute | solution.py:276
  25.3 7.0 %collective-permute-start.7 = (bf16[9,112,128]{2,1,0:T(8,128)(2,1)S(1)}, bf16[9,112,128]{2,1,0:T(8,128)(2,1)S(1)}, u32[]{:S(2)}, u32[]{:S(2)}) collective-permute-start(bf16[9,112,128]{2,1,0:T(8,128)(2,1)S(1)} %get-tuple-element.39.mine_on), channel_id=1, source_target_pairs={{0,4},{1,5},{2,6},{3,7},{4,0},{5,1},{6,2},{7,3},{8,12},{9,13},{10,... | collective-permute-start | bytes 774152 | tf_op jit(solution)/shard_map/ppermute | solution.py:276
  27.5 8.9 %collective-permute-start.6 = (bf16[9,112,128]{2,1,0:T(8,128)(2,1)S(1)}, bf16[9,112,128]{2,1,0:T(8,128)(2,1)S(1)}, u32[]{:S(2)}, u32[]{:S(2)}) collective-permute-start(bf16[9,112,128]{2,1,0:T(8,128)(2,1)S(1)} %middle_far.1.mine_cr), channel_id=1, source_target_pairs={{4,8},{5,9},{6,10},{7,11},{8,4},{9,5},{10,6},{11,7},{12,16},{13,17... | collective-permute-start | bytes 774152 | tf_op jit(solution)/shard_map/ppermute | solution.py:276
